TPU v7x, 32 devices: a whole 2x2x4 slice. The times are simulated.
32 devices in a mesh: groups: 2 (over y), ctx: 4 (over z), dp: 2 (over x), tp: 2 (over core).
Axes of the slice: x: 2, y: 2, z: 4, core: 2. Of those that a mesh axis runs over, the one named last changes fastest.
Arguments:
- queries: bfloat16 [4, 1280, 2048], P(('groups', 'dp'), 'ctx', 'tp'), parts along dimension 0, may hold values from -6 to 6
- key_vectors: bfloat16 [4, 1280, 2048], P(('groups', 'dp'), 'ctx', 'tp'), parts along dimension 0, may hold values from -6 to 6
- value_vectors: bfloat16 [4, 1280, 2048], P(('groups', 'dp'), 'ctx', 'tp'), parts along dimension 0, may hold values from -6 to 6
- grad_output: bfloat16 [4, 1280, 2048], P(('groups', 'dp'), 'ctx', 'tp'), parts along dimension 0, may hold values from -6 to 6
Outputs:
- normed_out: bfloat16 [4, 1280, 2048], P(('groups', 'dp'), 'ctx', 'tp'), parts along dimension 0
- grad_queries: bfloat16 [4, 1280, 2048], P(('groups', 'dp'), 'ctx', 'tp'), parts along dimension 0
- grad_keys: bfloat16 [4, 1280, 2048], P(('groups', 'dp'), 'ctx', 'tp'), parts along dimension 0
- grad_values: bfloat16 [4, 1280, 2048], P(('groups', 'dp'), 'ctx', 'tp'), parts along dimension 0
There are 2 independent parts, one for each index of `groups`. A program takes and returns all parts, laid end to end along the dimension named above; each array names one. Nothing has to cross between parts.
All inputs are finite; a program needn't handle non-finite values.
Results may differ from a plain program's by a relative error of at most 0.0059.
Values may be sent and summed in bfloat16 or wider, within the bound.
No kernel may reach another device: no remote copies, remote signals or barrier semaphores. Data moves between devices by JAX's collectives and lax.ppermute only.
A program may use at most 64 MiB of HBM per device.

v0:
```python
import jax
import jax.numpy as jnp
from jax import lax
from jax.sharding import PartitionSpec as P

DH = 128


norm_eps = 1e-06


def shards(queries, key_vectors, value_vectors, grad_output):
    block_len = queries.shape[1]
    head_count = queries.shape[2] // DH
    query_rows = queries.reshape(block_len, head_count, DH)
    key_rows = key_vectors.reshape(block_len, head_count, DH)
    value_rows = value_vectors.reshape(block_len, head_count, DH)
    grad_rows = grad_output.reshape(block_len, head_count, DH)
    rows = lax.broadcasted_iota(jnp.int32, (block_len, block_len), 0)
    columns = lax.broadcasted_iota(jnp.int32, (block_len, block_len), 1)
    causal = (columns <= rows)[None]
    local_state = jnp.einsum(
        "shd,she->hde", key_rows, value_rows, preferred_element_type=jnp.float32
    )
    state_shape = local_state.shape
    shares = lax.all_to_all(
        local_state.reshape(1, -1), "ctx", split_axis=1, concat_axis=0, tiled=True
    )
    running = jnp.cumsum(shares, axis=0)
    earlier_shares = (running - shares).astype(jnp.bfloat16)
    earlier_low = lax.all_to_all(
        earlier_shares, "ctx", split_axis=0, concat_axis=1, tiled=True
    ).reshape(state_shape)
    raw_scores = jnp.einsum(
        "thd,shd->hts", query_rows, key_rows, preferred_element_type=jnp.float32
    )
    scores_low = jnp.where(causal, raw_scores, 0.0).astype(jnp.bfloat16)
    mixed = jnp.einsum("hts,she->the", scores_low, value_rows, preferred_element_type=jnp.float32)
    mixed = mixed + jnp.einsum(
        "thd,hde->the", query_rows, earlier_low, preferred_element_type=jnp.float32
    )
    inverse = lax.rsqrt(jnp.mean(mixed * mixed, axis=-1, keepdims=True) + norm_eps)
    normed = mixed * inverse
    grad_f = grad_rows.astype(jnp.float32)
    grad_mixed = inverse * (grad_f - normed * jnp.mean(grad_f * normed, axis=-1, keepdims=True))
    grad_low = grad_mixed.astype(jnp.bfloat16)
    grad_state = jnp.einsum(
        "thd,the->hde", query_rows, grad_low, preferred_element_type=jnp.float32
    )
    grad_shares = lax.all_to_all(
        grad_state.reshape(1, -1), "ctx", split_axis=1, concat_axis=0, tiled=True
    )
    grad_total = jnp.sum(grad_shares, axis=0, keepdims=True)
    later_shares = (grad_total - jnp.cumsum(grad_shares, axis=0)).astype(jnp.bfloat16)
    later_low = lax.all_to_all(
        later_shares, "ctx", split_axis=0, concat_axis=1, tiled=True
    ).reshape(state_shape)
    raw_grad = jnp.einsum("the,she->hts", grad_low, value_rows, preferred_element_type=jnp.float32)
    grad_scores = jnp.where(causal, raw_grad, 0.0).astype(jnp.bfloat16)
    grad_q = jnp.einsum("hts,shd->thd", grad_scores, key_rows, preferred_element_type=jnp.float32)
    grad_q = grad_q + jnp.einsum(
        "the,hde->thd", grad_low, earlier_low, preferred_element_type=jnp.float32
    )
    grad_k = jnp.einsum("hts,thd->shd", grad_scores, query_rows, preferred_element_type=jnp.float32)
    grad_k = grad_k + jnp.einsum(
        "she,hde->shd", value_rows, later_low, preferred_element_type=jnp.float32
    )
    grad_v = jnp.einsum("hts,the->she", scores_low, grad_low, preferred_element_type=jnp.float32)
    grad_v = grad_v + jnp.einsum(
        "shd,hde->she", key_rows, later_low, preferred_element_type=jnp.float32
    )
    out_shape = queries.shape
    return (
        normed.astype(jnp.bfloat16).reshape(out_shape),
        grad_q.astype(jnp.bfloat16).reshape(out_shape),
        grad_k.astype(jnp.bfloat16).reshape(out_shape),
        grad_v.astype(jnp.bfloat16).reshape(out_shape),
    )


def solution(mesh):
    placed = (
        P(("groups", "dp"), "ctx", "tp"),
        P(("groups", "dp"), "ctx", "tp"),
        P(("groups", "dp"), "ctx", "tp"),
        P(("groups", "dp"), "ctx", "tp"),
    )
    return jax.shard_map(
        shards,
        mesh=mesh,
        in_specs=placed,
        out_specs=(
            P(("groups", "dp"), "ctx", "tp"),
            P(("groups", "dp"), "ctx", "tp"),
            P(("groups", "dp"), "ctx", "tp"),
            P(("groups", "dp"), "ctx", "tp"),
        ),
        check_vma=False,
    )
```

profile of v0, /device:TPU:0, one launch (start us, length us, event | category | flops | bytes accessed | tf_op | source)
XLA Modules:
  0.0 100.5 jit_solution(13804386962089446467)
XLA Ops:
  0.6 1.3 %copy.92 = bf16[40,8,8,128]{3,2,1,0:T(8,128)(2,1)S(1)} copy(bf16[40,8,8,128]{3,1,2,0:T(8,128)(2,1)} %bitcast.73) | data formatting | bytes 1310720
  2.1 1.2 %fusion.13 = f32[8,128,128]{2,1,0:T(8,128)} fusion(bf16[320,8,128]{2,1,0:T(8,128)(2,1)S(1)} %bitcast.61, bf16[320,8,128]{2,1,0:T(8,128)(2,1)S(1)} %bitcast.65), kind=kOutput, calls=%fused_computation.31 | convolution fusion | flops 83886080 | bytes 1835008 | tf_op jit(solution)/shard_map/shd,she->hde/dot_general | solution.py:22
  3.3 6.3 %all-to-all-start = ((f32[1,4,32768]{2,0,1:T(1,128)}), f32[1,4,32768]{2,0,1:T(1,128)S(1)}, u32[]{:S(2)}, u32[]{:S(2)}) async-start(f32[1,4,32768]{2,0,1:T(1,128)} %bitcast.1), calls=%async_computation | async-start | bytes 1048576 | tf_op jit(solution)/shard_map/all_to_all | solution.py:26
  9.8 2.0 %select_convert_fusion.1 = bf16[8,320,320]{2,1,0:T(8,128)(2,1)} fusion(pred[320,320]{1,0:T(8,128)(4,1)S(1)} %iota_compare_fusion, bf16[320,8,128]{2,1,0:T(8,128)(2,1)S(1)} %bitcast.66, bf16[320,8,128]{2,1,0:T(8,128)(2,1)S(1)} %bitcast.69), kind=kOutput, calls=%fused_computation.5 | convolution fusion | flops 211353600 | bytes 3051520 | tf_op jit(solution)/shard_map/thd,shd->hts/dot_general | solution.py:34
  11.8 12.3 %all-to-all-done = f32[1,4,32768]{2,0,1:T(1,128)S(1)} async-done(((f32[1,4,32768]{2,0,1:T(1,128)}), f32[1,4,32768]{2,0,1:T(1,128)S(1)}, u32[]{:S(2)}, u32[]{:S(2)}) %all-to-all-start) | async-done | bytes 524320 | tf_op jit(solution)/shard_map/all_to_all | solution.py:26
  25.0 2.3 %reduce.3 = bf16[4,32768]{1,0:T(4,128)(2,1)S(1)} reduce(bf16[4,1,32768]{2,1,0:T(2,128)(2,1)S(1)} %fusion, bf16[]{:T(256)} %broadcast.40), dimensions={1}, to_apply=%fusion.reduce_sub_computation | reduce | bytes 524290 | tf_op jit(solution)/shard_map/jit(cumsum)/reduce_window_sum | solution.py:29
  28.4 3.4 %all-to-all-start.1 = ((bf16[4,2,16384]{2,1,0:T(2,128)(2,1)}), bf16[4,2,16384]{2,1,0:T(2,128)(2,1)S(1)}, u32[]{:S(2)}, u32[]{:S(2)}) async-start(bf16[4,2,16384]{2,1,0:T(2,128)(2,1)} %reshape.148), calls=%async_computation.1 | async-start | bytes 524288 | tf_op jit(solution)/shard_map/all_to_all | solution.py:31
  33.3 1.3 %copy-done.3 = bf16[8,320,320]{2,1,0:T(8,128)(2,1)S(1)} copy-done((bf16[8,320,320]{2,1,0:T(8,128)(2,1)S(1)}, bf16[8,320,320]{2,1,0:T(8,128)(2,1)}, u32[]{:S(2)}) %copy-start.3) | copy-done | bytes 1638424
  34.6 1.7 %convolution_bitcast_fusion.5 = f32[320,8,128]{2,0,1:T(8,128)} fusion(bf16[8,320,320]{2,1,0:T(8,128)(2,1)S(1)} %copy-done.3, bf16[320,8,128]{2,1,0:T(8,128)(2,1)S(1)} %bitcast.62), kind=kOutput, calls=%fused_computation.15 | convolution fusion | flops 209715200 | bytes 3604480 | tf_op jit(solution)/shard_map/hts,she->the/dot_general | solution.py:38
  36.3 3.8 %all-to-all-done.1 = bf16[4,2,16384]{2,1,0:T(2,128)(2,1)S(1)} async-done(((bf16[4,2,16384]{2,1,0:T(2,128)(2,1)}), bf16[4,2,16384]{2,1,0:T(2,128)(2,1)S(1)}, u32[]{:S(2)}, u32[]{:S(2)}) %all-to-all-start.1) | async-done | bytes 262176 | tf_op jit(solution)/shard_map/all_to_all | solution.py:31
  41.1 3.4 %reduce.1 = bf16[4,32768]{1,0:T(4,128)(2,1)} reduce(bf16[4,1,32768]{2,1,0:T(2,128)(2,1)} %reshape.149, bf16[]{:T(256)} %constant.16), dimensions={1}, to_apply=%all_to_all.18.reduce_sub_computation | reduce | bytes 524290 | tf_op jit(solution)/shard_map/all_to_all | solution.py:31
  45.7 2.0 %multiply_reduce_fusion.1 = (f32[320,8]{0,1:T(8,128)S(1)}, f32[320,8,128]{2,0,1:T(8,128)S(1)}) fusion(f32[320,8,128]{2,0,1:T(8,128)} %convolution_bitcast_fusion.5, bf16[8,128,128]{2,1,0:T(8,128)(2,1)S(1)} %reshape.139, bf16[320,8,128]{2,1,0:T(8,128)(2,1)S(1)} %bitcast.70), kind=kOutput, calls=%fused_computation.22 | convolution fusion | flops 84866560 | bytes 3549184 | tf_op jit(solution)/shard_map/thd,hde->the/dot_general | solution.py:39
  48.6 1.6 %multiply_convert_fusion = (bf16[320,8,128]{2,0,1:T(8,128)(2,1)S(1)}, bf16[320,8,128]{2,0,1:T(8,128)(2,1)}) fusion(f32[320,8,128]{2,1,0:T(8,128)S(1)} %bitcast.60, f32[320,8,128]{2,0,1:T(8,128)S(1)} %get-tuple-element.7, f32[320,8]{0,1:T(8,128)S(1)} %broadcast_multiply_fusion, f32[320,8]{0,1:T(8,128)S(1)} %add_rsqrt_fusion), kind=kLoop, calls=%fused_computation.20 | loop fusion | flops 1966080 | bytes 3952640 | tf_op jit(solution)/shard_map/convert_element_type | solution.py:46
  51.6 4.3 %all-to-all-start.2 = ((f32[1,4,32768]{2,0,1:T(1,128)}), f32[1,4,32768]{2,0,1:T(1,128)}, u32[]{:S(2)}, u32[]{:S(2)}) async-start(f32[1,4,32768]{2,0,1:T(1,128)} %bitcast.8), calls=%async_computation.2 | async-start | bytes 1048576 | tf_op jit(solution)/shard_map/all_to_all | solution.py:50
  56.7 1.3 %copy-done.5 = bf16[8,320,320]{2,1,0:T(8,128)(2,1)} copy-done((bf16[8,320,320]{2,1,0:T(8,128)(2,1)}, bf16[8,320,320]{2,1,0:T(8,128)(2,1)S(1)}, u32[]{:S(2)}) %copy-start.5) | copy-done | bytes 1638424
  58.6 9.6 %all-to-all-done.2 = f32[1,4,32768]{2,0,1:T(1,128)} async-done(((f32[1,4,32768]{2,0,1:T(1,128)}), f32[1,4,32768]{2,0,1:T(1,128)}, u32[]{:S(2)}, u32[]{:S(2)}) %all-to-all-start.2) | async-done | bytes 524320 | tf_op jit(solution)/shard_map/all_to_all | solution.py:50
  68.2 2.2 %reduce_sum.29 = f32[32768]{0:T(1024)} reduce(f32[1,4,32768]{2,0,1:T(1,128)} %all-to-all-done.2, f32[]{:T(128)} %constant.9.clone.1), dimensions={0,1}, to_apply=%region_3.4 | reduce | flops 98304 | bytes 655364 | tf_op jit(solution)/shard_map/reduce_sum | solution.py:53
  70.3 2.3 %fusion.1 = bf16[4,1,32768]{2,1,0:T(2,128)(2,1)} fusion(f32[1,4,32768]{2,0,1:T(1,128)} %all-to-all-done.2, f32[32768]{0:T(1024)} %reduce_sum.29), kind=kOutput, calls=%fused_computation.3 | output fusion | flops 655360 | bytes 917504 | tf_op jit(solution)/shard_map/jit(cumsum)/reduce_window_sum | solution.py:54
  72.6 4.0 %reduce.4 = bf16[4,32768]{1,0:T(4,128)(2,1)} reduce(bf16[4,1,32768]{2,1,0:T(2,128)(2,1)} %fusion.1, bf16[]{:T(256)} %broadcast.40), dimensions={1}, to_apply=%fusion.1.reduce_sub_computation | reduce | bytes 524290 | tf_op jit(solution)/shard_map/jit(cumsum)/reduce_window_sum | solution.py:54
  76.6 2.0 %reshape.150 = bf16[4,2,16384]{2,1,0:T(2,128)(2,1)} reshape(bf16[4,32768]{1,0:T(4,128)(2,1)} %reduce.4) | data formatting | bytes 524288
  78.6 4.0 %all-to-all-start.3 = ((bf16[4,2,16384]{2,1,0:T(2,128)(2,1)}), bf16[4,2,16384]{2,1,0:T(2,128)(2,1)}, u32[]{:S(2)}, u32[]{:S(2)}) async-start(bf16[4,2,16384]{2,1,0:T(2,128)(2,1)} %reshape.150), calls=%async_computation.3 | async-start | bytes 524288 | tf_op jit(solution)/shard_map/all_to_all | solution.py:55
  85.4 1.6 %copy.78 = bf16[320,8,128]{2,1,0:T(8,128)(2,1)S(1)} copy(bf16[320,8,128]{2,0,1:T(8,128)(2,1)} %fusion.5) | data formatting | bytes 1310720 | tf_op jit(solution)/shard_map/convert_element_type | solution.py:75
  88.1 3.4 %convolution_bitcast_fusion.2 = f32[320,8,128]{2,0,1:T(8,128)} fusion(bf16[8,320,320]{2,1,0:T(8,128)(2,1)} %copy-done.5, bf16[320,8,128]{2,1,0:T(8,128)(2,1)S(1)} %bitcast.72), kind=kOutput, calls=%fused_computation.11 | convolution fusion | flops 209715200 | bytes 3604480 | tf_op jit(solution)/shard_map/hts,thd->shd/dot_general | solution.py:64
  92.7 1.7 %reduce.2 = bf16[4,32768]{1,0:T(4,128)(2,1)S(1)} reduce(bf16[4,1,32768]{2,1,0:T(2,128)(2,1)S(1)} %reshape.151, bf16[]{:T(256)} %constant.16), dimensions={1}, to_apply=%all_to_all.41.reduce_sub_computation | reduce | bytes 524290 | tf_op jit(solution)/shard_map/all_to_all | solution.py:55
  (53 shorter events, 20.6 us)
Async XLA Ops:
  0.6 1.3 %copy-start.8 = (bf16[1,320,1024]{2,1,0:T(8,128)(2,1)S(1)}, bf16[1,320,1024]{2,1,0:T(8,128)(2,1)}, u32[]{:S(2)}) copy-start(bf16[1,320,1024]{2,1,0:T(8,128)(2,1)} %param.6) | copy-start | bytes 1966084
  2.1 7.6 %copy-start.9 = (bf16[1,320,1024]{2,1,0:T(8,128)(2,1)S(1)}, bf16[1,320,1024]{2,1,0:T(8,128)(2,1)}, u32[]{:S(2)}) copy-start(bf16[1,320,1024]{2,1,0:T(8,128)(2,1)} %param.4) | copy-start | bytes 1966084
  3.3 20.8 %all-to-all-start = ((f32[1,4,32768]{2,0,1:T(1,128)}), f32[1,4,32768]{2,0,1:T(1,128)S(1)}, u32[]{:S(2)}, u32[]{:S(2)}) async-start(f32[1,4,32768]{2,0,1:T(1,128)} %bitcast.1), calls=%async_computation | async-start | bytes 1048576 | tf_op jit(solution)/shard_map/all_to_all | solution.py:26
  9.8 35.9 %copy-start = (bf16[40,8,8,128]{3,2,1,0:T(8,128)(2,1)}, bf16[40,8,8,128]{3,2,1,0:T(8,128)(2,1)S(1)}, u32[]{:S(2)}) copy-start(bf16[40,8,8,128]{3,2,1,0:T(8,128)(2,1)S(1)} %copy.91) | copy-start | bytes 1966084
  9.8 2.0 %copy-start.10 = (pred[320,320]{1,0:T(8,128)(4,1)}, pred[320,320]{1,0:T(8,128)(4,1)S(1)}, u32[]{:S(2)}) copy-start(pred[320,320]{1,0:T(8,128)(4,1)S(1)} %iota_compare_fusion) | copy-start | bytes 307204
  28.4 11.8 %all-to-all-start.1 = ((bf16[4,2,16384]{2,1,0:T(2,128)(2,1)}), bf16[4,2,16384]{2,1,0:T(2,128)(2,1)S(1)}, u32[]{:S(2)}, u32[]{:S(2)}) async-start(bf16[4,2,16384]{2,1,0:T(2,128)(2,1)} %reshape.148), calls=%async_computation.1 | async-start | bytes 524288 | tf_op jit(solution)/shard_map/all_to_all | solution.py:31
  33.0 1.6 %copy-start.3 = (bf16[8,320,320]{2,1,0:T(8,128)(2,1)S(1)}, bf16[8,320,320]{2,1,0:T(8,128)(2,1)}, u32[]{:S(2)}) copy-start(bf16[8,320,320]{2,1,0:T(8,128)(2,1)} %select_convert_fusion.1) | copy-start | bytes 4915204
  48.5 1.6 %copy-start.1 = (bf16[40,8,8,128]{3,2,1,0:T(8,128)(2,1)S(1)}, bf16[40,8,8,128]{3,2,1,0:T(8,128)(2,1)}, u32[]{:S(2)}) copy-start(bf16[40,8,8,128]{3,2,1,0:T(8,128)(2,1)} %copy-done) | copy-start | bytes 1966084
  50.6 5.3 %copy-start.11 = (pred[320,320]{1,0:T(8,128)(4,1)S(1)}, pred[320,320]{1,0:T(8,128)(4,1)}, u32[]{:S(2)}) copy-start(pred[320,320]{1,0:T(8,128)(4,1)} %copy-done.10) | copy-start | bytes 307204
  51.6 16.5 %all-to-all-start.2 = ((f32[1,4,32768]{2,0,1:T(1,128)}), f32[1,4,32768]{2,0,1:T(1,128)}, u32[]{:S(2)}, u32[]{:S(2)}) async-start(f32[1,4,32768]{2,0,1:T(1,128)} %bitcast.8), calls=%async_computation.2 | async-start | bytes 1048576 | tf_op jit(solution)/shard_map/all_to_all | solution.py:50
  56.7 1.3 %copy-start.5 = (bf16[8,320,320]{2,1,0:T(8,128)(2,1)}, bf16[8,320,320]{2,1,0:T(8,128)(2,1)S(1)}, u32[]{:S(2)}) copy-start(bf16[8,320,320]{2,1,0:T(8,128)(2,1)S(1)} %select_convert_fusion) | copy-start | bytes 4915204
  78.6 12.9 %all-to-all-start.3 = ((bf16[4,2,16384]{2,1,0:T(2,128)(2,1)}), bf16[4,2,16384]{2,1,0:T(2,128)(2,1)}, u32[]{:S(2)}, u32[]{:S(2)}) async-start(bf16[4,2,16384]{2,1,0:T(2,128)(2,1)} %reshape.150), calls=%async_computation.3 | async-start | bytes 524288 | tf_op jit(solution)/shard_map/all_to_all | solution.py:55
  82.6 1.2 %copy-start.7 = (bf16[320,8,128]{2,0,1:T(8,128)(2,1)S(1)}, bf16[320,8,128]{2,0,1:T(8,128)(2,1)}, u32[]{:S(2)}) copy-start(bf16[320,8,128]{2,0,1:T(8,128)(2,1)} %get-tuple-element.5) | copy-start | bytes 1966084
  85.4 2.7 %copy-start.2 = (bf16[40,8,8,128]{3,2,1,0:T(8,128)(2,1)S(1)}, bf16[40,8,8,128]{3,2,1,0:T(8,128)(2,1)}, u32[]{:S(2)}) copy-start(bf16[40,8,8,128]{3,2,1,0:T(8,128)(2,1)} %copy-done) | copy-start | bytes 1966084
  94.7 1.5 %copy-start.4 = (bf16[8,320,320]{2,1,0:T(8,128)(2,1)S(1)}, bf16[8,320,320]{2,1,0:T(8,128)(2,1)}, u32[]{:S(2)}) copy-start(bf16[8,320,320]{2,1,0:T(8,128)(2,1)} %select_convert_fusion.1) | copy-start | bytes 4915204
  97.1 1.6 %copy-start.6 = (f32[320,8,128]{2,0,1:T(8,128)S(1)}, f32[320,8,128]{2,0,1:T(8,128)}, u32[]{:S(2)}) copy-start(f32[320,8,128]{2,0,1:T(8,128)} %convolution_bitcast_fusion.2) | copy-start | bytes 3932164
where the time goes:
time: 101 us
  waiting for transfers between devices  25.7 us (25%)
  local copies, waits for them, and re-layouts  21 us (21%)
  other arithmetic  19.9 us (20%)
  starting transfers between devices  18.1 us (18%)
  matrix products  14.8 us (15%)
    all_to_all x1, waiting for transfers between devices, shards(): lax.all_to_all(local_state.reshape(1, -1), 'ctx', split_axis=1, concat_ax...  12.3 us
    unnamed x32, local copies, waits for them, and re-layouts  10.7 us
    all_to_all x1, waiting for transfers between devices, shards(): lax.all_to_all(grad_state.reshape(1, -1), 'ctx', split_axis=1, concat_axi...  9.56 us
    all_to_all x1, starting transfers between devices, shards(): lax.all_to_all(local_state.reshape(1, -1), 'ctx', split_axis=1, concat_ax...  6.32 us
    another operation x2, other arithmetic, shards(): jnp.cumsum(grad_shares, axis=0)  6.27 us
    all_to_all x1, starting transfers between devices, shards(): lax.all_to_all(grad_state.reshape(1, -1), 'ctx', split_axis=1, concat_axi...  4.33 us
    all_to_all x1, starting transfers between devices, shards(): lax.all_to_all(later_shares, 'ctx', split_axis=0, concat_axis=1, tiled=True)  4.04 us
    all_to_all x1, waiting for transfers between devices, shards(): lax.all_to_all(earlier_shares, 'ctx', split_axis=0, concat_axis=1, tiled=...  3.82 us
  transfers between devices with their start and end apart: 4, of which 3 were waited for; matrix products, arithmetic and copies ran while one was open for 15% of the time, Pallas kernels for 0%

commit v1 on v0

v1 whole, which is shorter than its diff:
```python
import jax
import jax.numpy as jnp
from jax import lax
from jax.experimental import pallas as pl
from jax.experimental.pallas import tpu as pltpu
from jax.sharding import PartitionSpec as P

DH = 128
norm_eps = 1e-06
F32 = jnp.float32
BF16 = jnp.bfloat16

VMEM_SPEC = pl.BlockSpec(memory_space=pltpu.VMEM)
ANY_SPEC = pl.BlockSpec(memory_space=pl.ANY)
PARAMS = pltpu.CompilerParams(vmem_limit_bytes=48 << 20)


def dot_nn(a, b):
    return lax.dot_general(a, b, (((1,), (0,)), ((), ())), preferred_element_type=F32)


def dot_nt(a, b):
    return lax.dot_general(a, b, (((1,), (1,)), ((), ())), preferred_element_type=F32)


def dot_tn(a, b):
    return lax.dot_general(a, b, (((0,), (0,)), ((), ())), preferred_element_type=F32)


def head(index):
    return slice(index * DH, (index + 1) * DH)


def causal(length):
    rows = lax.broadcasted_iota(jnp.int32, (length, length), 0)
    columns = lax.broadcasted_iota(jnp.int32, (length, length), 1)
    return columns <= rows


def state_kernel(order_ref, k_ref, v_ref, first_ref, second_ref):
    half_heads = first_ref.shape[0] // DH
    for place, out_ref in enumerate((first_ref, second_ref)):
        base = order_ref[place] * half_heads
        for h in range(half_heads):
            cols = pl.ds(pl.multiple_of((base + h) * DH, DH), DH)
            out_ref[head(h), :] = dot_tn(k_ref[:, cols], v_ref[:, cols]).astype(BF16)


def states(order, k, v):
    half_rows = k.shape[1] // 2
    shape = jax.ShapeDtypeStruct((half_rows, DH), BF16)
    return pl.pallas_call(
        state_kernel,
        out_shape=(shape, shape),
        in_specs=[pl.BlockSpec(memory_space=pltpu.SMEM), VMEM_SPEC, VMEM_SPEC],
        out_specs=(VMEM_SPEC, VMEM_SPEC),
        compiler_params=PARAMS,
        name="states",
    )(order, k, v)


def intra_kernel(q_ref, k_ref, v_ref, out_ref):
    mask = causal(q_ref.shape[0])
    for h in range(q_ref.shape[1] // DH):
        scores = dot_nt(q_ref[:, head(h)], k_ref[:, head(h)])
        scores = jnp.where(mask, scores, 0.0).astype(BF16)
        out_ref[:, head(h)] = dot_nn(scores, v_ref[:, head(h)])


def intra(q, k, v):
    length, width = q.shape
    steps = 2
    spec = pl.BlockSpec((length, width // steps), lambda i: (0, i))
    return pl.pallas_call(
        intra_kernel,
        out_shape=jax.ShapeDtypeStruct(q.shape, F32),
        grid=(steps,),
        in_specs=[spec] * 3,
        out_specs=spec,
        compiler_params=PARAMS,
        cost_estimate=pl.CostEstimate(flops=4 * length * length * width, transcendentals=0, bytes_accessed=10 * length * width),
        name="intra",
    )(q, k, v)


def mid_kernel(half_ref, q_ref, g_ref, intra_ref, e_ref, *refs):
    normed_ref, grad_ref, state_ref = refs[-3:]
    for h in range(q_ref.shape[1] // DH):
        q = q_ref[:, head(h)]
        mixed = intra_ref[:, head(h)] + dot_nn(q, e_ref[head(h), :])
        inverse = lax.rsqrt(jnp.mean(mixed * mixed, axis=-1, keepdims=True) + norm_eps)
        normed = mixed * inverse
        g = g_ref[:, head(h)].astype(F32)
        grad = inverse * (g - normed * jnp.mean(g * normed, axis=-1, keepdims=True))
        grad = grad.astype(BF16)
        normed_ref[:, head(h)] = normed.astype(BF16)
        grad_ref[:, head(h)] = grad
        state_ref[head(h), :] = dot_tn(q, grad).astype(BF16)


def mid(half, q, g, intra_out, earlier, filled=None):
    length, width = q.shape
    columns = pl.BlockSpec((length, width // 2), lambda i, half: (0, half[0]))
    whole = pl.BlockSpec(earlier.shape, lambda i, half: (0, 0))
    extra = () if filled is None else filled
    return pl.pallas_call(
        mid_kernel,
        out_shape=(
            jax.ShapeDtypeStruct(q.shape, BF16),
            jax.ShapeDtypeStruct(q.shape, BF16),
            jax.ShapeDtypeStruct(earlier.shape, BF16),
        ),
        grid_spec=pltpu.PrefetchScalarGridSpec(
            num_scalar_prefetch=1,
            grid=(1,),
            in_specs=[columns, columns, columns, whole] + [ANY_SPEC] * len(extra),
            out_specs=(columns, columns, whole),
        ),
        input_output_aliases={5: 0, 6: 1} if extra else {},
        compiler_params=PARAMS,
        cost_estimate=pl.CostEstimate(flops=2 * length * width * DH, transcendentals=0, bytes_accessed=6 * length * width),
        name="mid",
    )(half, q, g, intra_out, earlier, *extra)


def back_kernel(half_ref, q_ref, k_ref, v_ref, grad_ref, e0_ref, e1_ref, gq_ref, gk_ref, gv_ref):
    mask = causal(q_ref.shape[0])
    early = pl.program_id(0) == half_ref[0]
    for h in range(q_ref.shape[1] // DH):
        q, k, v, grad = (ref[:, head(h)] for ref in (q_ref, k_ref, v_ref, grad_ref))
        e = jnp.where(early, e0_ref[head(h), :], e1_ref[head(h), :])
        scores = jnp.where(mask, dot_nt(q, k), 0.0).astype(BF16)
        grad_scores = jnp.where(mask, dot_nt(grad, v), 0.0).astype(BF16)
        gq_ref[:, head(h)] = (dot_nn(grad_scores, k) + dot_nt(grad, e)).astype(BF16)
        gk_ref[:, head(h)] = dot_tn(grad_scores, q)
        gv_ref[:, head(h)] = dot_tn(scores, grad)


def back(half, q, k, v, grad, e_first, e_second):
    length, width = q.shape
    columns = pl.BlockSpec((length, width // 2), lambda i, half: (0, i))
    whole = pl.BlockSpec(e_first.shape, lambda i, half: (0, 0))
    return pl.pallas_call(
        back_kernel,
        out_shape=(
            jax.ShapeDtypeStruct(q.shape, BF16),
            jax.ShapeDtypeStruct(q.shape, F32),
            jax.ShapeDtypeStruct(q.shape, F32),
        ),
        grid_spec=pltpu.PrefetchScalarGridSpec(
            num_scalar_prefetch=1,
            grid=(2,),
            in_specs=[columns] * 4 + [whole] * 2,
            out_specs=(columns,) * 3,
        ),
        compiler_params=PARAMS,
        cost_estimate=pl.CostEstimate(flops=10 * length * length * width, transcendentals=0, bytes_accessed=18 * length * width),
        name="back",
    )(half, q, k, v, grad, e_first, e_second)


def post_kernel(half_ref, k_ref, v_ref, gk_in_ref, gv_in_ref, l_ref, *refs):
    gk_ref, gv_ref = refs[-2:]
    for h in range(k_ref.shape[1] // DH):
        later = l_ref[head(h), :]
        gk_ref[:, head(h)] = (gk_in_ref[:, head(h)] + dot_nt(v_ref[:, head(h)], later)).astype(BF16)
        gv_ref[:, head(h)] = (gv_in_ref[:, head(h)] + dot_nn(k_ref[:, head(h)], later)).astype(BF16)


def post(half, k, v, gk_in, gv_in, later, filled=None):
    length, width = k.shape
    columns = pl.BlockSpec((length, width // 2), lambda i, half: (0, half[0]))
    whole = pl.BlockSpec(later.shape, lambda i, half: (0, 0))
    extra = () if filled is None else filled
    return pl.pallas_call(
        post_kernel,
        out_shape=(jax.ShapeDtypeStruct(k.shape, BF16), jax.ShapeDtypeStruct(k.shape, BF16)),
        grid_spec=pltpu.PrefetchScalarGridSpec(
            num_scalar_prefetch=1,
            grid=(1,),
            in_specs=[columns] * 4 + [whole] + [ANY_SPEC] * len(extra),
            out_specs=(columns, columns),
        ),
        input_output_aliases={6: 0, 7: 1} if extra else {},
        compiler_params=PARAMS,
        cost_estimate=pl.CostEstimate(flops=2 * length * width * DH, transcendentals=0, bytes_accessed=8 * length * width),
        name="post",
    )(half, k, v, gk_in, gv_in, later, *extra)


def index(value):
    return jnp.asarray(value, jnp.int32).reshape(1)


def shards_four(queries, key_vectors, value_vectors, grad_output):
    out_shape = queries.shape
    q, k, v, g = (x.reshape(x.shape[1:]) for x in (queries, key_vectors, value_vectors, grad_output))
    me = lax.axis_index("ctx")

    def send(x, pairs):
        return lax.ppermute(x, "ctx", pairs)

    flip = jnp.where(me == 0, 0, 1).astype(jnp.int32)
    s1, s2 = states(jnp.stack([flip, 1 - flip]), k, v)
    r1 = send(s1, [(0, 1), (1, 2)])
    r2 = send(s2, [(0, 2), (2, 1)])
    intra_out = intra(q, k, v)
    f1, f2, fs1, fs2 = (x.astype(F32) for x in (r1, r2, s1, s2))
    s3 = (f1 + jnp.where(me == 1, fs2, f2 + fs1)).astype(BF16)
    s4 = (f2 + jnp.where(me == 1, f1 + fs2, 0.0)).astype(BF16)
    r3 = send(s3, [(1, 2), (2, 3)])
    r4 = send(s4, [(1, 3), (2, 1)])
    e_early = jnp.where(me == 1, r1, r3)
    h_early = index(jnp.where(me == 3, 1, 0))
    normed, grad, g_early = mid(h_early, q, g, intra_out, e_early)
    u1 = send(g_early, [(3, 2), (2, 1)])
    e_late = jnp.where(me == 2, (f1 + f2).astype(BF16), r4)
    normed, grad, g_late = mid(1 - h_early, q, g, intra_out, e_late, (normed, grad))
    u2 = send(g_late, [(3, 1), (1, 2)])
    grad_q, gk_in, gv_in = back(h_early, q, k, v, grad, e_early, e_late)
    f1, f2, fe, fl = (x.astype(F32) for x in (u1, u2, g_early, g_late))
    t3 = (f1 + jnp.where(me == 2, fl, f2 + fe)).astype(BF16)
    t4 = (f2 + jnp.where(me == 2, f1 + fl, 0.0)).astype(BF16)
    w3 = send(t3, [(2, 1), (1, 0)])
    w4 = send(t4, [(2, 0), (1, 2)])
    l_early = jnp.where(me == 2, u1, w3)
    p_early = index(jnp.where(me == 0, 0, 1))
    grad_k, grad_v = post(p_early, k, v, gk_in, gv_in, l_early)
    l_late = jnp.where(me == 1, (f1 + f2).astype(BF16), w4)
    grad_k, grad_v = post(1 - p_early, k, v, gk_in, gv_in, l_late, (grad_k, grad_v))
    return tuple(x.reshape(out_shape) for x in (normed, grad_q, grad_k, grad_v))


def scan_states(first, second, count, backward):
    rows = first.shape[0] * 2
    shares = jnp.concatenate([first, second], axis=0).reshape(count, rows // count, DH)
    shares = lax.all_to_all(shares, "ctx", split_axis=0, concat_axis=0, tiled=True).astype(F32)
    running = jnp.cumsum(shares, axis=0)
    sums = running[-1:] - running if backward else running - shares
    sums = lax.all_to_all(sums.astype(BF16), "ctx", split_axis=0, concat_axis=0, tiled=True)
    sums = sums.reshape(rows, DH)
    return sums[: rows // 2], sums[rows // 2 :]


def shards_any(count, queries, key_vectors, value_vectors, grad_output):
    out_shape = queries.shape
    q, k, v, g = (x.reshape(x.shape[1:]) for x in (queries, key_vectors, value_vectors, grad_output))
    s1, s2 = states(jnp.array([0, 1], jnp.int32), k, v)
    e1, e2 = scan_states(s1, s2, count, False)
    intra_out = intra(q, k, v)
    low, high = index(0), index(1)
    normed, grad, g1 = mid(low, q, g, intra_out, e1)
    normed, grad, g2 = mid(high, q, g, intra_out, e2, (normed, grad))
    l1, l2 = scan_states(g1, g2, count, True)
    grad_q, gk_in, gv_in = back(low, q, k, v, grad, e1, e2)
    grad_k, grad_v = post(low, k, v, gk_in, gv_in, l1)
    grad_k, grad_v = post(high, k, v, gk_in, gv_in, l2, (grad_k, grad_v))
    return tuple(x.reshape(out_shape) for x in (normed, grad_q, grad_k, grad_v))


def solution(mesh):
    placed = P(("groups", "dp"), "ctx", "tp")
    count = mesh.shape["ctx"]

    def shards(*args):
        if count == 4:
            return shards_four(*args)
        return shards_any(count, *args)

    return jax.shard_map(
        shards,
        mesh=mesh,
        in_specs=(placed,) * 4,
        out_specs=(placed,) * 4,
        check_vma=False,
    )
```

time: 101 us -> 51.4 us (0.51)
  other arithmetic: 19.9 us -> 0.45 us
  local copies, waits for them, and re-layouts: 21 us -> 2.19 us
  matrix products: 14.8 us -> 0 us
  Pallas kernels: 0 us -> 13.8 us
  starting transfers between devices: 18.1 us -> 12.5 us
  waiting for transfers between devices: 25.7 us -> 21.3 us
    all_to_all x4 -> x0, waiting for transfers between devices: 25.7 us -> none  [the longest x1 12.3 us: shards(): lax.all_to_all(local_state.reshape(1, -1), 'ctx', split_axis=1, concat_ax...]
    ppermute x0 -> x8, waiting for transfers between devices: none -> 21.3 us  [send(): return lax.ppermute(x, 'ctx', pairs)]
    all_to_all x4 -> x0, starting transfers between devices: 18.1 us -> none  [the longest x1 6.32 us: shards(): lax.all_to_all(local_state.reshape(1, -1), 'ctx', split_axis=1, concat_ax...]
    dot_general x12 -> x0, matrix products: 14.8 us -> none  [the longest x1 3.44 us: shards(): jnp.einsum('hts,thd->shd', grad_scores, query_rows, preferred_element_typ...]
    pallas_call x0 -> x7, Pallas kernels: none -> 13.8 us  [the longest x1 4.65 us: back(): pl.pallas_call(back_kernel, out_shape=(jax.ShapeDtypeStruct(q.shape, BF16...]
    ppermute x0 -> x8, starting transfers between devices: none -> 12.5 us  [send(): return lax.ppermute(x, 'ctx', pairs)]
    another operation x4 -> x1, other arithmetic: 8.99 us -> 0.08 us  [shards_four(): s1, s2 = states(jnp.stack([flip, 1 - flip]), k, v)]
    unnamed x32 -> x12, local copies, waits for them, and re-layouts: 10.7 us -> 2.19 us
  transfers between devices with their start and end apart: 4 -> 8, of which waited for: 3 -> 4; matrix products, arithmetic and copies ran while one was open for 15% -> 0% of each run, Pallas kernels for 0% -> 13%
where the time goes in v1:
time: 51.4 us; the launch traced here: 51.1 us
  waiting for transfers between devices  21.3 us (41%)
  Pallas kernels  13.8 us (27%)
  starting transfers between devices  12.5 us (24%)
  local copies, waits for them, and re-layouts  2.19 us (4%)
  between operations  0.83 us (2%)
    ppermute x8, waiting for transfers between devices, send(): return lax.ppermute(x, 'ctx', pairs)  21.3 us
    ppermute x8, starting transfers between devices, send(): return lax.ppermute(x, 'ctx', pairs)  12.5 us
    pallas_call x1, Pallas kernels, back(): pl.pallas_call(back_kernel, out_shape=(jax.ShapeDtypeStruct(q.shape, BF16...  4.65 us
    pallas_call x2, Pallas kernels, mid(): pl.pallas_call(mid_kernel, out_shape=(jax.ShapeDtypeStruct(q.shape, BF16)...  3.64 us
    pallas_call x2, Pallas kernels, post(): pl.pallas_call(post_kernel, out_shape=(jax.ShapeDtypeStruct(k.shape, BF16...  2.36 us
    unnamed x12, local copies, waits for them, and re-layouts  2.19 us
    pallas_call x1, Pallas kernels, intra(): pl.pallas_call(intra_kernel, out_shape=jax.ShapeDtypeStruct(q.shape, F32)...  2.1 us
    pallas_call x1, Pallas kernels, states(): pl.pallas_call(state_kernel, out_shape=(shape, shape), in_specs=[pl.Block...  1.06 us
  transfers between devices with their start and end apart: 8, of which 4 were waited for; matrix products, arithmetic and copies ran while one was open for 0% of the time, Pallas kernels for 13%

profile of v1, /device:TPU:0, one launch (start us, length us, event | category | flops | bytes accessed | tf_op | source)
XLA Modules:
  0.0 51.1 jit_solution(557341153729133997)
XLA Ops:
  0.7 1.1 %copy-done = bf16[1,320,1024]{2,1,0:T(8,128)(2,1)S(1)} copy-done((bf16[1,320,1024]{2,1,0:T(8,128)(2,1)S(1)}, bf16[1,320,1024]{2,1,0:T(8,128)(2,1)}, u32[]{:S(2)}) %copy-start) | copy-done | bytes 655384
  1.8 1.1 %copy-done.2 = bf16[1,320,1024]{2,1,0:T(8,128)(2,1)S(1)} copy-done((bf16[1,320,1024]{2,1,0:T(8,128)(2,1)S(1)}, bf16[1,320,1024]{2,1,0:T(8,128)(2,1)}, u32[]{:S(2)}) %copy-start.2) | copy-done | bytes 655384
  2.9 1.1 %states.1 = (bf16[512,128]{1,0:T(8,128)(2,1)S(1)}, bf16[512,128]{1,0:T(8,128)(2,1)S(1)}) custom-call(s32[2]{0:T(128)S(1)} %pad_add_fusion.order_ref, bf16[320,1024]{1,0:T(8,128)(2,1)S(1)} %bitcast.11, bf16[320,1024]{1,0:T(8,128)(2,1)S(1)} %bitcast.16), custom_call_target="tpu_custom_call" | custom-call | tf_op jit(solution)/shard_map/states/pallas_call | solution.py:52
  4.0 4.9 %collective-permute-start = (bf16[512,128]{1,0:T(8,128)(2,1)S(1)}, bf16[512,128]{1,0:T(8,128)(2,1)S(1)}, u32[]{:S(2)}, u32[]{:S(2)}) collective-permute-start(bf16[512,128]{1,0:T(8,128)(2,1)S(1)} %get-tuple-element.19), channel_id=1, source_target_pairs={{0,4},{4,8},{1,5},{5,9},{2,6},{6,10},{3,7},{7,11},{16,20},{20,24},... | collective-permute-start | bytes 393224 | tf_op jit(solution)/shard_map/ppermute | solution.py:201
  8.9 2.3 %collective-permute-start.1 = (bf16[512,128]{1,0:T(8,128)(2,1)S(1)}, bf16[512,128]{1,0:T(8,128)(2,1)S(1)}, u32[]{:S(2)}, u32[]{:S(2)}) collective-permute-start(bf16[512,128]{1,0:T(8,128)(2,1)S(1)} %get-tuple-element.20), channel_id=1, source_target_pairs={{0,8},{8,4},{1,9},{9,5},{2,10},{10,6},{3,11},{11,7},{16,24},{24,20... | collective-permute-start | bytes 393224 | tf_op jit(solution)/shard_map/ppermute | solution.py:201
  11.2 0.9 %collective-permute-done = bf16[512,128]{1,0:T(8,128)(2,1)S(1)} collective-permute-done((bf16[512,128]{1,0:T(8,128)(2,1)S(1)}, bf16[512,128]{1,0:T(8,128)(2,1)S(1)}, u32[]{:S(2)}, u32[]{:S(2)}) %collective-permute-start) | collective-permute-done | bytes 131104 | tf_op jit(solution)/shard_map/ppermute | solution.py:201
  12.1 2.4 %collective-permute-done.1 = bf16[512,128]{1,0:T(8,128)(2,1)S(1)} collective-permute-done((bf16[512,128]{1,0:T(8,128)(2,1)S(1)}, bf16[512,128]{1,0:T(8,128)(2,1)S(1)}, u32[]{:S(2)}, u32[]{:S(2)}) %collective-permute-start.1) | collective-permute-done | bytes 131104 | tf_op jit(solution)/shard_map/ppermute | solution.py:201
  14.5 0.1 fusion.1
  14.6 0.7 %collective-permute-start.3 = (bf16[512,128]{1,0:T(8,128)(2,1)S(1)}, bf16[512,128]{1,0:T(8,128)(2,1)S(1)}, u32[]{:S(2)}, u32[]{:S(2)}) collective-permute-start(bf16[512,128]{1,0:T(8,128)(2,1)S(1)} %get-tuple-element.36), channel_id=1, source_target_pairs={{4,8},{8,12},{5,9},{9,13},{6,10},{10,14},{7,11},{11,15},{20,24},{2... | collective-permute-start | bytes 393224 | tf_op jit(solution)/shard_map/ppermute | solution.py:201
  15.3 0.7 %collective-permute-start.2 = (bf16[512,128]{1,0:T(8,128)(2,1)S(1)}, bf16[512,128]{1,0:T(8,128)(2,1)S(1)}, u32[]{:S(2)}, u32[]{:S(2)}) collective-permute-start(bf16[512,128]{1,0:T(8,128)(2,1)S(1)} %get-tuple-element.37), channel_id=1, source_target_pairs={{4,12},{8,4},{5,13},{9,5},{6,14},{10,6},{7,15},{11,7},{20,28},{24,... | collective-permute-start | bytes 393224 | tf_op jit(solution)/shard_map/ppermute | solution.py:201
  16.0 2.1 %intra.1.intra_ref = f32[320,1024]{1,0:T(8,128)S(1)} custom-call(bf16[320,1024]{1,0:T(8,128)(2,1)S(1)} %bitcast.21, bf16[320,1024]{1,0:T(8,128)(2,1)S(1)} %bitcast.12, bf16[320,1024]{1,0:T(8,128)(2,1)S(1)} %bitcast.17), custom_call_target="tpu_custom_call" | custom-call | flops 419430400 | bytes 3276800 | tf_op jit(solution)/shard_map/intra/pallas_call | solution.py:74
  18.1 0.1 broadcast_select_fusion
  18.2 1.8 %mid.2 = (bf16[320,1024]{1,0:T(8,128)(2,1)}, bf16[320,1024]{1,0:T(8,128)(2,1)S(1)}, bf16[512,128]{1,0:T(8,128)(2,1)S(1)}) custom-call(s32[1]{0:T(128)} %bitcast.half_ref, bf16[320,1024]{1,0:T(8,128)(2,1)S(1)} %bitcast.22, bf16[320,1024]{1,0:T(8,128)(2,1)S(1)} %bitcast.25, f32[320,1024]{1,0:T(8,128)S(1)} %intra.1.intra_ref, ...), custom_call_target="tpu_custom_call" | custom-call | flops 83886080 | bytes 1966080 | tf_op jit(solution)/shard_map/mid/pallas_call | solution.py:106
  20.0 1.8 %mid.3 = (bf16[320,1024]{1,0:T(8,128)(2,1)}, bf16[320,1024]{1,0:T(8,128)(2,1)S(1)}, bf16[512,128]{1,0:T(8,128)(2,1)S(1)}) custom-call(s32[1]{0:T(128)S(6)} %sub.9.half_ref, bf16[320,1024]{1,0:T(8,128)(2,1)S(1)} %bitcast.23, bf16[320,1024]{1,0:T(8,128)(2,1)S(1)} %bitcast.26, ...), custom_call_target="tpu_custom_call", output_to_operand_aliasing={{0}: (5, {}), {1}: (6, {})} | custom-call | flops 83886080 | bytes 1966080 | tf_op jit(solution)/shard_map/mid/pallas_call | solution.py:106
  21.9 0.7 %collective-permute-start.5 = (bf16[512,128]{1,0:T(8,128)(2,1)S(1)}, bf16[512,128]{1,0:T(8,128)(2,1)S(1)}, u32[]{:S(2)}, u32[]{:S(2)}) collective-permute-start(bf16[512,128]{1,0:T(8,128)(2,1)S(1)} %get-tuple-element.29), channel_id=1, source_target_pairs={{12,4},{4,8},{13,5},{5,9},{14,6},{6,10},{15,7},{7,11},{28,20},{20,... | collective-permute-start | bytes 393224 | tf_op jit(solution)/shard_map/ppermute | solution.py:201
  22.5 0.7 %collective-permute-start.4 = (bf16[512,128]{1,0:T(8,128)(2,1)S(1)}, bf16[512,128]{1,0:T(8,128)(2,1)S(1)}, u32[]{:S(2)}, u32[]{:S(2)}) collective-permute-start(bf16[512,128]{1,0:T(8,128)(2,1)S(1)} %get-tuple-element.28), channel_id=1, source_target_pairs={{12,8},{8,4},{13,9},{9,5},{14,10},{10,6},{15,11},{11,7},{28,24},{2... | collective-permute-start | bytes 393224 | tf_op jit(solution)/shard_map/ppermute | solution.py:201
  23.2 0.1 fusion.5
  23.3 1.3 %collective-permute-start.7 = (bf16[512,128]{1,0:T(8,128)(2,1)S(1)}, bf16[512,128]{1,0:T(8,128)(2,1)S(1)}, u32[]{:S(2)}, u32[]{:S(2)}) collective-permute-start(bf16[512,128]{1,0:T(8,128)(2,1)S(1)} %get-tuple-element.34), channel_id=1, source_target_pairs={{8,4},{4,0},{9,5},{5,1},{10,6},{6,2},{11,7},{7,3},{24,20},{20,16},... | collective-permute-start | bytes 393224 | tf_op jit(solution)/shard_map/ppermute | solution.py:201
  24.6 1.3 %collective-permute-start.6 = (bf16[512,128]{1,0:T(8,128)(2,1)S(1)}, bf16[512,128]{1,0:T(8,128)(2,1)S(1)}, u32[]{:S(2)}, u32[]{:S(2)}) collective-permute-start(bf16[512,128]{1,0:T(8,128)(2,1)S(1)} %get-tuple-element.35), channel_id=1, source_target_pairs={{8,0},{4,8},{9,1},{5,9},{10,2},{6,10},{11,3},{7,11},{24,16},{20,24... | collective-permute-start | bytes 393224 | tf_op jit(solution)/shard_map/ppermute | solution.py:201
  25.9 4.7 %back.1 = (bf16[320,1024]{1,0:T(8,128)(2,1)}, f32[320,1024]{1,0:T(8,128)S(1)}, f32[320,1024]{1,0:T(8,128)S(1)}) custom-call(s32[1]{0:T(128)} %bitcast.half_ref, bf16[320,1024]{1,0:T(8,128)(2,1)S(1)} %bitcast.24, bf16[320,1024]{1,0:T(8,128)(2,1)S(1)} %bitcast.13, bf16[320,1024]{1,0:T(8,128)(2,1)S(1)} %bitcast.18, ...), custom_call_target="tpu_custom_call" | custom-call | flops 1048576000 | bytes 5898240 | tf_op jit(solution)/shard_map/back/pallas_call | solution.py:143
  30.6 15.3 %collective-permute-done.7 = bf16[512,128]{1,0:T(8,128)(2,1)S(1)} collective-permute-done((bf16[512,128]{1,0:T(8,128)(2,1)S(1)}, bf16[512,128]{1,0:T(8,128)(2,1)S(1)}, u32[]{:S(2)}, u32[]{:S(2)}) %collective-permute-start.7) | collective-permute-done | bytes 131104 | tf_op jit(solution)/shard_map/ppermute | solution.py:201
  45.9 2.8 %collective-permute-done.6 = bf16[512,128]{1,0:T(8,128)(2,1)S(1)} collective-permute-done((bf16[512,128]{1,0:T(8,128)(2,1)S(1)}, bf16[512,128]{1,0:T(8,128)(2,1)S(1)}, u32[]{:S(2)}, u32[]{:S(2)}) %collective-permute-start.6) | collective-permute-done | bytes 131104 | tf_op jit(solution)/shard_map/ppermute | solution.py:201
  48.7 1.2 %post.2 = (bf16[320,1024]{1,0:T(8,128)(2,1)}, bf16[320,1024]{1,0:T(8,128)(2,1)}) custom-call(s32[1]{0:T(128)} %bitcast.5.half_ref, bf16[320,1024]{1,0:T(8,128)(2,1)S(1)} %bitcast.14, bf16[320,1024]{1,0:T(8,128)(2,1)S(1)} %bitcast.19, f32[320,1024]{1,0:T(8,128)S(1)} %get-tuple-element.26.gk_in_ref, f32[320,1024]{1,0:T(8,128)S(1)} %get-tuple-element.27.gv_in_ref, ...), custom_call_target="tpu_custom_call" | custom-call | flops 83886080 | bytes 2621440 | tf_op jit(solution)/shard_map/post/pallas_call | solution.py:175
  49.9 1.2 %post.3 = (bf16[320,1024]{1,0:T(8,128)(2,1)}, bf16[320,1024]{1,0:T(8,128)(2,1)}) custom-call(s32[1]{0:T(128)S(6)} %sub.11.half_ref, bf16[320,1024]{1,0:T(8,128)(2,1)S(1)} %bitcast.15, bf16[320,1024]{1,0:T(8,128)(2,1)S(1)} %bitcast.20, f32[320,1024]{1,0:T(8,128)S(1)} %get-tuple-element.26.gk_in_ref, ...), custom_call_target="tpu_custom_call", output_to_operand_aliasing={{0}: (6, {}), {1}: (7, {})} | custom-call | flops 83886080 | bytes 2621440 | tf_op jit(solution)/shard_map/post/pallas_call | solution.py:175
  (16 shorter events, 0.2 us)
Async XLA Ops:
  0.7 1.1 %copy-start = (bf16[1,320,1024]{2,1,0:T(8,128)(2,1)S(1)}, bf16[1,320,1024]{2,1,0:T(8,128)(2,1)}, u32[]{:S(2)}) copy-start(bf16[1,320,1024]{2,1,0:T(8,128)(2,1)} %param.5) | copy-start | bytes 1966084
  1.8 1.1 %copy-start.2 = (bf16[1,320,1024]{2,1,0:T(8,128)(2,1)S(1)}, bf16[1,320,1024]{2,1,0:T(8,128)(2,1)}, u32[]{:S(2)}) copy-start(bf16[1,320,1024]{2,1,0:T(8,128)(2,1)} %param.6) | copy-start | bytes 1966084
  2.9 13.1 %copy-start.1 = (bf16[1,320,1024]{2,1,0:T(8,128)(2,1)S(1)}, bf16[1,320,1024]{2,1,0:T(8,128)(2,1)}, u32[]{:S(2)}) copy-start(bf16[1,320,1024]{2,1,0:T(8,128)(2,1)} %param.5) | copy-start | bytes 1966084
  2.9 13.1 %copy-start.3 = (bf16[1,320,1024]{2,1,0:T(8,128)(2,1)S(1)}, bf16[1,320,1024]{2,1,0:T(8,128)(2,1)}, u32[]{:S(2)}) copy-start(bf16[1,320,1024]{2,1,0:T(8,128)(2,1)} %param.6) | copy-start | bytes 1966084
  2.9 13.1 %copy-start.4 = (bf16[1,320,1024]{2,1,0:T(8,128)(2,1)S(1)}, bf16[1,320,1024]{2,1,0:T(8,128)(2,1)}, u32[]{:S(2)}) copy-start(bf16[1,320,1024]{2,1,0:T(8,128)(2,1)} %param.4) | copy-start | bytes 1966084
  4.0 8.1 %collective-permute-start = (bf16[512,128]{1,0:T(8,128)(2,1)S(1)}, bf16[512,128]{1,0:T(8,128)(2,1)S(1)}, u32[]{:S(2)}, u32[]{:S(2)}) collective-permute-start(bf16[512,128]{1,0:T(8,128)(2,1)S(1)} %get-tuple-element.19), channel_id=1, source_target_pairs={{0,4},{4,8},{1,5},{5,9},{2,6},{6,10},{3,7},{7,11},{16,20},{20,24},... | collective-permute-start | bytes 393224 | tf_op jit(solution)/shard_map/ppermute | solution.py:201
  8.9 5.6 %collective-permute-start.1 = (bf16[512,128]{1,0:T(8,128)(2,1)S(1)}, bf16[512,128]{1,0:T(8,128)(2,1)S(1)}, u32[]{:S(2)}, u32[]{:S(2)}) collective-permute-start(bf16[512,128]{1,0:T(8,128)(2,1)S(1)} %get-tuple-element.20), channel_id=1, source_target_pairs={{0,8},{8,4},{1,9},{9,5},{2,10},{10,6},{3,11},{11,7},{16,24},{24,20... | collective-permute-start | bytes 393224 | tf_op jit(solution)/shard_map/ppermute | solution.py:201
  14.6 3.5 %collective-permute-start.3 = (bf16[512,128]{1,0:T(8,128)(2,1)S(1)}, bf16[512,128]{1,0:T(8,128)(2,1)S(1)}, u32[]{:S(2)}, u32[]{:S(2)}) collective-permute-start(bf16[512,128]{1,0:T(8,128)(2,1)S(1)} %get-tuple-element.36), channel_id=1, source_target_pairs={{4,8},{8,12},{5,9},{9,13},{6,10},{10,14},{7,11},{11,15},{20,24},{2... | collective-permute-start | bytes 393224 | tf_op jit(solution)/shard_map/ppermute | solution.py:201
  15.3 2.8 %collective-permute-start.2 = (bf16[512,128]{1,0:T(8,128)(2,1)S(1)}, bf16[512,128]{1,0:T(8,128)(2,1)S(1)}, u32[]{:S(2)}, u32[]{:S(2)}) collective-permute-start(bf16[512,128]{1,0:T(8,128)(2,1)S(1)} %get-tuple-element.37), channel_id=1, source_target_pairs={{4,12},{8,4},{5,13},{9,5},{6,14},{10,6},{7,15},{11,7},{20,28},{24,... | collective-permute-start | bytes 393224 | tf_op jit(solution)/shard_map/ppermute | solution.py:201
  16.0 2.2 %copy-start.5 = (bf16[1,320,1024]{2,1,0:T(8,128)(2,1)S(1)}, bf16[1,320,1024]{2,1,0:T(8,128)(2,1)}, u32[]{:S(2)}) copy-start(bf16[1,320,1024]{2,1,0:T(8,128)(2,1)} %param.7) | copy-start | bytes 1966084
  21.9 1.3 %collective-permute-start.5 = (bf16[512,128]{1,0:T(8,128)(2,1)S(1)}, bf16[512,128]{1,0:T(8,128)(2,1)S(1)}, u32[]{:S(2)}, u32[]{:S(2)}) collective-permute-start(bf16[512,128]{1,0:T(8,128)(2,1)S(1)} %get-tuple-element.29), channel_id=1, source_target_pairs={{12,4},{4,8},{13,5},{5,9},{14,6},{6,10},{15,7},{7,11},{28,20},{20,... | collective-permute-start | bytes 393224 | tf_op jit(solution)/shard_map/ppermute | solution.py:201
  22.5 0.7 %collective-permute-start.4 = (bf16[512,128]{1,0:T(8,128)(2,1)S(1)}, bf16[512,128]{1,0:T(8,128)(2,1)S(1)}, u32[]{:S(2)}, u32[]{:S(2)}) collective-permute-start(bf16[512,128]{1,0:T(8,128)(2,1)S(1)} %get-tuple-element.28), channel_id=1, source_target_pairs={{12,8},{8,4},{13,9},{9,5},{14,10},{10,6},{15,11},{11,7},{28,24},{2... | collective-permute-start | bytes 393224 | tf_op jit(solution)/shard_map/ppermute | solution.py:201
  23.3 22.5 %collective-permute-start.7 = (bf16[512,128]{1,0:T(8,128)(2,1)S(1)}, bf16[512,128]{1,0:T(8,128)(2,1)S(1)}, u32[]{:S(2)}, u32[]{:S(2)}) collective-permute-start(bf16[512,128]{1,0:T(8,128)(2,1)S(1)} %get-tuple-element.34), channel_id=1, source_target_pairs={{8,4},{4,0},{9,5},{5,1},{10,6},{6,2},{11,7},{7,3},{24,20},{20,16},... | collective-permute-start | bytes 393224 | tf_op jit(solution)/shard_map/ppermute | solution.py:201
  24.6 24.0 %collective-permute-start.6 = (bf16[512,128]{1,0:T(8,128)(2,1)S(1)}, bf16[512,128]{1,0:T(8,128)(2,1)S(1)}, u32[]{:S(2)}, u32[]{:S(2)}) collective-permute-start(bf16[512,128]{1,0:T(8,128)(2,1)S(1)} %get-tuple-element.35), channel_id=1, source_target_pairs={{8,0},{4,8},{9,1},{5,9},{10,2},{6,10},{11,3},{7,11},{24,16},{20,24... | collective-permute-start | bytes 393224 | tf_op jit(solution)/shard_map/ppermute | solution.py:201

commit v2 on v0

v2 whole, which is shorter than its diff:
```python
import functools

import jax
import jax.numpy as jnp
from jax import lax
from jax.experimental import pallas as pl
from jax.experimental.pallas import tpu as pltpu
from jax.sharding import PartitionSpec as P

DH = 128
norm_eps = 1e-06
F32 = jnp.float32
BF16 = jnp.bfloat16

VMEM_SPEC = pl.BlockSpec(memory_space=pltpu.VMEM)
HBM_SPEC = pl.BlockSpec(memory_space=pltpu.HBM)
SMEM_SPEC = pl.BlockSpec(memory_space=pltpu.SMEM)
PARAMS = pltpu.CompilerParams(vmem_limit_bytes=16 << 20)


def cost(flops, moved):
    return pl.CostEstimate(flops=flops, transcendentals=0, bytes_accessed=moved)


def dot_nn(a, b):
    return lax.dot_general(a, b, (((1,), (0,)), ((), ())), preferred_element_type=F32)


def dot_nt(a, b):
    return lax.dot_general(a, b, (((1,), (1,)), ((), ())), preferred_element_type=F32)


def dot_tn(a, b):
    return lax.dot_general(a, b, (((0,), (0,)), ((), ())), preferred_element_type=F32)


def head(index):
    return slice(index * DH, (index + 1) * DH)


def causal(length):
    rows = lax.broadcasted_iota(jnp.int32, (length, length), 0)
    columns = lax.broadcasted_iota(jnp.int32, (length, length), 1)
    return columns <= rows


def half_columns(half, h, heads):
    return pl.ds(pl.multiple_of((half * heads + h) * DH, DH), DH)


def load_kernel(half_of, me_ref, k_ref, v_ref, out_ref, k_out, v_out, k_sem, v_sem):
    heads = out_ref.shape[0] // DH
    half = half_of(me_ref[0])
    copies = []
    for h in range(2 * heads):
        cols = half_columns(half if h < heads else 1 - half, h % heads, heads)
        pair = (
            pltpu.make_async_copy(k_ref.at[:, cols], k_out.at[:, cols], k_sem.at[h]),
            pltpu.make_async_copy(v_ref.at[:, cols], v_out.at[:, cols], v_sem.at[h]),
        )
        for copy in pair:
            copy.start()
        copies.append((cols, pair))
    for h, (cols, pair) in enumerate(copies):
        for copy in pair:
            copy.wait()
        if h < heads:
            out_ref[head(h), :] = dot_tn(k_out[:, cols], v_out[:, cols]).astype(BF16)


def load_states(half_of, me, k, v):
    length, width = k.shape
    heads = width // DH
    k, v = (pltpu.with_memory_space_constraint(x, pltpu.HBM) for x in (k, v))
    whole = jax.ShapeDtypeStruct(k.shape, BF16)
    return pl.pallas_call(
        functools.partial(load_kernel, half_of),
        out_shape=(jax.ShapeDtypeStruct((width // 2, DH), BF16), whole, whole),
        in_specs=[SMEM_SPEC, HBM_SPEC, HBM_SPEC],
        out_specs=(VMEM_SPEC,) * 3,
        scratch_shapes=[pltpu.SemaphoreType.DMA((heads,))] * 2,
        compiler_params=PARAMS,
        cost_estimate=cost(length * width * DH, 8 * length * width),
        name="load_states",
    )(me, k, v)


def state_kernel(half_of, me_ref, k_ref, v_ref, out_ref):
    heads = out_ref.shape[0] // DH
    half = half_of(me_ref[0])
    for h in range(heads):
        cols = half_columns(half, h, heads)
        out_ref[head(h), :] = dot_tn(k_ref[:, cols], v_ref[:, cols]).astype(BF16)


def states(half_of, me, k, v):
    length, width = k.shape
    return pl.pallas_call(
        functools.partial(state_kernel, half_of),
        out_shape=jax.ShapeDtypeStruct((width // 2, DH), BF16),
        in_specs=[SMEM_SPEC, VMEM_SPEC, VMEM_SPEC],
        out_specs=VMEM_SPEC,
        compiler_params=PARAMS,
        cost_estimate=cost(length * width * DH, 2 * length * width),
        name="states",
    )(me, k, v)


def intra_kernel(q_ref, k_ref, v_ref, out_ref, qt_ref, token_ref):
    mask = causal(q_ref.shape[0])
    for h in range(q_ref.shape[1] // DH):
        q = q_ref[:, head(h)]
        scores = jnp.where(mask, dot_nt(q, k_ref[:, head(h)]), 0.0).astype(BF16)
        out_ref[:, head(h)] = dot_nn(scores, v_ref[:, head(h)])
        qt_ref[head(h), :] = q.T
    token_ref[...] = jnp.zeros_like(token_ref)


TOKEN = jax.ShapeDtypeStruct((8, DH), F32)


def intra(q, k, v):
    length, width = q.shape
    return pl.pallas_call(
        intra_kernel,
        out_shape=(jax.ShapeDtypeStruct(q.shape, F32), jax.ShapeDtypeStruct((width, length), BF16), TOKEN),
        in_specs=[VMEM_SPEC] * 3,
        out_specs=(VMEM_SPEC,) * 3,
        compiler_params=PARAMS,
        cost_estimate=cost(4 * length * length * width, 12 * length * width),
        name="intra",
    )(q, k, v)


def add_kernel(a_ref, b_ref, token_ref, out_ref):
    out_ref[...] = (a_ref[...].astype(F32) + b_ref[...].astype(F32)).astype(BF16)


def add(a, b, token):
    return pl.pallas_call(
        add_kernel,
        out_shape=jax.ShapeDtypeStruct(a.shape, BF16),
        in_specs=[VMEM_SPEC] * 3,
        out_specs=VMEM_SPEC,
        compiler_params=PARAMS,
        cost_estimate=cost(a.size, 6 * a.size),
        name="add",
    )(a, b, token)


def combine_kernel(turn, me_ref, r1_ref, r2_ref, a_ref, b_ref, token_ref, x_ref, y_ref, both_ref):
    near = me_ref[0] == turn
    r1, r2, a, b = (ref[...].astype(F32) for ref in (r1_ref, r2_ref, a_ref, b_ref))
    x_ref[...] = (r1 + r2 + a).astype(BF16)
    y_ref[...] = (r2 + jnp.where(near, r1 + b, 0.0)).astype(BF16)
    both_ref[...] = (r1 + r2).astype(BF16)


def combine(turn, me, r1, r2, a, b, token):
    shape = jax.ShapeDtypeStruct(r1.shape, BF16)
    return pl.pallas_call(
        functools.partial(combine_kernel, turn),
        out_shape=(shape,) * 3,
        in_specs=[SMEM_SPEC] + [VMEM_SPEC] * 5,
        out_specs=(VMEM_SPEC,) * 3,
        compiler_params=PARAMS,
        cost_estimate=cost(r1.size, 10 * r1.size),
        name="combine",
    )(me, r1, r2, a, b, token)


def pick(me, choices, refs, rows):
    value = refs[-1][rows, :]
    for turn, ref in zip(choices, refs[:-1]):
        value = jnp.where(me == turn, ref[rows, :], value)
    return value


def mid_kernel(half_of, turns, me_ref, q_ref, qt_ref, g_ref, intra_ref, token_ref, *refs):
    e_refs, (normed_ref, grad_ref, state_ref, done_ref) = refs[:-4], refs[-4:]
    heads = state_ref.shape[0] // DH
    half = half_of(me_ref[0])
    for h in range(heads):
        cols = half_columns(half, h, heads)
        earlier = pick(me_ref[0], turns, e_refs, head(h))
        mixed = intra_ref[:, cols] + dot_nn(q_ref[:, cols], earlier)
        g = g_ref[:, cols].astype(F32)
        inverse = lax.rsqrt(jnp.mean(mixed * mixed, axis=-1, keepdims=True) + norm_eps)
        along = jnp.mean(g * mixed, axis=-1, keepdims=True) * inverse
        normed = mixed * inverse
        grad = (inverse * (g - normed * along)).astype(BF16)
        grad_ref[:, head(h)] = grad
        state_ref[head(h), :] = dot_nn(qt_ref[cols, :], grad).astype(BF16)
        normed_ref[:, head(h)] = normed.astype(BF16)
    done_ref[...] = jnp.zeros_like(done_ref)


def mid(half_of, turns, me, q, qt, g, intra_out, token, earlier):
    length, width = q.shape
    half_shape = jax.ShapeDtypeStruct((length, width // 2), BF16)
    return pl.pallas_call(
        functools.partial(mid_kernel, half_of, turns),
        out_shape=(half_shape, half_shape, jax.ShapeDtypeStruct(earlier[0].shape, BF16), TOKEN),
        in_specs=[SMEM_SPEC] + [VMEM_SPEC] * (5 + len(earlier)),
        out_specs=(VMEM_SPEC,) * 4,
        compiler_params=PARAMS,
        cost_estimate=cost(2 * length * width * DH, 6 * length * width),
        name="mid",
    )(me, q, qt, g, intra_out, token, *earlier)


def back_kernel(half_of, turns, me_ref, q_ref, k_ref, v_ref, grad_ref, normed_in_ref, *refs):
    e_refs, (normed_ref, gq_ref, gk_ref, gv_ref, token_ref, gq_buf, gq_sem, normed_sem) = refs[: len(turns) + 1], refs[-8:]
    length = q_ref.shape[0]
    rows = lax.broadcasted_iota(jnp.int32, (length, length), 0)
    columns = lax.broadcasted_iota(jnp.int32, (length, length), 1)
    mask, mask_t = columns <= rows, rows <= columns
    heads = gk_ref.shape[1] // DH
    half = half_of(me_ref[0])
    copies = []
    for h in range(heads):
        cols = half_columns(half, h, heads)
        copies.append(pltpu.make_async_copy(normed_in_ref.at[:, head(h)], normed_ref.at[:, cols], normed_sem.at[h]))
        copies[-1].start()
    for h in range(heads):
        cols = half_columns(half, h, heads)
        q, k, v = (ref[:, cols] for ref in (q_ref, k_ref, v_ref))
        grad = grad_ref[:, head(h)]
        earlier = pick(me_ref[0], turns, e_refs, head(h))
        scores_t = jnp.where(mask_t, dot_nt(k, q), 0.0).astype(BF16)
        grad_scores = jnp.where(mask, dot_nt(grad, v), 0.0).astype(BF16)
        grad_scores_t = jnp.where(mask_t, dot_nt(v, grad), 0.0).astype(BF16)
        gq_buf[h] = (dot_nn(grad_scores, k) + dot_nt(grad, earlier)).astype(BF16)
        copies.append(pltpu.make_async_copy(gq_buf.at[h], gq_ref.at[:, cols], gq_sem.at[h]))
        copies[-1].start()
        gk_ref[:, head(h)] = dot_nn(grad_scores_t, q)
        gv_ref[:, head(h)] = dot_nn(scores_t, grad)
    token_ref[...] = jnp.zeros_like(token_ref)
    for copy in copies:
        copy.wait()


def back(half_of, turns, me, q, k, v, grad, normed, earlier, filled=()):
    length, width = q.shape
    heads = width // (2 * DH)
    whole = jax.ShapeDtypeStruct(q.shape, BF16)
    half_shape = jax.ShapeDtypeStruct((length, width // 2), F32)
    first_filled = 6 + len(earlier)
    return pl.pallas_call(
        functools.partial(back_kernel, half_of, turns),
        out_shape=(whole, whole, half_shape, half_shape, TOKEN),
        in_specs=[SMEM_SPEC] + [VMEM_SPEC] * (5 + len(earlier)) + [HBM_SPEC] * len(filled),
        out_specs=(HBM_SPEC, HBM_SPEC, VMEM_SPEC, VMEM_SPEC, VMEM_SPEC),
        scratch_shapes=[pltpu.VMEM((heads, length, DH), BF16)] + [pltpu.SemaphoreType.DMA((heads,))] * 2,
        input_output_aliases={first_filled: 0, first_filled + 1: 1} if filled else {},
        compiler_params=PARAMS,
        cost_estimate=cost(6 * length * length * width, 9 * length * width),
        name="back",
    )(me, q, k, v, grad, normed, *earlier, *filled)


def post_kernel(half_of, turns, me_ref, k_ref, v_ref, gk_in_ref, gv_in_ref, token_ref, *refs):
    l_refs, (gk_ref, gv_ref, gk_buf, gv_buf, gk_sem, gv_sem) = refs[: len(turns) + 1], refs[-6:]
    heads = gk_in_ref.shape[1] // DH
    half = half_of(me_ref[0])
    copies = []
    for h in range(heads):
        cols = half_columns(half, h, heads)
        later = pick(me_ref[0], turns, l_refs, head(h))
        gk_buf[h] = (gk_in_ref[:, head(h)] + dot_nt(v_ref[:, cols], later)).astype(BF16)
        copies.append(pltpu.make_async_copy(gk_buf.at[h], gk_ref.at[:, cols], gk_sem.at[h]))
        copies[-1].start()
        gv_buf[h] = (gv_in_ref[:, head(h)] + dot_nn(k_ref[:, cols], later)).astype(BF16)
        copies.append(pltpu.make_async_copy(gv_buf.at[h], gv_ref.at[:, cols], gv_sem.at[h]))
        copies[-1].start()
    for copy in copies:
        copy.wait()


def post(half_of, turns, me, k, v, gk_in, gv_in, token, later, filled=()):
    length, width = k.shape
    heads = width // (2 * DH)
    first_filled = 6 + len(later)
    return pl.pallas_call(
        functools.partial(post_kernel, half_of, turns),
        out_shape=(jax.ShapeDtypeStruct(k.shape, BF16), jax.ShapeDtypeStruct(k.shape, BF16)),
        in_specs=[SMEM_SPEC] + [VMEM_SPEC] * (5 + len(later)) + [HBM_SPEC] * len(filled),
        out_specs=(HBM_SPEC, HBM_SPEC),
        scratch_shapes=[pltpu.VMEM((heads, length, DH), BF16)] * 2 + [pltpu.SemaphoreType.DMA((heads,))] * 2,
        input_output_aliases={first_filled: 0, first_filled + 1: 1} if filled else {},
        compiler_params=PARAMS,
        cost_estimate=cost(2 * length * width * DH, 8 * length * width),
        name="post",
    )(me, k, v, gk_in, gv_in, token, *later, *filled)


def ends_half(me):
    return jnp.where((me == 0) | (me == 3), 1, 0)


def inner_half(me):
    return 1 - ends_half(me)


def zero_half(me):
    return jnp.where(me == 0, 0, 1)


def rest_half(me):
    return 1 - zero_half(me)


def rows_of(array):
    return array.reshape(array.shape[1:])


def shards_four(queries, key_vectors, value_vectors, grad_output):
    out_shape = queries.shape
    q, k, v, g = (rows_of(x) for x in (queries, key_vectors, value_vectors, grad_output))
    me = lax.axis_index("ctx").astype(jnp.int32).reshape(1)

    def send(x, pairs):
        return lax.ppermute(x, "ctx", pairs)

    s1, k, v = load_states(zero_half, me, k, v)
    r1 = send(s1, [(0, 1), (1, 2)])
    s2 = states(rest_half, me, k, v)
    r2 = send(s2, [(0, 2), (2, 1)])
    intra_out, qt, token = intra(q, k, v)
    r3b = send(add(r1, s2, token), [(1, 2)])
    s3, s4, r12 = combine(1, me, r1, r2, s1, s2, token)
    r3a = send(s3, [(2, 3)])
    r4 = send(s4, [(1, 3), (2, 1)])
    e_early = (r1, r3b, r3a)
    e_late = (r12, r4)
    normed_early, grad_early, g_early, token = mid(ends_half, (1, 2), me, q, qt, g, intra_out, token, e_early)
    u1 = send(g_early, [(3, 2), (2, 1)])
    normed_late, grad_late, g_late, token = mid(inner_half, (2,), me, q, qt, g, intra_out, token, e_late)
    u2 = send(g_late, [(3, 1), (1, 2)])
    normed, grad_q, gk_late, gv_late, token = back(inner_half, (2,), me, q, k, v, grad_late, normed_late, e_late)
    w3b = send(add(u1, g_late, token), [(2, 1)])
    t3, t4, u12 = combine(2, me, u1, u2, g_early, g_late, token)
    w3a = send(t3, [(1, 0)])
    w4 = send(t4, [(2, 0), (1, 2)])
    normed, grad_q, gk_early, gv_early, token = back(
        ends_half, (1, 2), me, q, k, v, grad_early, normed_early, e_early, (normed, grad_q)
    )
    filled = post(inner_half, (2, 1), me, k, v, gk_late, gv_late, token, (u1, w3b, w3a))
    grad_k, grad_v = post(ends_half, (1,), me, k, v, gk_early, gv_early, token, (u12, w4), filled)
    return tuple(x.reshape(out_shape) for x in (normed, grad_q, grad_k, grad_v))


def scan_states(first, second, count, backward):
    rows = first.shape[0] * 2
    shares = jnp.concatenate([first, second], axis=0).reshape(count, rows // count, DH)
    shares = lax.all_to_all(shares, "ctx", split_axis=0, concat_axis=0, tiled=True).astype(F32)
    running = jnp.cumsum(shares, axis=0)
    sums = running[-1:] - running if backward else running - shares
    sums = lax.all_to_all(sums.astype(BF16), "ctx", split_axis=0, concat_axis=0, tiled=True)
    sums = sums.reshape(rows, DH)
    return sums[: rows // 2], sums[rows // 2 :]


def low_half(me):
    return 0


def high_half(me):
    return 1


def shards_any(count, queries, key_vectors, value_vectors, grad_output):
    out_shape = queries.shape
    q, k, v, g = (rows_of(x) for x in (queries, key_vectors, value_vectors, grad_output))
    me = lax.axis_index("ctx").astype(jnp.int32).reshape(1)
    s1, k, v = load_states(low_half, me, k, v)
    e1, e2 = scan_states(s1, states(high_half, me, k, v), count, False)
    intra_out, qt, token = intra(q, k, v)
    normed1, grad1, g1, token = mid(low_half, (), me, q, qt, g, intra_out, token, (e1,))
    normed2, grad2, g2, token = mid(high_half, (), me, q, qt, g, intra_out, token, (e2,))
    l1, l2 = scan_states(g1, g2, count, True)
    normed, grad_q, gk1, gv1, token = back(low_half, (), me, q, k, v, grad1, normed1, (e1,))
    normed, grad_q, gk2, gv2, token = back(high_half, (), me, q, k, v, grad2, normed2, (e2,), (normed, grad_q))
    filled = post(low_half, (), me, k, v, gk1, gv1, token, (l1,))
    grad_k, grad_v = post(high_half, (), me, k, v, gk2, gv2, token, (l2,), filled)
    return tuple(x.reshape(out_shape) for x in (normed, grad_q, grad_k, grad_v))


def solution(mesh):
    placed = P(("groups", "dp"), "ctx", "tp")
    count = mesh.shape["ctx"]

    def shards(*args):
        if count == 4:
            return shards_four(*args)
        return shards_any(count, *args)

    return jax.shard_map(
        shards,
        mesh=mesh,
        in_specs=(placed,) * 4,
        out_specs=(placed,) * 4,
        check_vma=False,
    )
```

time: 101 us -> 44.3 us (0.44)
  local copies, waits for them, and re-layouts: 21 us -> 0.01 us
  other arithmetic: 19.9 us -> 0 us
  matrix products: 14.8 us -> 0 us
  Pallas kernels: 0 us -> 14.4 us
  waiting for transfers between devices: 25.7 us -> 14.9 us
  starting transfers between devices: 18.1 us -> 13.8 us
    all_to_all x4 -> x0, waiting for transfers between devices: 25.7 us -> none  [the longest x1 12.3 us: shards(): lax.all_to_all(local_state.reshape(1, -1), 'ctx', split_axis=1, concat_ax...]
    all_to_all x4 -> x0, starting transfers between devices: 18.1 us -> none  [the longest x1 6.32 us: shards(): lax.all_to_all(local_state.reshape(1, -1), 'ctx', split_axis=1, concat_ax...]
    ppermute x0 -> x10, waiting for transfers between devices: none -> 14.9 us  [send(): return lax.ppermute(x, 'ctx', pairs)]
    dot_general x12 -> x0, matrix products: 14.8 us -> none  [the longest x1 3.44 us: shards(): jnp.einsum('hts,thd->shd', grad_scores, query_rows, preferred_element_typ...]
    pallas_call x0 -> x13, Pallas kernels: none -> 14.4 us  [the longest x2 4.93 us: back(): pl.pallas_call(functools.partial(back_kernel, half_of, turns), out_shape=...]
    ppermute x0 -> x10, starting transfers between devices: none -> 13.8 us  [send(): return lax.ppermute(x, 'ctx', pairs)]
    unnamed x32 -> x4, local copies, waits for them, and re-layouts: 10.7 us -> 0.01 us
    another operation x4 -> x0, other arithmetic: 8.99 us -> none  [the longest x2 6.27 us: shards(): jnp.cumsum(grad_shares, axis=0)]
  transfers between devices with their start and end apart: 4 -> 10, of which waited for: 3 -> 3; matrix products, arithmetic and copies ran while one was open for 15% -> 0% of each run, Pallas kernels for 0% -> 25%
where the time goes in v2:
time: 44.3 us; the launch traced here: 44 us
  waiting for transfers between devices  14.9 us (34%)
  Pallas kernels  14.4 us (33%)
  starting transfers between devices  13.8 us (31%)
  between operations  0.88 us (2%)
    ppermute x10, waiting for transfers between devices, send(): return lax.ppermute(x, 'ctx', pairs)  14.9 us
    ppermute x10, starting transfers between devices, send(): return lax.ppermute(x, 'ctx', pairs)  13.8 us
    pallas_call x2, Pallas kernels, back(): pl.pallas_call(functools.partial(back_kernel, half_of, turns), out_shape=...  4.93 us
    pallas_call x2, Pallas kernels, mid(): pl.pallas_call(functools.partial(mid_kernel, half_of, turns), out_shape=(...  2.8 us
    pallas_call x2, Pallas kernels, post(): pl.pallas_call(functools.partial(post_kernel, half_of, turns), out_shape=...  2.27 us
    pallas_call x1, Pallas kernels, load_states(): pl.pallas_call(functools.partial(load_kernel, half_of), out_shape=(jax.Sh...  2.06 us
    pallas_call x1, Pallas kernels, intra(): pl.pallas_call(intra_kernel, out_shape=(jax.ShapeDtypeStruct(q.shape, F32...  1.68 us
  transfers between devices with their start and end apart: 10, of which 3 were waited for; matrix products, arithmetic and copies ran while one was open for 0% of the time, Pallas kernels for 25%

profile of v2, /device:TPU:0, one launch (start us, length us, event | category | flops | bytes accessed | tf_op | source)
XLA Modules:
  0.0 44.0 jit_solution(1275612407721334881)
XLA Ops:
  0.6 2.1 %load_states.1 = (bf16[512,128]{1,0:T(8,128)(2,1)S(1)}, bf16[320,1024]{1,0:T(8,128)(2,1)S(1)}, bf16[320,1024]{1,0:T(8,128)(2,1)S(1)}) custom-call(s32[1]{0:T(128)} %bitcast.me_ref, bf16[320,1024]{1,0:T(8,128)(2,1)} %bitcast.20, bf16[320,1024]{1,0:T(8,128)(2,1)} %bitcast.21), custom_call_target="tpu_custom_call" | custom-call | flops 41943040 | bytes 2621440 | tf_op jit(solution)/shard_map/load_states/pallas_call | solution.py:76
  2.7 4.9 %collective-permute-start = (bf16[512,128]{1,0:T(8,128)(2,1)S(1)}, bf16[512,128]{1,0:T(8,128)(2,1)S(1)}, u32[]{:S(2)}, u32[]{:S(2)}) collective-permute-start(bf16[512,128]{1,0:T(8,128)(2,1)S(1)} %get-tuple-element.42.a_ref), channel_id=1, source_target_pairs={{0,4},{4,8},{1,5},{5,9},{2,6},{6,10},{3,7},{7,11},{16,20},{20,24},... | collective-permute-start | bytes 393224 | tf_op jit(solution)/shard_map/ppermute | solution.py:323
  7.7 0.4 states.1.b_ref
  8.0 2.3 %collective-permute-start.2 = (bf16[512,128]{1,0:T(8,128)(2,1)S(1)}, bf16[512,128]{1,0:T(8,128)(2,1)S(1)}, u32[]{:S(2)}, u32[]{:S(2)}) collective-permute-start(bf16[512,128]{1,0:T(8,128)(2,1)S(1)} %states.1.b_ref), channel_id=1, source_target_pairs={{0,8},{8,4},{1,9},{9,5},{2,10},{10,6},{3,11},{11,7},{16,24},{24,20... | collective-permute-start | bytes 393224 | tf_op jit(solution)/shard_map/ppermute | solution.py:323
  10.4 1.7 %intra.1 = (f32[320,1024]{1,0:T(8,128)S(1)}, bf16[1024,320]{1,0:T(8,128)(2,1)S(1)}, f32[8,128]{1,0:T(8,128)S(1)}) custom-call(bf16[320,1024]{1,0:T(8,128)(2,1)S(1)} %bitcast.9, bf16[320,1024]{1,0:T(8,128)(2,1)S(1)} %get-tuple-element.37.k_ref, bf16[320,1024]{1,0:T(8,128)(2,1)S(1)} %get-tuple-element.38.v_ref), custom_call_target="tpu_custom_call" | custom-call | flops 419430400 | bytes 3932160 | tf_op jit(solution)/shard_map/intra/pallas_call | solution.py:124
  12.1 0.7 %collective-permute-start.1 = (bf16[512,128]{1,0:T(8,128)(2,1)S(1)}, bf16[512,128]{1,0:T(8,128)(2,1)S(1)}, u32[]{:S(2)}, u32[]{:S(2)}) collective-permute-start(bf16[512,128]{1,0:T(8,128)(2,1)S(1)} %add.2), channel_id=1, source_target_pairs={{4,8},{5,9},{6,10},{7,11},{20,24},{21,25},{22,26},{23,27}} | collective-permute-start | bytes 393224 | tf_op jit(solution)/shard_map/ppermute | solution.py:323
  12.8 0.5 %collective-permute-done.2.r2_ref = bf16[512,128]{1,0:T(8,128)(2,1)S(1)} collective-permute-done((bf16[512,128]{1,0:T(8,128)(2,1)S(1)}, bf16[512,128]{1,0:T(8,128)(2,1)S(1)}, u32[]{:S(2)}, u32[]{:S(2)}) %collective-permute-start.2) | collective-permute-done | bytes 131104 | tf_op jit(solution)/shard_map/ppermute | solution.py:323
  13.2 0.1 combine.2
  13.4 0.7 %collective-permute-start.3 = (bf16[512,128]{1,0:T(8,128)(2,1)S(1)}, bf16[512,128]{1,0:T(8,128)(2,1)S(1)}, u32[]{:S(2)}, u32[]{:S(2)}) collective-permute-start(bf16[512,128]{1,0:T(8,128)(2,1)S(1)} %get-tuple-element.43), channel_id=1, source_target_pairs={{8,12},{9,13},{10,14},{11,15},{24,28},{25,29},{26,30},{27,31}} | collective-permute-start | bytes 393224 | tf_op jit(solution)/shard_map/ppermute | solution.py:323
  14.0 0.7 %collective-permute-start.4 = (bf16[512,128]{1,0:T(8,128)(2,1)S(1)}, bf16[512,128]{1,0:T(8,128)(2,1)S(1)}, u32[]{:S(2)}, u32[]{:S(2)}) collective-permute-start(bf16[512,128]{1,0:T(8,128)(2,1)S(1)} %get-tuple-element.48), channel_id=1, source_target_pairs={{4,12},{8,4},{5,13},{9,5},{6,14},{10,6},{7,15},{11,7},{20,28},{24,... | collective-permute-start | bytes 393224 | tf_op jit(solution)/shard_map/ppermute | solution.py:323
  14.7 1.2 %mid.2 = (bf16[320,512]{1,0:T(8,128)(2,1)S(1)}, bf16[320,512]{1,0:T(8,128)(2,1)S(1)}, bf16[512,128]{1,0:T(8,128)(2,1)S(1)}, f32[8,128]{1,0:T(8,128)S(1)}) custom-call(s32[1]{0:T(128)} %bitcast.me_ref, bf16[320,1024]{1,0:T(8,128)(2,1)S(1)} %bitcast.10, bf16[1024,320]{1,0:T(8,128)(2,1)S(1)} %get-tuple-element.39.qt_ref, bf16[320,1024]{1,0:T(8,128)(2,1)S(1)} %bitcast.14, ...), custom_call_target="tpu_custom_call" | custom-call | flops 83886080 | bytes 1966080 | tf_op jit(solution)/shard_map/mid/pallas_call | solution.py:201
  15.9 0.7 %collective-permute-start.5 = (bf16[512,128]{1,0:T(8,128)(2,1)S(1)}, bf16[512,128]{1,0:T(8,128)(2,1)S(1)}, u32[]{:S(2)}, u32[]{:S(2)}) collective-permute-start(bf16[512,128]{1,0:T(8,128)(2,1)S(1)} %get-tuple-element.58.a_ref), channel_id=1, source_target_pairs={{12,8},{8,4},{13,9},{9,5},{14,10},{10,6},{15,11},{11,7},{28,24},{2... | collective-permute-start | bytes 393224 | tf_op jit(solution)/shard_map/ppermute | solution.py:323
  16.6 1.6 %mid.3 = (bf16[320,512]{1,0:T(8,128)(2,1)S(1)}, bf16[320,512]{1,0:T(8,128)(2,1)S(1)}, bf16[512,128]{1,0:T(8,128)(2,1)S(1)}, f32[8,128]{1,0:T(8,128)}) custom-call(s32[1]{0:T(128)} %bitcast.me_ref, bf16[320,1024]{1,0:T(8,128)(2,1)S(1)} %bitcast.11, bf16[1024,320]{1,0:T(8,128)(2,1)S(1)} %get-tuple-element.39.qt_ref, bf16[320,1024]{1,0:T(8,128)(2,1)S(1)} %bitcast.15, ...), custom_call_target="tpu_custom_call" | custom-call | flops 83886080 | bytes 1966080 | tf_op jit(solution)/shard_map/mid/pallas_call | solution.py:201
  18.2 0.7 %collective-permute-start.6 = (bf16[512,128]{1,0:T(8,128)(2,1)S(1)}, bf16[512,128]{1,0:T(8,128)(2,1)S(1)}, u32[]{:S(2)}, u32[]{:S(2)}) collective-permute-start(bf16[512,128]{1,0:T(8,128)(2,1)S(1)} %get-tuple-element.59.b_ref), channel_id=1, source_target_pairs={{12,4},{4,8},{13,5},{5,9},{14,6},{6,10},{15,7},{7,11},{28,20},{20,... | collective-permute-start | bytes 393224 | tf_op jit(solution)/shard_map/ppermute | solution.py:323
  18.9 2.5 %back.2 = (bf16[320,1024]{1,0:T(8,128)(2,1)}, bf16[320,1024]{1,0:T(8,128)(2,1)}, f32[320,512]{1,0:T(8,128)S(1)}, f32[320,512]{1,0:T(8,128)S(1)}, f32[8,128]{1,0:T(8,128)S(1)}) custom-call(s32[1]{0:T(128)} %bitcast.me_ref, bf16[320,1024]{1,0:T(8,128)(2,1)S(1)} %bitcast.12, bf16[320,1024]{1,0:T(8,128)(2,1)S(1)} %get-tuple-element.37.k_ref, ...), custom_call_target="tpu_custom_call" | custom-call | flops 629145600 | bytes 2949120 | tf_op jit(solution)/shard_map/back/pallas_call | solution.py:249
  21.4 0.7 %collective-permute-start.8 = (bf16[512,128]{1,0:T(8,128)(2,1)S(1)}, bf16[512,128]{1,0:T(8,128)(2,1)S(1)}, u32[]{:S(2)}, u32[]{:S(2)}) collective-permute-start(bf16[512,128]{1,0:T(8,128)(2,1)S(1)} %add.3), channel_id=1, source_target_pairs={{8,4},{9,5},{10,6},{11,7},{24,20},{25,21},{26,22},{27,23}} | collective-permute-start | bytes 393224 | tf_op jit(solution)/shard_map/ppermute | solution.py:323
  22.1 0.1 combine.3
  22.2 1.3 %collective-permute-start.9 = (bf16[512,128]{1,0:T(8,128)(2,1)S(1)}, bf16[512,128]{1,0:T(8,128)(2,1)S(1)}, u32[]{:S(2)}, u32[]{:S(2)}) collective-permute-start(bf16[512,128]{1,0:T(8,128)(2,1)S(1)} %get-tuple-element.65), channel_id=1, source_target_pairs={{4,0},{5,1},{6,2},{7,3},{20,16},{21,17},{22,18},{23,19}} | collective-permute-start | bytes 393224 | tf_op jit(solution)/shard_map/ppermute | solution.py:323
  23.5 1.3 %collective-permute-start.7 = (bf16[512,128]{1,0:T(8,128)(2,1)S(1)}, bf16[512,128]{1,0:T(8,128)(2,1)S(1)}, u32[]{:S(2)}, u32[]{:S(2)}) collective-permute-start(bf16[512,128]{1,0:T(8,128)(2,1)S(1)} %get-tuple-element.62), channel_id=1, source_target_pairs={{8,0},{4,8},{9,1},{5,9},{10,2},{6,10},{11,3},{7,11},{24,16},{20,24... | collective-permute-start | bytes 393224 | tf_op jit(solution)/shard_map/ppermute | solution.py:323
  24.8 2.5 %back.3 = (bf16[320,1024]{1,0:T(8,128)(2,1)}, bf16[320,1024]{1,0:T(8,128)(2,1)}, f32[320,512]{1,0:T(8,128)S(1)}, f32[320,512]{1,0:T(8,128)S(1)}, f32[8,128]{1,0:T(8,128)S(1)}) custom-call(s32[1]{0:T(128)} %bitcast.me_ref, bf16[320,1024]{1,0:T(8,128)(2,1)S(1)} %bitcast.13, ...), custom_call_target="tpu_custom_call", output_to_operand_aliasing={{0}: (9, {}), {1}: (10, {})} | custom-call | flops 629145600 | bytes 2949120 | tf_op jit(solution)/shard_map/back/pallas_call | solution.py:249
  27.3 13.9 %collective-permute-done.9.refs_2_ = bf16[512,128]{1,0:T(8,128)(2,1)S(1)} collective-permute-done((bf16[512,128]{1,0:T(8,128)(2,1)S(1)}, bf16[512,128]{1,0:T(8,128)(2,1)S(1)}, u32[]{:S(2)}, u32[]{:S(2)}) %collective-permute-start.9) | collective-permute-done | bytes 131104 | tf_op jit(solution)/shard_map/ppermute | solution.py:323
  41.3 1.1 %post.2 = (bf16[320,1024]{1,0:T(8,128)(2,1)}, bf16[320,1024]{1,0:T(8,128)(2,1)}) custom-call(s32[1]{0:T(128)} %bitcast.me_ref, bf16[320,1024]{1,0:T(8,128)(2,1)S(1)} %get-tuple-element.37.k_ref, bf16[320,1024]{1,0:T(8,128)(2,1)S(1)} %get-tuple-element.38.v_ref, f32[320,512]{1,0:T(8,128)S(1)} %get-tuple-element.63.gk_in_ref, ...), custom_call_target="tpu_custom_call" | custom-call | flops 83886080 | bytes 2621440 | tf_op jit(solution)/shard_map/post/pallas_call | solution.py:284
  42.4 0.4 collective-permute-done.7.refs_1_
  42.8 1.1 %post.3 = (bf16[320,1024]{1,0:T(8,128)(2,1)}, bf16[320,1024]{1,0:T(8,128)(2,1)}) custom-call(s32[1]{0:T(128)} %bitcast.me_ref, bf16[320,1024]{1,0:T(8,128)(2,1)S(1)} %get-tuple-element.37.k_ref, bf16[320,1024]{1,0:T(8,128)(2,1)S(1)} %get-tuple-element.38.v_ref, ...), custom_call_target="tpu_custom_call", output_to_operand_aliasing={{0}: (8, {}), {1}: (9, {})} | custom-call | flops 83886080 | bytes 2621440 | tf_op jit(solution)/shard_map/post/pallas_call | solution.py:284
  (13 shorter events, 0.1 us)
Async XLA Ops:
  0.6 9.7 %copy-start = (bf16[1,320,1024]{2,1,0:T(8,128)(2,1)S(1)}, bf16[1,320,1024]{2,1,0:T(8,128)(2,1)}, u32[]{:S(2)}) copy-start(bf16[1,320,1024]{2,1,0:T(8,128)(2,1)} %param.4) | copy-start | bytes 1966084
  2.7 9.3 %collective-permute-start = (bf16[512,128]{1,0:T(8,128)(2,1)S(1)}, bf16[512,128]{1,0:T(8,128)(2,1)S(1)}, u32[]{:S(2)}, u32[]{:S(2)}) collective-permute-start(bf16[512,128]{1,0:T(8,128)(2,1)S(1)} %get-tuple-element.42.a_ref), channel_id=1, source_target_pairs={{0,4},{4,8},{1,5},{5,9},{2,6},{6,10},{3,7},{7,11},{16,20},{20,24},... | collective-permute-start | bytes 393224 | tf_op jit(solution)/shard_map/ppermute | solution.py:323
  8.0 5.2 %collective-permute-start.2 = (bf16[512,128]{1,0:T(8,128)(2,1)S(1)}, bf16[512,128]{1,0:T(8,128)(2,1)S(1)}, u32[]{:S(2)}, u32[]{:S(2)}) collective-permute-start(bf16[512,128]{1,0:T(8,128)(2,1)S(1)} %states.1.b_ref), channel_id=1, source_target_pairs={{0,8},{8,4},{1,9},{9,5},{2,10},{10,6},{3,11},{11,7},{16,24},{24,20... | collective-permute-start | bytes 393224 | tf_op jit(solution)/shard_map/ppermute | solution.py:323
  10.3 4.4 %copy-start.1 = (bf16[1,320,1024]{2,1,0:T(8,128)(2,1)S(1)}, bf16[1,320,1024]{2,1,0:T(8,128)(2,1)}, u32[]{:S(2)}) copy-start(bf16[1,320,1024]{2,1,0:T(8,128)(2,1)} %param.7) | copy-start | bytes 1966084
  12.1 2.6 %collective-permute-start.1 = (bf16[512,128]{1,0:T(8,128)(2,1)S(1)}, bf16[512,128]{1,0:T(8,128)(2,1)S(1)}, u32[]{:S(2)}, u32[]{:S(2)}) collective-permute-start(bf16[512,128]{1,0:T(8,128)(2,1)S(1)} %add.2), channel_id=1, source_target_pairs={{4,8},{5,9},{6,10},{7,11},{20,24},{21,25},{22,26},{23,27}} | collective-permute-start | bytes 393224 | tf_op jit(solution)/shard_map/ppermute | solution.py:323
  13.4 1.4 %collective-permute-start.3 = (bf16[512,128]{1,0:T(8,128)(2,1)S(1)}, bf16[512,128]{1,0:T(8,128)(2,1)S(1)}, u32[]{:S(2)}, u32[]{:S(2)}) collective-permute-start(bf16[512,128]{1,0:T(8,128)(2,1)S(1)} %get-tuple-element.43), channel_id=1, source_target_pairs={{8,12},{9,13},{10,14},{11,15},{24,28},{25,29},{26,30},{27,31}} | collective-permute-start | bytes 393224 | tf_op jit(solution)/shard_map/ppermute | solution.py:323
  14.0 2.6 %collective-permute-start.4 = (bf16[512,128]{1,0:T(8,128)(2,1)S(1)}, bf16[512,128]{1,0:T(8,128)(2,1)S(1)}, u32[]{:S(2)}, u32[]{:S(2)}) collective-permute-start(bf16[512,128]{1,0:T(8,128)(2,1)S(1)} %get-tuple-element.48), channel_id=1, source_target_pairs={{4,12},{8,4},{5,13},{9,5},{6,14},{10,6},{7,15},{11,7},{20,28},{24,... | collective-permute-start | bytes 393224 | tf_op jit(solution)/shard_map/ppermute | solution.py:323
  15.9 5.4 %collective-permute-start.5 = (bf16[512,128]{1,0:T(8,128)(2,1)S(1)}, bf16[512,128]{1,0:T(8,128)(2,1)S(1)}, u32[]{:S(2)}, u32[]{:S(2)}) collective-permute-start(bf16[512,128]{1,0:T(8,128)(2,1)S(1)} %get-tuple-element.58.a_ref), channel_id=1, source_target_pairs={{12,8},{8,4},{13,9},{9,5},{14,10},{10,6},{15,11},{11,7},{28,24},{2... | collective-permute-start | bytes 393224 | tf_op jit(solution)/shard_map/ppermute | solution.py:323
  18.2 3.9 %collective-permute-start.6 = (bf16[512,128]{1,0:T(8,128)(2,1)S(1)}, bf16[512,128]{1,0:T(8,128)(2,1)S(1)}, u32[]{:S(2)}, u32[]{:S(2)}) collective-permute-start(bf16[512,128]{1,0:T(8,128)(2,1)S(1)} %get-tuple-element.59.b_ref), channel_id=1, source_target_pairs={{12,4},{4,8},{13,5},{5,9},{14,6},{6,10},{15,7},{7,11},{28,20},{20,... | collective-permute-start | bytes 393224 | tf_op jit(solution)/shard_map/ppermute | solution.py:323
  21.4 5.9 %collective-permute-start.8 = (bf16[512,128]{1,0:T(8,128)(2,1)S(1)}, bf16[512,128]{1,0:T(8,128)(2,1)S(1)}, u32[]{:S(2)}, u32[]{:S(2)}) collective-permute-start(bf16[512,128]{1,0:T(8,128)(2,1)S(1)} %add.3), channel_id=1, source_target_pairs={{8,4},{9,5},{10,6},{11,7},{24,20},{25,21},{26,22},{27,23}} | collective-permute-start | bytes 393224 | tf_op jit(solution)/shard_map/ppermute | solution.py:323
  22.2 19.0 %collective-permute-start.9 = (bf16[512,128]{1,0:T(8,128)(2,1)S(1)}, bf16[512,128]{1,0:T(8,128)(2,1)S(1)}, u32[]{:S(2)}, u32[]{:S(2)}) collective-permute-start(bf16[512,128]{1,0:T(8,128)(2,1)S(1)} %get-tuple-element.65), channel_id=1, source_target_pairs={{4,0},{5,1},{6,2},{7,3},{20,16},{21,17},{22,18},{23,19}} | collective-permute-start | bytes 393224 | tf_op jit(solution)/shard_map/ppermute | solution.py:323
  23.5 19.3 %collective-permute-start.7 = (bf16[512,128]{1,0:T(8,128)(2,1)S(1)}, bf16[512,128]{1,0:T(8,128)(2,1)S(1)}, u32[]{:S(2)}, u32[]{:S(2)}) collective-permute-start(bf16[512,128]{1,0:T(8,128)(2,1)S(1)} %get-tuple-element.62), channel_id=1, source_target_pairs={{8,0},{4,8},{9,1},{5,9},{10,2},{6,10},{11,3},{7,11},{24,16},{20,24... | collective-permute-start | bytes 393224 | tf_op jit(solution)/shard_map/ppermute | solution.py:323

commit v3 on v2

v3 whole, which is shorter than its diff:
```python
import functools

import jax
import jax.numpy as jnp
from jax import lax
from jax.experimental import pallas as pl
from jax.experimental.pallas import tpu as pltpu
from jax.sharding import PartitionSpec as P

DH = 128
norm_eps = 1e-06
F32 = jnp.float32
BF16 = jnp.bfloat16

VMEM_SPEC = pl.BlockSpec(memory_space=pltpu.VMEM)
HBM_SPEC = pl.BlockSpec(memory_space=pltpu.HBM)
SMEM_SPEC = pl.BlockSpec(memory_space=pltpu.SMEM)
COST = pl.CostEstimate(flops=0, transcendentals=0, bytes_accessed=4096)
PARAMS = pltpu.CompilerParams(vmem_limit_bytes=16 << 20)


def params(name, parts):
    return dict(compiler_params=PARAMS, cost_estimate=COST, name=name, out_shape=parts)


def dot_nn(a, b):
    return lax.dot_general(a, b, (((1,), (0,)), ((), ())), preferred_element_type=F32)


def dot_nt(a, b):
    return lax.dot_general(a, b, (((1,), (1,)), ((), ())), preferred_element_type=F32)


def dot_tn(a, b):
    return lax.dot_general(a, b, (((0,), (0,)), ((), ())), preferred_element_type=F32)


def head(index):
    return slice(index * DH, (index + 1) * DH)


def causal(length):
    rows = lax.broadcasted_iota(jnp.int32, (length, length), 0)
    columns = lax.broadcasted_iota(jnp.int32, (length, length), 1)
    return columns <= rows


def half_columns(half, h, heads):
    return pl.ds(pl.multiple_of((half * heads + h) * DH, DH), DH)


def among(me, roles):
    hit = me == roles[0]
    for role in roles[1:]:
        hit = hit | (me == role)
    return hit


def on(me, roles):
    return pl.when(among(me, roles)) if roles else lambda body: body()


def state_kernel(plan, duplicate, me_ref, k_ref, v_ref, token_ref, *refs):
    spare, outs = refs[: len(duplicate[:1])], refs[len(duplicate[:1]) : -5]
    done_ref, k_buf, v_buf, k_sem, v_sem = refs[-5:]
    heads = outs[0].shape[0] // DH
    done_ref[...] = token_ref[...]
    if duplicate:

        @on(me_ref[0], (duplicate[0],))
        def _():
            outs[duplicate[1]][...] = spare[0][...]

    for roles, pieces in plan:

        @on(me_ref[0], roles)
        def _():
            copies = []
            for half, out in pieces:
                for h in range(heads):
                    cols, slot = head(half * heads + h), len(copies)
                    pair = (
                        pltpu.make_async_copy(k_ref.at[:, cols], k_buf.at[slot], k_sem.at[slot]),
                        pltpu.make_async_copy(v_ref.at[:, cols], v_buf.at[slot], v_sem.at[slot]),
                    )
                    for copy in pair:
                        copy.start()
                    copies.append((outs[out], head(h), pair))
            for slot, (out_ref, rows, pair) in enumerate(copies):
                for copy in pair:
                    copy.wait()
                out_ref[rows, :] = dot_tn(k_buf[slot], v_buf[slot]).astype(BF16)


def states(plan, me, k, v, token, duplicate=(), spare=()):
    length, width = k.shape
    count = 1 + max(out for _, pieces in plan for _, out in pieces)
    slots = max(len(pieces) for _, pieces in plan) * width // (2 * DH)
    k, v = (pltpu.with_memory_space_constraint(x, pltpu.HBM) for x in (k, v))
    shape = jax.ShapeDtypeStruct((width // 2, DH), BF16)
    return pl.pallas_call(
        functools.partial(state_kernel, plan, duplicate),
        in_specs=[SMEM_SPEC, HBM_SPEC, HBM_SPEC] + [VMEM_SPEC] * (1 + len(spare)),
        out_specs=(VMEM_SPEC,) * (count + 1),
        scratch_shapes=[pltpu.VMEM((slots, length, DH), BF16)] * 2 + [pltpu.SemaphoreType.DMA((slots,))] * 2,
        **params("states", (shape,) * count + (TOKEN,)),
    )(me, k, v, token, *spare)


TOKEN = jax.ShapeDtypeStruct((8, DH), F32)


def intra_kernel(q_ref, k_ref, v_ref, token_ref, out_ref, qt_ref, done_ref):
    mask = causal(q_ref.shape[0])
    for h in range(q_ref.shape[1] // DH):
        q = q_ref[:, head(h)]
        scores = jnp.where(mask, dot_nt(q, k_ref[:, head(h)]), 0.0).astype(BF16)
        out_ref[:, head(h)] = dot_nn(scores, v_ref[:, head(h)])
        qt_ref[head(h), :] = q.T
    done_ref[...] = token_ref[...]


def intra(q, k, v, token):
    length, width = q.shape
    return pl.pallas_call(
        intra_kernel,
        in_specs=[VMEM_SPEC] * 4,
        out_specs=(VMEM_SPEC,) * 3,
        **params("intra", (jax.ShapeDtypeStruct(q.shape, F32), jax.ShapeDtypeStruct((width, length), BF16), TOKEN)),
    )(q, k, v, token)


def total(refs, rows=slice(None)):
    value = refs[0][rows, :].astype(F32)
    for ref in refs[1:]:
        value = value + ref[rows, :].astype(F32)
    return value.astype(BF16)


def add_kernel(token_ref, *refs):
    refs[-2][...] = total(refs[:-2])
    refs[-1][...] = token_ref[...]


def add(token, *arrays):
    return pl.pallas_call(
        add_kernel,
        in_specs=[VMEM_SPEC] * (1 + len(arrays)),
        out_specs=(VMEM_SPEC,) * 2,
        **params("add", (jax.ShapeDtypeStruct(arrays[0].shape, BF16), TOKEN)),
    )(token, *arrays)


def half_columns(half, h, heads):
    return pl.ds(pl.multiple_of((half * heads + h) * DH, DH), DH)


def mid_kernel(half_of, roles, keep, merge, me_ref, q_ref, qt_ref, g_ref, intra_ref, token_ref, *refs):
    normed_ref, grad_ref, earlier_ref, done_ref, *state_refs = refs[-5 - merge :]
    other, e_refs = refs[: len(keep) + merge], refs[len(keep) + merge : -5 - merge]
    state_ref = state_refs[0]
    heads = state_ref.shape[0] // DH
    done_ref[...] = token_ref[...]
    if keep:

        @on(me_ref[0], keep)
        def _():
            state_ref[...] = other[0][...]

    if merge:

        @pl.when(jnp.logical_not(among(me_ref[0], roles)))
        def _():
            state_refs[1][...] = other[-1][...]

    @on(me_ref[0], roles)
    def _():
        half = half_of(me_ref[0])
        for h in range(heads):
            cols = half_columns(half, h, heads)
            earlier = total(e_refs, head(h))
            earlier_ref[head(h), :] = earlier
            mixed = intra_ref[:, cols] + dot_nn(q_ref[:, cols], earlier)
            g = g_ref[:, cols].astype(F32)
            inverse = lax.rsqrt(jnp.mean(mixed * mixed, axis=-1, keepdims=True) + norm_eps)
            along = jnp.mean(g * mixed, axis=-1, keepdims=True) * inverse
            normed = mixed * inverse
            grad = (inverse * (g - normed * along)).astype(BF16)
            grad_ref[:, head(h)] = grad
            for ref in state_refs:
                ref[head(h), :] = dot_nn(qt_ref[cols, :], grad).astype(BF16)
            normed_ref[:, head(h)] = normed.astype(BF16)


def mid(half_of, roles, me, shared, token, earlier, keep=(), other=()):
    merge = len(other) - len(keep)
    length, width = shared[0].shape
    half_shape = jax.ShapeDtypeStruct((length, width // 2), BF16)
    state_shape = jax.ShapeDtypeStruct(earlier[0].shape, BF16)
    normed, grad, low, token, *states_out = pl.pallas_call(
        functools.partial(mid_kernel, half_of, roles, keep, merge),
        in_specs=[SMEM_SPEC] + [VMEM_SPEC] * (5 + len(other) + len(earlier)),
        out_specs=(VMEM_SPEC,) * (5 + merge),
        **params("mid", (half_shape, half_shape, state_shape, TOKEN) + (state_shape,) * (1 + merge)),
    )(me, *shared, token, *other, *earlier)
    return (normed, grad, low), *states_out, token


def back_kernel(half_of, roles, sets, me_ref, q_ref, k_ref, v_ref, token_ref, *refs):
    normed_ref, gq_ref, gk_ref, gv_ref, done_ref, gq_buf, n_buf, gq_sem, n_sem = refs[-9:]
    length = q_ref.shape[0]
    rows = lax.broadcasted_iota(jnp.int32, (length, length), 0)
    columns = lax.broadcasted_iota(jnp.int32, (length, length), 1)
    mask, mask_t = columns <= rows, rows <= columns
    heads = gk_ref.shape[1] // DH
    half = half_of(me_ref[0])

    def chosen(index, place):
        value = refs[index][place]
        if sets > 1:
            value = jnp.where(among(me_ref[0], roles), refs[3 + index][place], value)
        return value

    copies = []
    for h in range(heads):
        cols = half_columns(half, h, heads)
        n_buf[h] = chosen(0, (slice(None), head(h)))
        copies.append(pltpu.make_async_copy(n_buf.at[h], normed_ref.at[:, cols], n_sem.at[h]))
        copies[-1].start()
        q, k, v = (ref[:, cols] for ref in (q_ref, k_ref, v_ref))
        grad = chosen(1, (slice(None), head(h)))
        earlier = chosen(2, (head(h), slice(None)))
        scores_t = jnp.where(mask_t, dot_nt(k, q), 0.0).astype(BF16)
        grad_scores = jnp.where(mask, dot_nt(grad, v), 0.0).astype(BF16)
        grad_scores_t = jnp.where(mask_t, dot_nt(v, grad), 0.0).astype(BF16)
        gq_buf[h] = (dot_nn(grad_scores, k) + dot_nt(grad, earlier)).astype(BF16)
        copies.append(pltpu.make_async_copy(gq_buf.at[h], gq_ref.at[:, cols], gq_sem.at[h]))
        copies[-1].start()
        gk_ref[:, head(h)] = dot_nn(grad_scores_t, q)
        gv_ref[:, head(h)] = dot_nn(scores_t, grad)
    done_ref[...] = token_ref[...]
    for copy in copies:
        copy.wait()


def back(half_of, roles, me, q, k, v, token, sets, filled=()):
    length, width = q.shape
    heads = width // (2 * DH)
    whole = jax.ShapeDtypeStruct(q.shape, BF16)
    half_shape = jax.ShapeDtypeStruct((length, width // 2), F32)
    first = 5 + 3 * len(sets)
    buffers = pltpu.VMEM((heads, length, DH), BF16)
    return pl.pallas_call(
        functools.partial(back_kernel, half_of, roles, len(sets)),
        in_specs=[SMEM_SPEC] + [VMEM_SPEC] * (first - 1) + [HBM_SPEC] * len(filled),
        out_specs=(HBM_SPEC, HBM_SPEC, VMEM_SPEC, VMEM_SPEC, VMEM_SPEC),
        scratch_shapes=[buffers, buffers] + [pltpu.SemaphoreType.DMA((heads,))] * 2,
        input_output_aliases={first: 0, first + 1: 1} if filled else {},
        **params("back", (whole, whole, half_shape, half_shape, TOKEN)),
    )(me, q, k, v, token, *(x for one in sets for x in one), *filled)


def post_kernel(half_of, parts, me_ref, k_ref, v_ref, gk_in_ref, gv_in_ref, token_ref, *refs):
    l_refs, (gk_ref, gv_ref, done_ref, gk_buf, gv_buf, gk_sem, gv_sem) = refs[:parts], refs[-7:]
    done_ref[...] = token_ref[...]
    heads = gk_in_ref.shape[1] // DH
    half = half_of(me_ref[0])
    copies = []
    for h in range(heads):
        cols = half_columns(half, h, heads)
        later = total(l_refs, head(h))
        gk_buf[h] = (gk_in_ref[:, head(h)] + dot_nt(v_ref[:, cols], later)).astype(BF16)
        copies.append(pltpu.make_async_copy(gk_buf.at[h], gk_ref.at[:, cols], gk_sem.at[h]))
        copies[-1].start()
        gv_buf[h] = (gv_in_ref[:, head(h)] + dot_nn(k_ref[:, cols], later)).astype(BF16)
        copies.append(pltpu.make_async_copy(gv_buf.at[h], gv_ref.at[:, cols], gv_sem.at[h]))
        copies[-1].start()
    for copy in copies:
        copy.wait()


def post(half_of, me, k, v, gk_in, gv_in, token, later, filled=()):
    length, width = k.shape
    heads = width // (2 * DH)
    first = 6 + len(later)
    return pl.pallas_call(
        functools.partial(post_kernel, half_of, len(later)),
        in_specs=[SMEM_SPEC] + [VMEM_SPEC] * (first - 1) + [HBM_SPEC] * len(filled),
        out_specs=(HBM_SPEC, HBM_SPEC, VMEM_SPEC),
        scratch_shapes=[pltpu.VMEM((heads, length, DH), BF16)] * 2 + [pltpu.SemaphoreType.DMA((heads,))] * 2,
        input_output_aliases={first: 0, first + 1: 1} if filled else {},
        **params("post", (jax.ShapeDtypeStruct(k.shape, BF16), jax.ShapeDtypeStruct(k.shape, BF16), TOKEN)),
    )(me, k, v, gk_in, gv_in, token, *later, *filled)


def even_half(me):
    return 1 - lax.rem(me, 2)


def odd_half(me):
    return lax.rem(me, 2)


def rows_of(array):
    return array.reshape(array.shape[1:])


def shards_four(queries, key_vectors, value_vectors, grad_output):
    out_shape = queries.shape
    q, k, v, g = (rows_of(x) for x in (queries, key_vectors, value_vectors, grad_output))
    me = lax.axis_index("ctx").astype(jnp.int32).reshape(1)
    token = jnp.zeros(TOKEN.shape, TOKEN.dtype)

    def send(x, pairs):
        return lax.ppermute(x, "ctx", pairs)

    s_a, token = states((((0,), ((0, 0),)),), me, k, v, token)
    r_a = send(s_a, [(0, 1)])
    s_x, s_b, token = states((((0,), ((1, 0),)), ((1,), ((1, 1), (0, 0)))), me, k, v, token)
    r_b = send(s_b, [(1, 2)])
    s_c, s_y, token = states((((2,), ((0, 0), (1, 1))),), me, k, v, token, (0, 0), (s_x,))
    r_c = send(s_c, [(0, 2), (2, 3)])
    intra_out, qt, token = intra(q, k, v, token)
    shared = (q, qt, g, intra_out)
    s12, token = add(token, r_a, s_x)
    r_far = send(s12, [(1, 3)])
    r_near = send(s12, [(0, 1), (1, 2)])
    s123, token = add(token, r_b, r_c, s_y)
    first, g_first, token = mid(even_half, (0, 1, 2), me, shared, token, (r_a, r_b, r_c))
    r_last = send(s123, [(2, 3)])
    first_end, g_one, token = mid(even_half, (3,), me, shared, token, (r_c, r_far), (2,), (g_first,))
    u_one = send(g_one, [(3, 2), (2, 1)])
    second, g_rest, token = mid(odd_half, (0, 1, 2), me, shared, token, (r_near,))
    second_end, g_two, g_second, token = mid(odd_half, (3,), me, shared, token, (r_last,), (1,), (g_first, g_rest))
    u_two = send(g_two, [(3, 1), (1, 0)])
    normed, grad_q, gk_second, gv_second, token = back(odd_half, (3,), me, q, k, v, token, (second, second_end))
    g12, token = add(token, u_one, g_second)
    w_far = send(g12, [(2, 0)])
    w_near = send(g12, [(3, 2), (2, 1)])
    g123, token = add(token, u_one, u_two, g_second)
    w_last = send(g123, [(1, 0)])
    normed, grad_q, gk_first, gv_first, token = back(
        even_half, (3,), me, q, k, v, token, (first, first_end), (normed, grad_q)
    )
    *filled, token = post(odd_half, me, k, v, gk_second, gv_second, token, (u_one, u_two, w_far))
    l_near, token = add(token, w_near)
    grad_k, grad_v, token = post(even_half, me, k, v, gk_first, gv_first, token, (l_near, w_last), filled)
    return tuple(x.reshape(out_shape) for x in (normed, grad_q, grad_k, grad_v))


def scan_states(first, second, count, backward):
    rows = first.shape[0] * 2
    shares = jnp.concatenate([first, second], axis=0).reshape(count, rows // count, DH)
    shares = lax.all_to_all(shares, "ctx", split_axis=0, concat_axis=0, tiled=True).astype(F32)
    running = jnp.cumsum(shares, axis=0)
    sums = running[-1:] - running if backward else running - shares
    sums = lax.all_to_all(sums.astype(BF16), "ctx", split_axis=0, concat_axis=0, tiled=True)
    sums = sums.reshape(rows, DH)
    return sums[: rows // 2], sums[rows // 2 :]


def low_half(me):
    return 0


def high_half(me):
    return 1


def shards_any(count, queries, key_vectors, value_vectors, grad_output):
    out_shape = queries.shape
    q, k, v, g = (rows_of(x) for x in (queries, key_vectors, value_vectors, grad_output))
    me = lax.axis_index("ctx").astype(jnp.int32).reshape(1)
    token = jnp.zeros(TOKEN.shape, TOKEN.dtype)
    s1, s2, token = states((((), ((0, 0), (1, 1))),), me, k, v, token)
    e1, e2 = scan_states(s1, s2, count, False)
    intra_out, qt, token = intra(q, k, v, token)
    shared = (q, qt, g, intra_out)
    low, g1, token = mid(low_half, (), me, shared, token, (e1,))
    high, g2, token = mid(high_half, (), me, shared, token, (e2,))
    l1, l2 = scan_states(g1, g2, count, True)
    normed, grad_q, gk1, gv1, token = back(low_half, (), me, q, k, v, token, (low,))
    normed, grad_q, gk2, gv2, token = back(high_half, (), me, q, k, v, token, (high,), (normed, grad_q))
    *filled, token = post(low_half, me, k, v, gk1, gv1, token, (l1,))
    grad_k, grad_v, token = post(high_half, me, k, v, gk2, gv2, token, (l2,), filled)
    return tuple(x.reshape(out_shape) for x in (normed, grad_q, grad_k, grad_v))


def solution(mesh):
    placed = P(("groups", "dp"), "ctx", "tp")
    count = mesh.shape["ctx"]

    def shards(*args):
        if count == 4:
            return shards_four(*args)
        return shards_any(count, *args)

    return jax.shard_map(
        shards,
        mesh=mesh,
        in_specs=(placed,) * 4,
        out_specs=(placed,) * 4,
        check_vma=False,
    )
```

time: 44.3 us -> 38.5 us (0.87)
  waiting for transfers between devices: 14.9 us -> 5.66 us
  Pallas kernels: 14.4 us -> 16.3 us
  starting transfers between devices: 13.8 us -> 15 us
    ppermute x10 -> x11, waiting for transfers between devices: 14.9 us -> 5.66 us  [send(): return lax.ppermute(x, 'ctx', pairs)]
    pallas_call x13 -> x17, Pallas kernels: 14.4 us -> 16.3 us  [the longest x2 5.14 us: back(): pl.pallas_call(functools.partial(back_kernel, half_of, roles, len(sets)),...]
    ppermute x10 -> x11, starting transfers between devices: 13.8 us -> 15 us  [send(): return lax.ppermute(x, 'ctx', pairs)]
  transfers between devices with their start and end apart: 10 -> 11, of which waited for: 3 -> 4; matrix products, arithmetic and copies ran while one was open for 0% -> 0% of each run, Pallas kernels for 25% -> 33%
where the time goes in v3:
time: 38.5 us; the launch traced here: 38.2 us
  Pallas kernels  16.3 us (42%)
  starting transfers between devices  15 us (39%)
  waiting for transfers between devices  5.66 us (15%)
  between operations  1.12 us (3%)
    ppermute x11, starting transfers between devices, send(): return lax.ppermute(x, 'ctx', pairs)  15 us
    ppermute x11, waiting for transfers between devices, send(): return lax.ppermute(x, 'ctx', pairs)  5.66 us
    pallas_call x2, Pallas kernels, back(): pl.pallas_call(functools.partial(back_kernel, half_of, roles, len(sets)),...  5.14 us
    pallas_call x3, Pallas kernels, states(): pl.pallas_call(functools.partial(state_kernel, plan, duplicate), in_specs...  4.08 us
    pallas_call x2, Pallas kernels, post(): pl.pallas_call(functools.partial(post_kernel, half_of, len(later)), in_sp...  2.84 us
    pallas_call x4, Pallas kernels, mid(): pl.pallas_call(functools.partial(mid_kernel, half_of, roles, keep, merge)...  2.39 us
    pallas_call x1, Pallas kernels, intra(): pl.pallas_call(intra_kernel, in_specs=[VMEM_SPEC] * 4, out_specs=(VMEM_SP...  1.69 us
  transfers between devices with their start and end apart: 11, of which 4 were waited for; matrix products, arithmetic and copies ran while one was open for 0% of the time, Pallas kernels for 33%

profile of v3, /device:TPU:0, one launch (start us, length us, event | category | flops | bytes accessed | tf_op | source)
XLA Modules:
  0.0 38.2 jit_solution(12109451535176633806)
XLA Ops:
  0.6 1.9 %states.3 = (bf16[512,128]{1,0:T(8,128)(2,1)S(1)}, f32[8,128]{1,0:T(8,128)S(1)}) custom-call(s32[1]{0:T(128)} %bitcast.me_ref, bf16[320,1024]{1,0:T(8,128)(2,1)} %bitcast.9, bf16[320,1024]{1,0:T(8,128)(2,1)} %bitcast.17, f32[8,128]{1,0:T(8,128)S(1)} %broadcast_in_dim.3.token_ref), custom_call_target="tpu_custom_call" | custom-call | bytes 4096 | tf_op jit(solution)/shard_map/states/pallas_call | solution.py:101
  2.5 3.2 %collective-permute-start = (bf16[512,128]{1,0:T(8,128)(2,1)S(1)}, bf16[512,128]{1,0:T(8,128)(2,1)S(1)}, u32[]{:S(2)}, u32[]{:S(2)}) collective-permute-start(bf16[512,128]{1,0:T(8,128)(2,1)S(1)} %get-tuple-element.68), channel_id=1, source_target_pairs={{0,4},{1,5},{2,6},{3,7},{16,20},{17,21},{18,22},{19,23}} | collective-permute-start | bytes 393224 | tf_op jit(solution)/shard_map/ppermute | solution.py:315
  5.7 2.1 %states.4 = (bf16[512,128]{1,0:T(8,128)(2,1)S(1)}, bf16[512,128]{1,0:T(8,128)(2,1)S(1)}, f32[8,128]{1,0:T(8,128)S(1)}) custom-call(s32[1]{0:T(128)} %bitcast.me_ref, bf16[320,1024]{1,0:T(8,128)(2,1)} %bitcast.10, bf16[320,1024]{1,0:T(8,128)(2,1)} %bitcast.18, f32[8,128]{1,0:T(8,128)S(1)} %get-tuple-element.61.token_ref), custom_call_target="tpu_custom_call" | custom-call | bytes 4096 | tf_op jit(solution)/shard_map/states/pallas_call | solution.py:101
  7.8 0.7 %collective-permute-start.1 = (bf16[512,128]{1,0:T(8,128)(2,1)S(1)}, bf16[512,128]{1,0:T(8,128)(2,1)S(1)}, u32[]{:S(2)}, u32[]{:S(2)}) collective-permute-start(bf16[512,128]{1,0:T(8,128)(2,1)S(1)} %get-tuple-element.70), channel_id=1, source_target_pairs={{4,8},{5,9},{6,10},{7,11},{20,24},{21,25},{22,26},{23,27}} | collective-permute-start | bytes 393224 | tf_op jit(solution)/shard_map/ppermute | solution.py:315
  8.5 0.2 states.5
  8.6 3.1 %collective-permute-start.2 = (bf16[512,128]{1,0:T(8,128)(2,1)S(1)}, bf16[512,128]{1,0:T(8,128)(2,1)S(1)}, u32[]{:S(2)}, u32[]{:S(2)}) collective-permute-start(bf16[512,128]{1,0:T(8,128)(2,1)S(1)} %get-tuple-element.71), channel_id=1, source_target_pairs={{0,8},{8,12},{1,9},{9,13},{2,10},{10,14},{3,11},{11,15},{16,24},{2... | collective-permute-start | bytes 393224 | tf_op jit(solution)/shard_map/ppermute | solution.py:315
  11.8 1.7 %intra.1 = (f32[320,1024]{1,0:T(8,128)S(1)}, bf16[1024,320]{1,0:T(8,128)(2,1)S(1)}, f32[8,128]{1,0:T(8,128)S(1)}) custom-call(bf16[320,1024]{1,0:T(8,128)(2,1)S(1)} %bitcast.25, bf16[320,1024]{1,0:T(8,128)(2,1)S(1)} %bitcast.12, bf16[320,1024]{1,0:T(8,128)(2,1)S(1)} %bitcast.20, f32[8,128]{1,0:T(8,128)S(1)} %get-tuple-element.64.token_ref), custom_call_target="tpu_custom_call" | custom-call | bytes 4096 | tf_op jit(solution)/shard_map/intra/pallas_call | solution.py:125
  13.6 0.7 %collective-permute-start.3 = (bf16[512,128]{1,0:T(8,128)(2,1)S(1)}, bf16[512,128]{1,0:T(8,128)(2,1)S(1)}, u32[]{:S(2)}, u32[]{:S(2)}) collective-permute-start(bf16[512,128]{1,0:T(8,128)(2,1)S(1)} %get-tuple-element.76), channel_id=1, source_target_pairs={{4,12},{5,13},{6,14},{7,15},{20,28},{21,29},{22,30},{23,31}} | collective-permute-start | bytes 393224 | tf_op jit(solution)/shard_map/ppermute | solution.py:315
  14.3 1.3 %collective-permute-start.4 = (bf16[512,128]{1,0:T(8,128)(2,1)S(1)}, bf16[512,128]{1,0:T(8,128)(2,1)S(1)}, u32[]{:S(2)}, u32[]{:S(2)}) collective-permute-start(bf16[512,128]{1,0:T(8,128)(2,1)S(1)} %get-tuple-element.76), channel_id=1, source_target_pairs={{0,4},{4,8},{1,5},{5,9},{2,6},{6,10},{3,7},{7,11},{16,20},{20,24},... | collective-permute-start | bytes 393224 | tf_op jit(solution)/shard_map/ppermute | solution.py:315
  15.6 0.7 %collective-permute-start.5 = (bf16[512,128]{1,0:T(8,128)(2,1)S(1)}, bf16[512,128]{1,0:T(8,128)(2,1)S(1)}, u32[]{:S(2)}, u32[]{:S(2)}) collective-permute-start(bf16[512,128]{1,0:T(8,128)(2,1)S(1)} %get-tuple-element.80), channel_id=1, source_target_pairs={{8,12},{9,13},{10,14},{11,15},{24,28},{25,29},{26,30},{27,31}} | collective-permute-start | bytes 393224 | tf_op jit(solution)/shard_map/ppermute | solution.py:315
  16.3 1.2 %mid.4 = (bf16[320,512]{1,0:T(8,128)(2,1)S(1)}, bf16[320,512]{1,0:T(8,128)(2,1)S(1)}, bf16[512,128]{1,0:T(8,128)(2,1)S(1)}, f32[8,128]{1,0:T(8,128)S(1)}, bf16[512,128]{1,0:T(8,128)(2,1)S(1)}) custom-call(s32[1]{0:T(128)} %bitcast.me_ref, bf16[320,1024]{1,0:T(8,128)(2,1)S(1)} %bitcast.26, bf16[1024,320]{1,0:T(8,128)(2,1)S(1)} %get-tuple-element.65.qt_ref, ...), custom_call_target="tpu_custom_call" | custom-call | bytes 4096 | tf_op jit(solution)/shard_map/mid/pallas_call | solution.py:200
  17.6 0.7 %collective-permute-start.6 = (bf16[512,128]{1,0:T(8,128)(2,1)S(1)}, bf16[512,128]{1,0:T(8,128)(2,1)S(1)}, u32[]{:S(2)}, u32[]{:S(2)}) collective-permute-start(bf16[512,128]{1,0:T(8,128)(2,1)S(1)} %get-tuple-element.89), channel_id=1, source_target_pairs={{12,8},{8,4},{13,9},{9,5},{14,10},{10,6},{15,11},{11,7},{28,24},{2... | collective-permute-start | bytes 393224 | tf_op jit(solution)/shard_map/ppermute | solution.py:315
  18.3 1.2 %mid.6 = (bf16[320,512]{1,0:T(8,128)(2,1)S(1)}, bf16[320,512]{1,0:T(8,128)(2,1)S(1)}, bf16[512,128]{1,0:T(8,128)(2,1)S(1)}, f32[8,128]{1,0:T(8,128)S(1)}, bf16[512,128]{1,0:T(8,128)(2,1)S(1)}) custom-call(s32[1]{0:T(128)} %bitcast.me_ref, bf16[320,1024]{1,0:T(8,128)(2,1)S(1)} %bitcast.28, bf16[1024,320]{1,0:T(8,128)(2,1)S(1)} %get-tuple-element.65.qt_ref, ...), custom_call_target="tpu_custom_call" | custom-call | bytes 4096 | tf_op jit(solution)/shard_map/mid/pallas_call | solution.py:200
  19.5 1.3 %collective-permute-start.7 = (bf16[512,128]{1,0:T(8,128)(2,1)S(1)}, bf16[512,128]{1,0:T(8,128)(2,1)S(1)}, u32[]{:S(2)}, u32[]{:S(2)}) collective-permute-start(bf16[512,128]{1,0:T(8,128)(2,1)S(1)} %get-tuple-element.92), channel_id=1, source_target_pairs={{12,4},{4,0},{13,5},{5,1},{14,6},{6,2},{15,7},{7,3},{28,20},{20,16... | collective-permute-start | bytes 393224 | tf_op jit(solution)/shard_map/ppermute | solution.py:315
  20.8 2.6 %back.2 = (bf16[320,1024]{1,0:T(8,128)(2,1)}, bf16[320,1024]{1,0:T(8,128)(2,1)}, f32[320,512]{1,0:T(8,128)S(1)}, f32[320,512]{1,0:T(8,128)S(1)}, f32[8,128]{1,0:T(8,128)S(1)}) custom-call(s32[1]{0:T(128)} %bitcast.me_ref, bf16[320,1024]{1,0:T(8,128)(2,1)S(1)} %bitcast.30, bf16[320,1024]{1,0:T(8,128)(2,1)S(1)} %bitcast.13, bf16[320,1024]{1,0:T(8,128)(2,1)S(1)} %bitcast.21, ...), custom_call_target="tpu_custom_call" | custom-call | bytes 4096 | tf_op jit(solution)/shard_map/back/pallas_call | solution.py:253
  23.4 1.3 %collective-permute-start.8 = (bf16[512,128]{1,0:T(8,128)(2,1)S(1)}, bf16[512,128]{1,0:T(8,128)(2,1)S(1)}, u32[]{:S(2)}, u32[]{:S(2)}) collective-permute-start(bf16[512,128]{1,0:T(8,128)(2,1)S(1)} %get-tuple-element.109), channel_id=1, source_target_pairs={{8,0},{9,1},{10,2},{11,3},{24,16},{25,17},{26,18},{27,19}} | collective-permute-start | bytes 393224 | tf_op jit(solution)/shard_map/ppermute | solution.py:315
  24.7 0.7 %collective-permute-start.9 = (bf16[512,128]{1,0:T(8,128)(2,1)S(1)}, bf16[512,128]{1,0:T(8,128)(2,1)S(1)}, u32[]{:S(2)}, u32[]{:S(2)}) collective-permute-start(bf16[512,128]{1,0:T(8,128)(2,1)S(1)} %get-tuple-element.109), channel_id=1, source_target_pairs={{12,8},{8,4},{13,9},{9,5},{14,10},{10,6},{15,11},{11,7},{28,24},{2... | collective-permute-start | bytes 393224 | tf_op jit(solution)/shard_map/ppermute | solution.py:315
  25.4 3.0 %collective-permute-done.7.refs_1_ = bf16[512,128]{1,0:T(8,128)(2,1)S(1)} collective-permute-done((bf16[512,128]{1,0:T(8,128)(2,1)S(1)}, bf16[512,128]{1,0:T(8,128)(2,1)S(1)}, u32[]{:S(2)}, u32[]{:S(2)}) %collective-permute-start.7) | collective-permute-done | bytes 131104 | tf_op jit(solution)/shard_map/ppermute | solution.py:315
  28.5 1.5 %collective-permute-start.10 = (bf16[512,128]{1,0:T(8,128)(2,1)S(1)}, bf16[512,128]{1,0:T(8,128)(2,1)S(1)}, u32[]{:S(2)}, u32[]{:S(2)}) collective-permute-start(bf16[512,128]{1,0:T(8,128)(2,1)S(1)} %get-tuple-element.113), channel_id=1, source_target_pairs={{4,0},{5,1},{6,2},{7,3},{20,16},{21,17},{22,18},{23,19}} | collective-permute-start | bytes 393224 | tf_op jit(solution)/shard_map/ppermute | solution.py:315
  30.0 2.6 %back.3 = (bf16[320,1024]{1,0:T(8,128)(2,1)}, bf16[320,1024]{1,0:T(8,128)(2,1)}, f32[320,512]{1,0:T(8,128)S(1)}, f32[320,512]{1,0:T(8,128)S(1)}, f32[8,128]{1,0:T(8,128)S(1)}) custom-call(s32[1]{0:T(128)} %bitcast.me_ref, bf16[320,1024]{1,0:T(8,128)(2,1)S(1)} %bitcast.31, ...), custom_call_target="tpu_custom_call", output_to_operand_aliasing={{0}: (11, {}), {1}: (12, {})} | custom-call | bytes 4096 | tf_op jit(solution)/shard_map/back/pallas_call | solution.py:253
  32.5 1.4 %collective-permute-done.8.refs_2_ = bf16[512,128]{1,0:T(8,128)(2,1)S(1)} collective-permute-done((bf16[512,128]{1,0:T(8,128)(2,1)S(1)}, bf16[512,128]{1,0:T(8,128)(2,1)S(1)}, u32[]{:S(2)}, u32[]{:S(2)}) %collective-permute-start.8) | collective-permute-done | bytes 131104 | tf_op jit(solution)/shard_map/ppermute | solution.py:315
  34.0 1.1 %post.2 = (bf16[320,1024]{1,0:T(8,128)(2,1)}, bf16[320,1024]{1,0:T(8,128)(2,1)}, f32[8,128]{1,0:T(8,128)S(1)}) custom-call(s32[1]{0:T(128)} %bitcast.me_ref, bf16[320,1024]{1,0:T(8,128)(2,1)S(1)} %bitcast.15, bf16[320,1024]{1,0:T(8,128)(2,1)S(1)} %bitcast.23, f32[320,512]{1,0:T(8,128)S(1)} %get-tuple-element.106.gk_in_ref, ...), custom_call_target="tpu_custom_call" | custom-call | bytes 4096 | tf_op jit(solution)/shard_map/post/pallas_call | solution.py:286
  35.1 1.1 %collective-permute-done.10.refs_1_ = bf16[512,128]{1,0:T(8,128)(2,1)S(1)} collective-permute-done((bf16[512,128]{1,0:T(8,128)(2,1)S(1)}, bf16[512,128]{1,0:T(8,128)(2,1)S(1)}, u32[]{:S(2)}, u32[]{:S(2)}) %collective-permute-start.10) | collective-permute-done | bytes 131104 | tf_op jit(solution)/shard_map/ppermute | solution.py:315
  36.3 1.7 %post.3 = (bf16[320,1024]{1,0:T(8,128)(2,1)}, bf16[320,1024]{1,0:T(8,128)(2,1)}, f32[8,128]{1,0:T(8,128)}) custom-call(s32[1]{0:T(128)} %bitcast.me_ref, bf16[320,1024]{1,0:T(8,128)(2,1)S(1)} %bitcast.16, bf16[320,1024]{1,0:T(8,128)(2,1)S(1)} %bitcast.24, f32[320,512]{1,0:T(8,128)S(1)} %get-tuple-element.104.gk_in_ref, ...), custom_call_target="tpu_custom_call", output_to_operand_aliasing={{0}: (8, {}), {1}: (9, {})} | custom-call | bytes 4096 | tf_op jit(solution)/shard_map/post/pallas_call | solution.py:286
  (24 shorter events, 0.4 us)
Async XLA Ops:
  2.5 11.0 %collective-permute-start = (bf16[512,128]{1,0:T(8,128)(2,1)S(1)}, bf16[512,128]{1,0:T(8,128)(2,1)S(1)}, u32[]{:S(2)}, u32[]{:S(2)}) collective-permute-start(bf16[512,128]{1,0:T(8,128)(2,1)S(1)} %get-tuple-element.68), channel_id=1, source_target_pairs={{0,4},{1,5},{2,6},{3,7},{16,20},{17,21},{18,22},{19,23}} | collective-permute-start | bytes 393224 | tf_op jit(solution)/shard_map/ppermute | solution.py:315
  5.7 6.1 %copy-start = (bf16[1,320,1024]{2,1,0:T(8,128)(2,1)S(1)}, bf16[1,320,1024]{2,1,0:T(8,128)(2,1)}, u32[]{:S(2)}) copy-start(bf16[1,320,1024]{2,1,0:T(8,128)(2,1)} %param.5) | copy-start | bytes 1966084
  5.7 6.1 %copy-start.1 = (bf16[1,320,1024]{2,1,0:T(8,128)(2,1)S(1)}, bf16[1,320,1024]{2,1,0:T(8,128)(2,1)}, u32[]{:S(2)}) copy-start(bf16[1,320,1024]{2,1,0:T(8,128)(2,1)} %param.6) | copy-start | bytes 1966084
  5.7 6.1 %copy-start.2 = (bf16[1,320,1024]{2,1,0:T(8,128)(2,1)S(1)}, bf16[1,320,1024]{2,1,0:T(8,128)(2,1)}, u32[]{:S(2)}) copy-start(bf16[1,320,1024]{2,1,0:T(8,128)(2,1)} %param.4) | copy-start | bytes 1966084
  7.8 7.8 %collective-permute-start.1 = (bf16[512,128]{1,0:T(8,128)(2,1)S(1)}, bf16[512,128]{1,0:T(8,128)(2,1)S(1)}, u32[]{:S(2)}, u32[]{:S(2)}) collective-permute-start(bf16[512,128]{1,0:T(8,128)(2,1)S(1)} %get-tuple-element.70), channel_id=1, source_target_pairs={{4,8},{5,9},{6,10},{7,11},{20,24},{21,25},{22,26},{23,27}} | collective-permute-start | bytes 393224 | tf_op jit(solution)/shard_map/ppermute | solution.py:315
  8.6 6.9 %collective-permute-start.2 = (bf16[512,128]{1,0:T(8,128)(2,1)S(1)}, bf16[512,128]{1,0:T(8,128)(2,1)S(1)}, u32[]{:S(2)}, u32[]{:S(2)}) collective-permute-start(bf16[512,128]{1,0:T(8,128)(2,1)S(1)} %get-tuple-element.71), channel_id=1, source_target_pairs={{0,8},{8,12},{1,9},{9,13},{2,10},{10,14},{3,11},{11,15},{16,24},{2... | collective-permute-start | bytes 393224 | tf_op jit(solution)/shard_map/ppermute | solution.py:315
  11.8 4.5 %copy-start.3 = (bf16[1,320,1024]{2,1,0:T(8,128)(2,1)S(1)}, bf16[1,320,1024]{2,1,0:T(8,128)(2,1)}, u32[]{:S(2)}) copy-start(bf16[1,320,1024]{2,1,0:T(8,128)(2,1)} %param.7) | copy-start | bytes 1966084
  13.6 3.9 %collective-permute-start.3 = (bf16[512,128]{1,0:T(8,128)(2,1)S(1)}, bf16[512,128]{1,0:T(8,128)(2,1)S(1)}, u32[]{:S(2)}, u32[]{:S(2)}) collective-permute-start(bf16[512,128]{1,0:T(8,128)(2,1)S(1)} %get-tuple-element.76), channel_id=1, source_target_pairs={{4,12},{5,13},{6,14},{7,15},{20,28},{21,29},{22,30},{23,31}} | collective-permute-start | bytes 393224 | tf_op jit(solution)/shard_map/ppermute | solution.py:315
  14.3 4.0 %collective-permute-start.4 = (bf16[512,128]{1,0:T(8,128)(2,1)S(1)}, bf16[512,128]{1,0:T(8,128)(2,1)S(1)}, u32[]{:S(2)}, u32[]{:S(2)}) collective-permute-start(bf16[512,128]{1,0:T(8,128)(2,1)S(1)} %get-tuple-element.76), channel_id=1, source_target_pairs={{0,4},{4,8},{1,5},{5,9},{2,6},{6,10},{3,7},{7,11},{16,20},{20,24},... | collective-permute-start | bytes 393224 | tf_op jit(solution)/shard_map/ppermute | solution.py:315
  15.6 3.8 %collective-permute-start.5 = (bf16[512,128]{1,0:T(8,128)(2,1)S(1)}, bf16[512,128]{1,0:T(8,128)(2,1)S(1)}, u32[]{:S(2)}, u32[]{:S(2)}) collective-permute-start(bf16[512,128]{1,0:T(8,128)(2,1)S(1)} %get-tuple-element.80), channel_id=1, source_target_pairs={{8,12},{9,13},{10,14},{11,15},{24,28},{25,29},{26,30},{27,31}} | collective-permute-start | bytes 393224 | tf_op jit(solution)/shard_map/ppermute | solution.py:315
  17.6 5.8 %collective-permute-start.6 = (bf16[512,128]{1,0:T(8,128)(2,1)S(1)}, bf16[512,128]{1,0:T(8,128)(2,1)S(1)}, u32[]{:S(2)}, u32[]{:S(2)}) collective-permute-start(bf16[512,128]{1,0:T(8,128)(2,1)S(1)} %get-tuple-element.89), channel_id=1, source_target_pairs={{12,8},{8,4},{13,9},{9,5},{14,10},{10,6},{15,11},{11,7},{28,24},{2... | collective-permute-start | bytes 393224 | tf_op jit(solution)/shard_map/ppermute | solution.py:315
  19.5 8.9 %collective-permute-start.7 = (bf16[512,128]{1,0:T(8,128)(2,1)S(1)}, bf16[512,128]{1,0:T(8,128)(2,1)S(1)}, u32[]{:S(2)}, u32[]{:S(2)}) collective-permute-start(bf16[512,128]{1,0:T(8,128)(2,1)S(1)} %get-tuple-element.92), channel_id=1, source_target_pairs={{12,4},{4,0},{13,5},{5,1},{14,6},{6,2},{15,7},{7,3},{28,20},{20,16... | collective-permute-start | bytes 393224 | tf_op jit(solution)/shard_map/ppermute | solution.py:315
  23.4 10.5 %collective-permute-start.8 = (bf16[512,128]{1,0:T(8,128)(2,1)S(1)}, bf16[512,128]{1,0:T(8,128)(2,1)S(1)}, u32[]{:S(2)}, u32[]{:S(2)}) collective-permute-start(bf16[512,128]{1,0:T(8,128)(2,1)S(1)} %get-tuple-element.109), channel_id=1, source_target_pairs={{8,0},{9,1},{10,2},{11,3},{24,16},{25,17},{26,18},{27,19}} | collective-permute-start | bytes 393224 | tf_op jit(solution)/shard_map/ppermute | solution.py:315
  24.7 10.4 %collective-permute-start.9 = (bf16[512,128]{1,0:T(8,128)(2,1)S(1)}, bf16[512,128]{1,0:T(8,128)(2,1)S(1)}, u32[]{:S(2)}, u32[]{:S(2)}) collective-permute-start(bf16[512,128]{1,0:T(8,128)(2,1)S(1)} %get-tuple-element.109), channel_id=1, source_target_pairs={{12,8},{8,4},{13,9},{9,5},{14,10},{10,6},{15,11},{11,7},{28,24},{2... | collective-permute-start | bytes 393224 | tf_op jit(solution)/shard_map/ppermute | solution.py:315
  28.5 7.8 %collective-permute-start.10 = (bf16[512,128]{1,0:T(8,128)(2,1)S(1)}, bf16[512,128]{1,0:T(8,128)(2,1)S(1)}, u32[]{:S(2)}, u32[]{:S(2)}) collective-permute-start(bf16[512,128]{1,0:T(8,128)(2,1)S(1)} %get-tuple-element.113), channel_id=1, source_target_pairs={{4,0},{5,1},{6,2},{7,3},{20,16},{21,17},{22,18},{23,19}} | collective-permute-start | bytes 393224 | tf_op jit(solution)/shard_map/ppermute | solution.py:315

commit v4 on v3

--- a/solution.py
+++ b/solution.py
@@ -60,17 +60,40 @@
     return pl.when(among(me, roles)) if roles else lambda body: body()
 
 
-def state_kernel(plan, duplicate, me_ref, k_ref, v_ref, token_ref, *refs):
-    spare, outs = refs[: len(duplicate[:1])], refs[len(duplicate[:1]) : -5]
-    done_ref, k_buf, v_buf, k_sem, v_sem = refs[-5:]
+def near_state_kernel(half, roles, keep, me_ref, k_ref, v_ref, token_ref, *refs):
+    passed = (len(refs) - 2 - len(keep)) // 2
+    out_ref, done_ref, *copies = refs[-2 - passed :]
+    heads = out_ref.shape[0] // DH
+    done_ref[...] = token_ref[...]
+    for source, copy in zip(refs[len(keep) :], copies):
+        copy[...] = source[...]
+    if keep:
+
+        @on(me_ref[0], keep)
+        def _():
+            out_ref[...] = refs[0][...]
+
+    @on(me_ref[0], roles)
+    def _():
+        for h in range(heads):
+            cols = head(half * heads + h)
+            out_ref[head(h), :] = dot_tn(k_ref[:, cols], v_ref[:, cols]).astype(BF16)
+
+
+def near_states(half, roles, me, k, v, token, keep=(), spare=(), passed=()):
+    shape = jax.ShapeDtypeStruct((k.shape[1] // 2, DH), BF16)
+    return pl.pallas_call(
+        functools.partial(near_state_kernel, half, roles, keep),
+        in_specs=[SMEM_SPEC] + [VMEM_SPEC] * (3 + len(spare) + len(passed)),
+        out_specs=(VMEM_SPEC,) * (2 + len(passed)),
+        **params("near_states", (shape, TOKEN) + (shape,) * len(passed)),
+    )(me, k, v, token, *spare, *passed)
+
+
+def state_kernel(plan, me_ref, k_ref, v_ref, token_ref, *refs):
+    outs, (done_ref, k_buf, v_buf, k_sem, v_sem) = refs[:-5], refs[-5:]
     heads = outs[0].shape[0] // DH
     done_ref[...] = token_ref[...]
-    if duplicate:
-
-        @on(me_ref[0], (duplicate[0],))
-        def _():
-            outs[duplicate[1]][...] = spare[0][...]
-
     for roles, pieces in plan:
 
         @on(me_ref[0], roles)
@@ -92,19 +115,19 @@
                 out_ref[rows, :] = dot_tn(k_buf[slot], v_buf[slot]).astype(BF16)
 
 
-def states(plan, me, k, v, token, duplicate=(), spare=()):
+def states(plan, me, k, v, token):
     length, width = k.shape
     count = 1 + max(out for _, pieces in plan for _, out in pieces)
     slots = max(len(pieces) for _, pieces in plan) * width // (2 * DH)
     k, v = (pltpu.with_memory_space_constraint(x, pltpu.HBM) for x in (k, v))
     shape = jax.ShapeDtypeStruct((width // 2, DH), BF16)
     return pl.pallas_call(
-        functools.partial(state_kernel, plan, duplicate),
-        in_specs=[SMEM_SPEC, HBM_SPEC, HBM_SPEC] + [VMEM_SPEC] * (1 + len(spare)),
+        functools.partial(state_kernel, plan),
+        in_specs=[SMEM_SPEC, HBM_SPEC, HBM_SPEC, VMEM_SPEC],
         out_specs=(VMEM_SPEC,) * (count + 1),
         scratch_shapes=[pltpu.VMEM((slots, length, DH), BF16)] * 2 + [pltpu.SemaphoreType.DMA((slots,))] * 2,
         **params("states", (shape,) * count + (TOKEN,)),
-    )(me, k, v, token, *spare)
+    )(me, k, v, token)
 
 
 TOKEN = jax.ShapeDtypeStruct((8, DH), F32)
@@ -187,8 +210,9 @@
             normed = mixed * inverse
             grad = (inverse * (g - normed * along)).astype(BF16)
             grad_ref[:, head(h)] = grad
+            state = dot_nn(qt_ref[cols, :], grad).astype(BF16)
             for ref in state_refs:
-                ref[head(h), :] = dot_nn(qt_ref[cols, :], grad).astype(BF16)
+                ref[head(h), :] = state
             normed_ref[:, head(h)] = normed.astype(BF16)
 
 
@@ -260,9 +284,13 @@
     )(me, q, k, v, token, *(x for one in sets for x in one), *filled)
 
 
+def post_first_kernel(half_of, parts, *refs):
+    refs[-5][...] = refs[5][...]
+    post_kernel(half_of, parts, *refs[:-5], *refs[-4:])
+
+
 def post_kernel(half_of, parts, me_ref, k_ref, v_ref, gk_in_ref, gv_in_ref, token_ref, *refs):
-    l_refs, (gk_ref, gv_ref, done_ref, gk_buf, gv_buf, gk_sem, gv_sem) = refs[:parts], refs[-7:]
-    done_ref[...] = token_ref[...]
+    l_refs, (gk_ref, gv_ref, gk_buf, gv_buf, gk_sem, gv_sem) = refs[:parts], refs[-6:]
     heads = gk_in_ref.shape[1] // DH
     half = half_of(me_ref[0])
     copies = []
@@ -283,13 +311,14 @@
     length, width = k.shape
     heads = width // (2 * DH)
     first = 6 + len(later)
-    return pl.pallas_call(
-        functools.partial(post_kernel, half_of, len(later)),
+    whole = jax.ShapeDtypeStruct(k.shape, BF16)
+    return pl.pallas_call(
+        functools.partial(post_kernel if filled else post_first_kernel, half_of, len(later)),
         in_specs=[SMEM_SPEC] + [VMEM_SPEC] * (first - 1) + [HBM_SPEC] * len(filled),
-        out_specs=(HBM_SPEC, HBM_SPEC, VMEM_SPEC),
+        out_specs=(HBM_SPEC, HBM_SPEC) if filled else (HBM_SPEC, HBM_SPEC, VMEM_SPEC),
         scratch_shapes=[pltpu.VMEM((heads, length, DH), BF16)] * 2 + [pltpu.SemaphoreType.DMA((heads,))] * 2,
         input_output_aliases={first: 0, first + 1: 1} if filled else {},
-        **params("post", (jax.ShapeDtypeStruct(k.shape, BF16), jax.ShapeDtypeStruct(k.shape, BF16), TOKEN)),
+        **params("post", (whole, whole) if filled else (whole, whole, TOKEN)),
     )(me, k, v, gk_in, gv_in, token, *later, *filled)
 
 
@@ -316,15 +345,17 @@
 
     s_a, token = states((((0,), ((0, 0),)),), me, k, v, token)
     r_a = send(s_a, [(0, 1)])
-    s_x, s_b, token = states((((0,), ((1, 0),)), ((1,), ((1, 1), (0, 0)))), me, k, v, token)
+    s_b, token = near_states(1, (0, 1), me, k, v, token)
     r_b = send(s_b, [(1, 2)])
-    s_c, s_y, token = states((((2,), ((0, 0), (1, 1))),), me, k, v, token, (0, 0), (s_x,))
+    s_c, token = near_states(0, (1, 2), me, k, v, token, (0,), (s_b,))
     r_c = send(s_c, [(0, 2), (2, 3)])
     intra_out, qt, token = intra(q, k, v, token)
     shared = (q, qt, g, intra_out)
-    s12, token = add(token, r_a, s_x)
+    s12, token = add(token, r_a, s_c)
     r_far = send(s12, [(1, 3)])
+    s_y, token, s12 = near_states(1, (2,), me, k, v, token, passed=(s12,))
     r_near = send(s12, [(0, 1), (1, 2)])
+    r_b, token = add(token, r_b)
     s123, token = add(token, r_b, r_c, s_y)
     first, g_first, token = mid(even_half, (0, 1, 2), me, shared, token, (r_a, r_b, r_c))
     r_last = send(s123, [(2, 3)])
@@ -344,7 +375,7 @@
     )
     *filled, token = post(odd_half, me, k, v, gk_second, gv_second, token, (u_one, u_two, w_far))
     l_near, token = add(token, w_near)
-    grad_k, grad_v, token = post(even_half, me, k, v, gk_first, gv_first, token, (l_near, w_last), filled)
+    grad_k, grad_v = post(even_half, me, k, v, gk_first, gv_first, token, (l_near, w_last), filled)
     return tuple(x.reshape(out_shape) for x in (normed, grad_q, grad_k, grad_v))
 
 
@@ -382,7 +413,7 @@
     normed, grad_q, gk1, gv1, token = back(low_half, (), me, q, k, v, token, (low,))
     normed, grad_q, gk2, gv2, token = back(high_half, (), me, q, k, v, token, (high,), (normed, grad_q))
     *filled, token = post(low_half, me, k, v, gk1, gv1, token, (l1,))
-    grad_k, grad_v, token = post(high_half, me, k, v, gk2, gv2, token, (l2,), filled)
+    grad_k, grad_v = post(high_half, me, k, v, gk2, gv2, token, (l2,), filled)
     return tuple(x.reshape(out_shape) for x in (normed, grad_q, grad_k, grad_v))
 
 

time: 38.5 us -> 36 us (0.935)
  Pallas kernels: 16.3 us -> 14 us
  waiting for transfers between devices: 5.66 us -> 3.85 us
  starting transfers between devices: 15 us -> 16.6 us
    pallas_call x5 -> x6, Pallas kernels: 6.91 us -> 4.56 us  [the longest x2 2.26 us: post(): pl.pallas_call(functools.partial(post_kernel if filled else post_first_ke...]
    ppermute x11, waiting for transfers between devices: 5.66 us -> 3.85 us  [send(): return lax.ppermute(x, 'ctx', pairs)]
    ppermute x11, starting transfers between devices: 15 us -> 16.6 us  [send(): return lax.ppermute(x, 'ctx', pairs)]
  transfers between devices with their start and end apart: 11 -> 11, of which waited for: 4 -> 3; matrix products, arithmetic and copies ran while one was open for 0% -> 0% of each run, Pallas kernels for 33% -> 31%
where the time goes in v4:
time: 36 us; the launch traced here: 35.7 us
  starting transfers between devices  16.6 us (46%)
  Pallas kernels  14 us (39%)
  waiting for transfers between devices  3.85 us (11%)
  between operations  1.15 us (3%)
    ppermute x11, starting transfers between devices, send(): return lax.ppermute(x, 'ctx', pairs)  16.6 us
    pallas_call x2, Pallas kernels, back(): pl.pallas_call(functools.partial(back_kernel, half_of, roles, len(sets)),...  5.14 us
    ppermute x11, waiting for transfers between devices, send(): return lax.ppermute(x, 'ctx', pairs)  3.85 us
    pallas_call x4, Pallas kernels, mid(): pl.pallas_call(functools.partial(mid_kernel, half_of, roles, keep, merge)...  2.4 us
    pallas_call x2, Pallas kernels, post(): pl.pallas_call(functools.partial(post_kernel if filled else post_first_ke...  2.26 us
    pallas_call x1, Pallas kernels, states(): pl.pallas_call(functools.partial(state_kernel, plan), in_specs=[SMEM_SPEC...  1.95 us
    pallas_call x1, Pallas kernels, intra(): pl.pallas_call(intra_kernel, in_specs=[VMEM_SPEC] * 4, out_specs=(VMEM_SP...  1.68 us
  transfers between devices with their start and end apart: 11, of which 3 were waited for; matrix products, arithmetic and copies ran while one was open for 0% of the time, Pallas kernels for 31%

profile of v4, /device:TPU:0, one launch (start us, length us, event | category | flops | bytes accessed | tf_op | source)
XLA Modules:
  0.0 35.7 jit_solution(8021109631350774576)
XLA Ops:
  0.7 1.9 %states.1 = (bf16[512,128]{1,0:T(8,128)(2,1)S(1)}, f32[8,128]{1,0:T(8,128)S(1)}) custom-call(s32[1]{0:T(128)} %bitcast.me_ref.refs_0_, bf16[320,1024]{1,0:T(8,128)(2,1)} %bitcast.9, bf16[320,1024]{1,0:T(8,128)(2,1)} %bitcast.18, f32[8,128]{1,0:T(8,128)S(1)} %broadcast_in_dim.3.token_ref), custom_call_target="tpu_custom_call" | custom-call | bytes 4096 | tf_op jit(solution)/shard_map/states/pallas_call | solution.py:124
  2.6 3.2 %collective-permute-start = (bf16[512,128]{1,0:T(8,128)(2,1)S(1)}, bf16[512,128]{1,0:T(8,128)(2,1)S(1)}, u32[]{:S(2)}, u32[]{:S(2)}) collective-permute-start(bf16[512,128]{1,0:T(8,128)(2,1)S(1)} %get-tuple-element.71), channel_id=1, source_target_pairs={{0,4},{1,5},{2,6},{3,7},{16,20},{17,21},{18,22},{19,23}} | collective-permute-start | bytes 393224 | tf_op jit(solution)/shard_map/ppermute | solution.py:344
  5.9 0.3 near_states.3
  6.2 0.7 %collective-permute-start.1 = (bf16[512,128]{1,0:T(8,128)(2,1)S(1)}, bf16[512,128]{1,0:T(8,128)(2,1)S(1)}, u32[]{:S(2)}, u32[]{:S(2)}) collective-permute-start(bf16[512,128]{1,0:T(8,128)(2,1)S(1)} %get-tuple-element.66.refs_0_), channel_id=1, source_target_pairs={{4,8},{5,9},{6,10},{7,11},{20,24},{21,25},{22,26},{23,27}} | collective-permute-start | bytes 393224 | tf_op jit(solution)/shard_map/ppermute | solution.py:344
  6.9 2.7 %collective-permute-start.2 = (bf16[512,128]{1,0:T(8,128)(2,1)S(1)}, bf16[512,128]{1,0:T(8,128)(2,1)S(1)}, u32[]{:S(2)}, u32[]{:S(2)}) collective-permute-start(bf16[512,128]{1,0:T(8,128)(2,1)S(1)} %get-tuple-element.72.refs_1_), channel_id=1, source_target_pairs={{0,8},{8,12},{1,9},{9,13},{2,10},{10,14},{3,11},{11,15},{16,24},{2... | collective-permute-start | bytes 393224 | tf_op jit(solution)/shard_map/ppermute | solution.py:344
  9.6 1.7 %intra.1 = (f32[320,1024]{1,0:T(8,128)S(1)}, bf16[1024,320]{1,0:T(8,128)(2,1)S(1)}, f32[8,128]{1,0:T(8,128)S(1)}) custom-call(bf16[320,1024]{1,0:T(8,128)(2,1)S(1)} %bitcast.27, bf16[320,1024]{1,0:T(8,128)(2,1)S(1)} %bitcast.12, bf16[320,1024]{1,0:T(8,128)(2,1)S(1)} %bitcast.21, f32[8,128]{1,0:T(8,128)S(1)} %get-tuple-element.67.token_ref), custom_call_target="tpu_custom_call" | custom-call | bytes 4096 | tf_op jit(solution)/shard_map/intra/pallas_call | solution.py:148
  11.4 0.8 %collective-permute-start.3 = (bf16[512,128]{1,0:T(8,128)(2,1)S(1)}, bf16[512,128]{1,0:T(8,128)(2,1)S(1)}, u32[]{:S(2)}, u32[]{:S(2)}) collective-permute-start(bf16[512,128]{1,0:T(8,128)(2,1)S(1)} %get-tuple-element.74.refs_0_), channel_id=1, source_target_pairs={{4,12},{5,13},{6,14},{7,15},{20,28},{21,29},{22,30},{23,31}} | collective-permute-start | bytes 393224 | tf_op jit(solution)/shard_map/ppermute | solution.py:344
  12.2 3.2 %collective-permute-start.4 = (bf16[512,128]{1,0:T(8,128)(2,1)S(1)}, bf16[512,128]{1,0:T(8,128)(2,1)S(1)}, u32[]{:S(2)}, u32[]{:S(2)}) collective-permute-start(bf16[512,128]{1,0:T(8,128)(2,1)S(1)} %get-tuple-element.83), channel_id=1, source_target_pairs={{0,4},{4,8},{1,5},{5,9},{2,6},{6,10},{3,7},{7,11},{16,20},{20,24},... | collective-permute-start | bytes 393224 | tf_op jit(solution)/shard_map/ppermute | solution.py:344
  15.5 0.1 add.8
  15.5 0.7 %collective-permute-start.5 = (bf16[512,128]{1,0:T(8,128)(2,1)S(1)}, bf16[512,128]{1,0:T(8,128)(2,1)S(1)}, u32[]{:S(2)}, u32[]{:S(2)}) collective-permute-start(bf16[512,128]{1,0:T(8,128)(2,1)S(1)} %get-tuple-element.86), channel_id=1, source_target_pairs={{8,12},{9,13},{10,14},{11,15},{24,28},{25,29},{26,30},{27,31}} | collective-permute-start | bytes 393224 | tf_op jit(solution)/shard_map/ppermute | solution.py:344
  16.2 1.2 %mid.4 = (bf16[320,512]{1,0:T(8,128)(2,1)S(1)}, bf16[320,512]{1,0:T(8,128)(2,1)S(1)}, bf16[512,128]{1,0:T(8,128)(2,1)S(1)}, f32[8,128]{1,0:T(8,128)S(1)}, bf16[512,128]{1,0:T(8,128)(2,1)S(1)}) custom-call(s32[1]{0:T(128)} %bitcast.me_ref.refs_0_, bf16[320,1024]{1,0:T(8,128)(2,1)S(1)} %bitcast.28, bf16[1024,320]{1,0:T(8,128)(2,1)S(1)} %get-tuple-element.68.qt_ref, ...), custom_call_target="tpu_custom_call" | custom-call | bytes 4096 | tf_op jit(solution)/shard_map/mid/pallas_call | solution.py:224
  17.4 0.7 %collective-permute-start.6 = (bf16[512,128]{1,0:T(8,128)(2,1)S(1)}, bf16[512,128]{1,0:T(8,128)(2,1)S(1)}, u32[]{:S(2)}, u32[]{:S(2)}) collective-permute-start(bf16[512,128]{1,0:T(8,128)(2,1)S(1)} %get-tuple-element.95), channel_id=1, source_target_pairs={{12,8},{8,4},{13,9},{9,5},{14,10},{10,6},{15,11},{11,7},{28,24},{2... | collective-permute-start | bytes 393224 | tf_op jit(solution)/shard_map/ppermute | solution.py:344
  18.1 1.2 %mid.6 = (bf16[320,512]{1,0:T(8,128)(2,1)S(1)}, bf16[320,512]{1,0:T(8,128)(2,1)S(1)}, bf16[512,128]{1,0:T(8,128)(2,1)S(1)}, f32[8,128]{1,0:T(8,128)S(1)}, bf16[512,128]{1,0:T(8,128)(2,1)S(1)}) custom-call(s32[1]{0:T(128)} %bitcast.me_ref.refs_0_, bf16[320,1024]{1,0:T(8,128)(2,1)S(1)} %bitcast.30, bf16[1024,320]{1,0:T(8,128)(2,1)S(1)} %get-tuple-element.68.qt_ref, ...), custom_call_target="tpu_custom_call" | custom-call | bytes 4096 | tf_op jit(solution)/shard_map/mid/pallas_call | solution.py:224
  19.4 1.3 %collective-permute-start.7 = (bf16[512,128]{1,0:T(8,128)(2,1)S(1)}, bf16[512,128]{1,0:T(8,128)(2,1)S(1)}, u32[]{:S(2)}, u32[]{:S(2)}) collective-permute-start(bf16[512,128]{1,0:T(8,128)(2,1)S(1)} %get-tuple-element.98), channel_id=1, source_target_pairs={{12,4},{4,0},{13,5},{5,1},{14,6},{6,2},{15,7},{7,3},{28,20},{20,16... | collective-permute-start | bytes 393224 | tf_op jit(solution)/shard_map/ppermute | solution.py:344
  20.7 2.6 %back.2 = (bf16[320,1024]{1,0:T(8,128)(2,1)}, bf16[320,1024]{1,0:T(8,128)(2,1)}, f32[320,512]{1,0:T(8,128)S(1)}, f32[320,512]{1,0:T(8,128)S(1)}, f32[8,128]{1,0:T(8,128)S(1)}) custom-call(s32[1]{0:T(128)} %bitcast.me_ref.refs_0_, bf16[320,1024]{1,0:T(8,128)(2,1)S(1)} %bitcast.32, bf16[320,1024]{1,0:T(8,128)(2,1)S(1)} %bitcast.14, ...), custom_call_target="tpu_custom_call" | custom-call | bytes 4096 | tf_op jit(solution)/shard_map/back/pallas_call | solution.py:277
  23.3 1.3 %collective-permute-start.8 = (bf16[512,128]{1,0:T(8,128)(2,1)S(1)}, bf16[512,128]{1,0:T(8,128)(2,1)S(1)}, u32[]{:S(2)}, u32[]{:S(2)}) collective-permute-start(bf16[512,128]{1,0:T(8,128)(2,1)S(1)} %get-tuple-element.115), channel_id=1, source_target_pairs={{8,0},{9,1},{10,2},{11,3},{24,16},{25,17},{26,18},{27,19}} | collective-permute-start | bytes 393224 | tf_op jit(solution)/shard_map/ppermute | solution.py:344
  24.6 0.7 %collective-permute-start.9 = (bf16[512,128]{1,0:T(8,128)(2,1)S(1)}, bf16[512,128]{1,0:T(8,128)(2,1)S(1)}, u32[]{:S(2)}, u32[]{:S(2)}) collective-permute-start(bf16[512,128]{1,0:T(8,128)(2,1)S(1)} %get-tuple-element.115), channel_id=1, source_target_pairs={{12,8},{8,4},{13,9},{9,5},{14,10},{10,6},{15,11},{11,7},{28,24},{2... | collective-permute-start | bytes 393224 | tf_op jit(solution)/shard_map/ppermute | solution.py:344
  25.3 1.2 %collective-permute-done.7.refs_1_.refs_7_ = bf16[512,128]{1,0:T(8,128)(2,1)S(1)} collective-permute-done((bf16[512,128]{1,0:T(8,128)(2,1)S(1)}, bf16[512,128]{1,0:T(8,128)(2,1)S(1)}, u32[]{:S(2)}, u32[]{:S(2)}) %collective-permute-start.7) | collective-permute-done | bytes 131104 | tf_op jit(solution)/shard_map/ppermute | solution.py:344
  26.5 1.5 %collective-permute-start.10 = (bf16[512,128]{1,0:T(8,128)(2,1)S(1)}, bf16[512,128]{1,0:T(8,128)(2,1)S(1)}, u32[]{:S(2)}, u32[]{:S(2)}) collective-permute-start(bf16[512,128]{1,0:T(8,128)(2,1)S(1)} %get-tuple-element.119), channel_id=1, source_target_pairs={{4,0},{5,1},{6,2},{7,3},{20,16},{21,17},{22,18},{23,19}} | collective-permute-start | bytes 393224 | tf_op jit(solution)/shard_map/ppermute | solution.py:344
  28.0 2.6 %back.3 = (bf16[320,1024]{1,0:T(8,128)(2,1)}, bf16[320,1024]{1,0:T(8,128)(2,1)}, f32[320,512]{1,0:T(8,128)S(1)}, f32[320,512]{1,0:T(8,128)S(1)}, f32[8,128]{1,0:T(8,128)S(1)}) custom-call(s32[1]{0:T(128)} %bitcast.me_ref.refs_0_, bf16[320,1024]{1,0:T(8,128)(2,1)S(1)} %bitcast.33, ...), custom_call_target="tpu_custom_call", output_to_operand_aliasing={{0}: (11, {}), {1}: (12, {})} | custom-call | bytes 4096 | tf_op jit(solution)/shard_map/back/pallas_call | solution.py:277
  30.5 2.0 %collective-permute-done.8.refs_8_ = bf16[512,128]{1,0:T(8,128)(2,1)S(1)} collective-permute-done((bf16[512,128]{1,0:T(8,128)(2,1)S(1)}, bf16[512,128]{1,0:T(8,128)(2,1)S(1)}, u32[]{:S(2)}, u32[]{:S(2)}) %collective-permute-start.8) | collective-permute-done | bytes 131104 | tf_op jit(solution)/shard_map/ppermute | solution.py:344
  32.5 1.1 %post.2 = (bf16[320,1024]{1,0:T(8,128)(2,1)}, bf16[320,1024]{1,0:T(8,128)(2,1)}, f32[8,128]{1,0:T(8,128)S(1)}) custom-call(s32[1]{0:T(128)} %bitcast.me_ref.refs_0_, bf16[320,1024]{1,0:T(8,128)(2,1)S(1)} %bitcast.16, bf16[320,1024]{1,0:T(8,128)(2,1)S(1)} %bitcast.25, f32[320,512]{1,0:T(8,128)S(1)} %get-tuple-element.112.refs_3_, ...), custom_call_target="tpu_custom_call" | custom-call | bytes 4096 | tf_op jit(solution)/shard_map/post/pallas_call | solution.py:315
  33.7 0.7 %collective-permute-done.10.refs_1_ = bf16[512,128]{1,0:T(8,128)(2,1)S(1)} collective-permute-done((bf16[512,128]{1,0:T(8,128)(2,1)S(1)}, bf16[512,128]{1,0:T(8,128)(2,1)S(1)}, u32[]{:S(2)}, u32[]{:S(2)}) %collective-permute-start.10) | collective-permute-done | bytes 131104 | tf_op jit(solution)/shard_map/ppermute | solution.py:344
  34.4 1.1 %post.3 = (bf16[320,1024]{1,0:T(8,128)(2,1)}, bf16[320,1024]{1,0:T(8,128)(2,1)}) custom-call(s32[1]{0:T(128)} %bitcast.me_ref.refs_0_, bf16[320,1024]{1,0:T(8,128)(2,1)S(1)} %bitcast.17, bf16[320,1024]{1,0:T(8,128)(2,1)S(1)} %bitcast.26, f32[320,512]{1,0:T(8,128)S(1)} %get-tuple-element.110.gk_in_ref, ...), custom_call_target="tpu_custom_call", output_to_operand_aliasing={{0}: (8, {}), {1}: (9, {})} | custom-call | bytes 4096 | tf_op jit(solution)/shard_map/post/pallas_call | solution.py:315
  (26 shorter events, 0.3 us)
Async XLA Ops:
  0.6 5.2 %copy-start.1 = (bf16[1,320,1024]{2,1,0:T(8,128)(2,1)S(1)}, bf16[1,320,1024]{2,1,0:T(8,128)(2,1)}, u32[]{:S(2)}) copy-start(bf16[1,320,1024]{2,1,0:T(8,128)(2,1)} %param.6) | copy-start | bytes 1966084
  0.6 5.2 %copy-start = (bf16[1,320,1024]{2,1,0:T(8,128)(2,1)S(1)}, bf16[1,320,1024]{2,1,0:T(8,128)(2,1)}, u32[]{:S(2)}) copy-start(bf16[1,320,1024]{2,1,0:T(8,128)(2,1)} %param.5) | copy-start | bytes 1966084
  2.6 8.7 %collective-permute-start = (bf16[512,128]{1,0:T(8,128)(2,1)S(1)}, bf16[512,128]{1,0:T(8,128)(2,1)S(1)}, u32[]{:S(2)}, u32[]{:S(2)}) collective-permute-start(bf16[512,128]{1,0:T(8,128)(2,1)S(1)} %get-tuple-element.71), channel_id=1, source_target_pairs={{0,4},{1,5},{2,6},{3,7},{16,20},{17,21},{18,22},{19,23}} | collective-permute-start | bytes 393224 | tf_op jit(solution)/shard_map/ppermute | solution.py:344
  5.9 3.8 %copy-start.2 = (bf16[1,320,1024]{2,1,0:T(8,128)(2,1)S(1)}, bf16[1,320,1024]{2,1,0:T(8,128)(2,1)}, u32[]{:S(2)}) copy-start(bf16[1,320,1024]{2,1,0:T(8,128)(2,1)} %param.4) | copy-start | bytes 1966084
  6.2 9.2 %collective-permute-start.1 = (bf16[512,128]{1,0:T(8,128)(2,1)S(1)}, bf16[512,128]{1,0:T(8,128)(2,1)S(1)}, u32[]{:S(2)}, u32[]{:S(2)}) collective-permute-start(bf16[512,128]{1,0:T(8,128)(2,1)S(1)} %get-tuple-element.66.refs_0_), channel_id=1, source_target_pairs={{4,8},{5,9},{6,10},{7,11},{20,24},{21,25},{22,26},{23,27}} | collective-permute-start | bytes 393224 | tf_op jit(solution)/shard_map/ppermute | solution.py:344
  6.9 8.6 %collective-permute-start.2 = (bf16[512,128]{1,0:T(8,128)(2,1)S(1)}, bf16[512,128]{1,0:T(8,128)(2,1)S(1)}, u32[]{:S(2)}, u32[]{:S(2)}) collective-permute-start(bf16[512,128]{1,0:T(8,128)(2,1)S(1)} %get-tuple-element.72.refs_1_), channel_id=1, source_target_pairs={{0,8},{8,12},{1,9},{9,13},{2,10},{10,14},{3,11},{11,15},{16,24},{2... | collective-permute-start | bytes 393224 | tf_op jit(solution)/shard_map/ppermute | solution.py:344
  11.3 4.9 %copy-start.3 = (bf16[1,320,1024]{2,1,0:T(8,128)(2,1)S(1)}, bf16[1,320,1024]{2,1,0:T(8,128)(2,1)}, u32[]{:S(2)}) copy-start(bf16[1,320,1024]{2,1,0:T(8,128)(2,1)} %param.7) | copy-start | bytes 1966084
  11.4 6.0 %collective-permute-start.3 = (bf16[512,128]{1,0:T(8,128)(2,1)S(1)}, bf16[512,128]{1,0:T(8,128)(2,1)S(1)}, u32[]{:S(2)}, u32[]{:S(2)}) collective-permute-start(bf16[512,128]{1,0:T(8,128)(2,1)S(1)} %get-tuple-element.74.refs_0_), channel_id=1, source_target_pairs={{4,12},{5,13},{6,14},{7,15},{20,28},{21,29},{22,30},{23,31}} | collective-permute-start | bytes 393224 | tf_op jit(solution)/shard_map/ppermute | solution.py:344
  12.2 5.9 %collective-permute-start.4 = (bf16[512,128]{1,0:T(8,128)(2,1)S(1)}, bf16[512,128]{1,0:T(8,128)(2,1)S(1)}, u32[]{:S(2)}, u32[]{:S(2)}) collective-permute-start(bf16[512,128]{1,0:T(8,128)(2,1)S(1)} %get-tuple-element.83), channel_id=1, source_target_pairs={{0,4},{4,8},{1,5},{5,9},{2,6},{6,10},{3,7},{7,11},{16,20},{20,24},... | collective-permute-start | bytes 393224 | tf_op jit(solution)/shard_map/ppermute | solution.py:344
  15.5 3.8 %collective-permute-start.5 = (bf16[512,128]{1,0:T(8,128)(2,1)S(1)}, bf16[512,128]{1,0:T(8,128)(2,1)S(1)}, u32[]{:S(2)}, u32[]{:S(2)}) collective-permute-start(bf16[512,128]{1,0:T(8,128)(2,1)S(1)} %get-tuple-element.86), channel_id=1, source_target_pairs={{8,12},{9,13},{10,14},{11,15},{24,28},{25,29},{26,30},{27,31}} | collective-permute-start | bytes 393224 | tf_op jit(solution)/shard_map/ppermute | solution.py:344
  17.4 5.8 %collective-permute-start.6 = (bf16[512,128]{1,0:T(8,128)(2,1)S(1)}, bf16[512,128]{1,0:T(8,128)(2,1)S(1)}, u32[]{:S(2)}, u32[]{:S(2)}) collective-permute-start(bf16[512,128]{1,0:T(8,128)(2,1)S(1)} %get-tuple-element.95), channel_id=1, source_target_pairs={{12,8},{8,4},{13,9},{9,5},{14,10},{10,6},{15,11},{11,7},{28,24},{2... | collective-permute-start | bytes 393224 | tf_op jit(solution)/shard_map/ppermute | solution.py:344
  19.4 7.1 %collective-permute-start.7 = (bf16[512,128]{1,0:T(8,128)(2,1)S(1)}, bf16[512,128]{1,0:T(8,128)(2,1)S(1)}, u32[]{:S(2)}, u32[]{:S(2)}) collective-permute-start(bf16[512,128]{1,0:T(8,128)(2,1)S(1)} %get-tuple-element.98), channel_id=1, source_target_pairs={{12,4},{4,0},{13,5},{5,1},{14,6},{6,2},{15,7},{7,3},{28,20},{20,16... | collective-permute-start | bytes 393224 | tf_op jit(solution)/shard_map/ppermute | solution.py:344
  23.3 9.2 %collective-permute-start.8 = (bf16[512,128]{1,0:T(8,128)(2,1)S(1)}, bf16[512,128]{1,0:T(8,128)(2,1)S(1)}, u32[]{:S(2)}, u32[]{:S(2)}) collective-permute-start(bf16[512,128]{1,0:T(8,128)(2,1)S(1)} %get-tuple-element.115), channel_id=1, source_target_pairs={{8,0},{9,1},{10,2},{11,3},{24,16},{25,17},{26,18},{27,19}} | collective-permute-start | bytes 393224 | tf_op jit(solution)/shard_map/ppermute | solution.py:344
  24.6 9.1 %collective-permute-start.9 = (bf16[512,128]{1,0:T(8,128)(2,1)S(1)}, bf16[512,128]{1,0:T(8,128)(2,1)S(1)}, u32[]{:S(2)}, u32[]{:S(2)}) collective-permute-start(bf16[512,128]{1,0:T(8,128)(2,1)S(1)} %get-tuple-element.115), channel_id=1, source_target_pairs={{12,8},{8,4},{13,9},{9,5},{14,10},{10,6},{15,11},{11,7},{28,24},{2... | collective-permute-start | bytes 393224 | tf_op jit(solution)/shard_map/ppermute | solution.py:344
  26.5 7.9 %collective-permute-start.10 = (bf16[512,128]{1,0:T(8,128)(2,1)S(1)}, bf16[512,128]{1,0:T(8,128)(2,1)S(1)}, u32[]{:S(2)}, u32[]{:S(2)}) collective-permute-start(bf16[512,128]{1,0:T(8,128)(2,1)S(1)} %get-tuple-element.119), channel_id=1, source_target_pairs={{4,0},{5,1},{6,2},{7,3},{20,16},{21,17},{22,18},{23,19}} | collective-permute-start | bytes 393224 | tf_op jit(solution)/shard_map/ppermute | solution.py:344

commit v5 on v4

--- a/solution.py
+++ b/solution.py
@@ -135,11 +135,17 @@
 
 def intra_kernel(q_ref, k_ref, v_ref, token_ref, out_ref, qt_ref, done_ref):
     mask = causal(q_ref.shape[0])
-    for h in range(q_ref.shape[1] // DH):
-        q = q_ref[:, head(h)]
-        scores = jnp.where(mask, dot_nt(q, k_ref[:, head(h)]), 0.0).astype(BF16)
+    heads = q_ref.shape[1] // DH
+
+    def scores_of(h):
+        return jnp.where(mask, dot_nt(q_ref[:, head(h)], k_ref[:, head(h)]), 0.0).astype(BF16)
+
+    scores = scores_of(0)
+    for h in range(heads):
+        ahead = scores_of(h + 1) if h + 1 < heads else None
         out_ref[:, head(h)] = dot_nn(scores, v_ref[:, head(h)])
-        qt_ref[head(h), :] = q.T
+        qt_ref[head(h), :] = q_ref[:, head(h)].T
+        scores = ahead
     done_ref[...] = token_ref[...]
 
 
@@ -176,6 +182,11 @@
 
 def half_columns(half, h, heads):
     return pl.ds(pl.multiple_of((half * heads + h) * DH, DH), DH)
+
+
+def half_copy(half, buf, ref, sem):
+    width = buf.shape[1]
+    return pltpu.make_async_copy(buf, ref.at[:, pl.ds(pl.multiple_of(half * width, width), width)], sem)
 
 
 def mid_kernel(half_of, roles, keep, merge, me_ref, q_ref, qt_ref, g_ref, intra_ref, token_ref, *refs):
@@ -199,21 +210,33 @@
     @on(me_ref[0], roles)
     def _():
         half = half_of(me_ref[0])
-        for h in range(heads):
-            cols = half_columns(half, h, heads)
+        cols = [half_columns(half, h, heads) for h in range(heads)]
+
+        def mixed_of(h):
             earlier = total(e_refs, head(h))
             earlier_ref[head(h), :] = earlier
-            mixed = intra_ref[:, cols] + dot_nn(q_ref[:, cols], earlier)
-            g = g_ref[:, cols].astype(F32)
-            inverse = lax.rsqrt(jnp.mean(mixed * mixed, axis=-1, keepdims=True) + norm_eps)
-            along = jnp.mean(g * mixed, axis=-1, keepdims=True) * inverse
-            normed = mixed * inverse
-            grad = (inverse * (g - normed * along)).astype(BF16)
-            grad_ref[:, head(h)] = grad
-            state = dot_nn(qt_ref[cols, :], grad).astype(BF16)
+            return intra_ref[:, cols[h]] + dot_nn(q_ref[:, cols[h]], earlier)
+
+        def put_state(h, grad):
+            state = dot_nn(qt_ref[cols[h], :], grad).astype(BF16)
             for ref in state_refs:
                 ref[head(h), :] = state
+
+        mixed, last = mixed_of(0), None
+        for h in range(heads):
+            ahead = mixed_of(h + 1) if h + 1 < heads else None
+            g = g_ref[:, cols[h]].astype(F32)
+            squares = jnp.mean(mixed * mixed, axis=-1, keepdims=True)
+            along = jnp.mean(g * mixed, axis=-1, keepdims=True)
+            if h:
+                put_state(h - 1, last)
+            inverse = lax.rsqrt(squares + norm_eps)
+            normed = mixed * inverse
+            last = (inverse * (g - normed * (along * inverse))).astype(BF16)
+            grad_ref[:, head(h)] = last
             normed_ref[:, head(h)] = normed.astype(BF16)
+            mixed = ahead
+        put_state(heads - 1, last)
 
 
 def mid(half_of, roles, me, shared, token, earlier, keep=(), other=()):
@@ -245,40 +268,38 @@
             value = jnp.where(among(me_ref[0], roles), refs[3 + index][place], value)
         return value
 
-    copies = []
+    n_buf[...] = chosen(0, (slice(None), slice(None)))
+    normed_copy = half_copy(half, n_buf, normed_ref, n_sem)
+    normed_copy.start()
     for h in range(heads):
         cols = half_columns(half, h, heads)
-        n_buf[h] = chosen(0, (slice(None), head(h)))
-        copies.append(pltpu.make_async_copy(n_buf.at[h], normed_ref.at[:, cols], n_sem.at[h]))
-        copies[-1].start()
         q, k, v = (ref[:, cols] for ref in (q_ref, k_ref, v_ref))
         grad = chosen(1, (slice(None), head(h)))
         earlier = chosen(2, (head(h), slice(None)))
         scores_t = jnp.where(mask_t, dot_nt(k, q), 0.0).astype(BF16)
         grad_scores = jnp.where(mask, dot_nt(grad, v), 0.0).astype(BF16)
         grad_scores_t = jnp.where(mask_t, dot_nt(v, grad), 0.0).astype(BF16)
-        gq_buf[h] = (dot_nn(grad_scores, k) + dot_nt(grad, earlier)).astype(BF16)
-        copies.append(pltpu.make_async_copy(gq_buf.at[h], gq_ref.at[:, cols], gq_sem.at[h]))
-        copies[-1].start()
+        gq_buf[:, head(h)] = (dot_nn(grad_scores, k) + dot_nt(grad, earlier)).astype(BF16)
         gk_ref[:, head(h)] = dot_nn(grad_scores_t, q)
         gv_ref[:, head(h)] = dot_nn(scores_t, grad)
     done_ref[...] = token_ref[...]
-    for copy in copies:
-        copy.wait()
+    gq_copy = half_copy(half, gq_buf, gq_ref, gq_sem)
+    gq_copy.start()
+    normed_copy.wait()
+    gq_copy.wait()
 
 
 def back(half_of, roles, me, q, k, v, token, sets, filled=()):
     length, width = q.shape
-    heads = width // (2 * DH)
     whole = jax.ShapeDtypeStruct(q.shape, BF16)
     half_shape = jax.ShapeDtypeStruct((length, width // 2), F32)
     first = 5 + 3 * len(sets)
-    buffers = pltpu.VMEM((heads, length, DH), BF16)
+    buffers = pltpu.VMEM((length, width // 2), BF16)
     return pl.pallas_call(
         functools.partial(back_kernel, half_of, roles, len(sets)),
         in_specs=[SMEM_SPEC] + [VMEM_SPEC] * (first - 1) + [HBM_SPEC] * len(filled),
         out_specs=(HBM_SPEC, HBM_SPEC, VMEM_SPEC, VMEM_SPEC, VMEM_SPEC),
-        scratch_shapes=[buffers, buffers] + [pltpu.SemaphoreType.DMA((heads,))] * 2,
+        scratch_shapes=[buffers, buffers] + [pltpu.SemaphoreType.DMA] * 2,
         input_output_aliases={first: 0, first + 1: 1} if filled else {},
         **params("back", (whole, whole, half_shape, half_shape, TOKEN)),
     )(me, q, k, v, token, *(x for one in sets for x in one), *filled)
@@ -293,30 +314,30 @@
     l_refs, (gk_ref, gv_ref, gk_buf, gv_buf, gk_sem, gv_sem) = refs[:parts], refs[-6:]
     heads = gk_in_ref.shape[1] // DH
     half = half_of(me_ref[0])
-    copies = []
+    laters = [total(l_refs, head(h)) for h in range(heads)]
     for h in range(heads):
-        cols = half_columns(half, h, heads)
-        later = total(l_refs, head(h))
-        gk_buf[h] = (gk_in_ref[:, head(h)] + dot_nt(v_ref[:, cols], later)).astype(BF16)
-        copies.append(pltpu.make_async_copy(gk_buf.at[h], gk_ref.at[:, cols], gk_sem.at[h]))
-        copies[-1].start()
-        gv_buf[h] = (gv_in_ref[:, head(h)] + dot_nn(k_ref[:, cols], later)).astype(BF16)
-        copies.append(pltpu.make_async_copy(gv_buf.at[h], gv_ref.at[:, cols], gv_sem.at[h]))
-        copies[-1].start()
-    for copy in copies:
-        copy.wait()
+        v = v_ref[:, half_columns(half, h, heads)]
+        gk_buf[:, head(h)] = (gk_in_ref[:, head(h)] + dot_nt(v, laters[h])).astype(BF16)
+    gk_copy = half_copy(half, gk_buf, gk_ref, gk_sem)
+    gk_copy.start()
+    for h in range(heads):
+        k = k_ref[:, half_columns(half, h, heads)]
+        gv_buf[:, head(h)] = (gv_in_ref[:, head(h)] + dot_nn(k, laters[h])).astype(BF16)
+    gv_copy = half_copy(half, gv_buf, gv_ref, gv_sem)
+    gv_copy.start()
+    gk_copy.wait()
+    gv_copy.wait()
 
 
 def post(half_of, me, k, v, gk_in, gv_in, token, later, filled=()):
     length, width = k.shape
-    heads = width // (2 * DH)
     first = 6 + len(later)
     whole = jax.ShapeDtypeStruct(k.shape, BF16)
     return pl.pallas_call(
         functools.partial(post_kernel if filled else post_first_kernel, half_of, len(later)),
         in_specs=[SMEM_SPEC] + [VMEM_SPEC] * (first - 1) + [HBM_SPEC] * len(filled),
         out_specs=(HBM_SPEC, HBM_SPEC) if filled else (HBM_SPEC, HBM_SPEC, VMEM_SPEC),
-        scratch_shapes=[pltpu.VMEM((heads, length, DH), BF16)] * 2 + [pltpu.SemaphoreType.DMA((heads,))] * 2,
+        scratch_shapes=[pltpu.VMEM((length, width // 2), BF16)] * 2 + [pltpu.SemaphoreType.DMA] * 2,
         input_output_aliases={first: 0, first + 1: 1} if filled else {},
         **params("post", (whole, whole) if filled else (whole, whole, TOKEN)),
     )(me, k, v, gk_in, gv_in, token, *later, *filled)

time: 36 us -> 35.3 us (0.981)
  Pallas kernels: 14 us -> 12.9 us
  waiting for transfers between devices: 3.85 us -> 4.68 us
    ppermute x11, waiting for transfers between devices: 3.85 us -> 4.68 us  [send(): return lax.ppermute(x, 'ctx', pairs)]
    pallas_call x4, Pallas kernels: 2.4 us -> 1.63 us  [mid(): pl.pallas_call(functools.partial(mid_kernel, half_of, roles, keep, merge)...]
    pallas_call x1, Pallas kernels: 1.68 us -> 1.2 us  [intra(): pl.pallas_call(intra_kernel, in_specs=[VMEM_SPEC] * 4, out_specs=(VMEM_SP...]
  transfers between devices with their start and end apart: 11 -> 11, of which waited for: 3 -> 4; matrix products, arithmetic and copies ran while one was open for 0% -> 0% of each run, Pallas kernels for 31% -> 28%
where the time goes in v5:
time: 35.3 us; the launch traced here: 35 us
  starting transfers between devices  16.5 us (47%)
  Pallas kernels  12.9 us (37%)
  waiting for transfers between devices  4.68 us (13%)
  between operations  0.98 us (3%)
    ppermute x11, starting transfers between devices, send(): return lax.ppermute(x, 'ctx', pairs)  16.5 us
    pallas_call x2, Pallas kernels, back(): pl.pallas_call(functools.partial(back_kernel, half_of, roles, len(sets)),...  5.24 us
    ppermute x11, waiting for transfers between devices, send(): return lax.ppermute(x, 'ctx', pairs)  4.68 us
    pallas_call x2, Pallas kernels, post(): pl.pallas_call(functools.partial(post_kernel if filled else post_first_ke...  2.25 us
    pallas_call x1, Pallas kernels, states(): pl.pallas_call(functools.partial(state_kernel, plan), in_specs=[SMEM_SPEC...  1.95 us
    pallas_call x4, Pallas kernels, mid(): pl.pallas_call(functools.partial(mid_kernel, half_of, roles, keep, merge)...  1.63 us
    pallas_call x1, Pallas kernels, intra(): pl.pallas_call(intra_kernel, in_specs=[VMEM_SPEC] * 4, out_specs=(VMEM_SP...  1.2 us
  transfers between devices with their start and end apart: 11, of which 4 were waited for; matrix products, arithmetic and copies ran while one was open for 0% of the time, Pallas kernels for 28%

profile of v5, /device:TPU:0, one launch (start us, length us, event | category | flops | bytes accessed | tf_op | source)
XLA Modules:
  0.0 35.0 jit_solution(7994650355666278913)
XLA Ops:
  0.7 1.9 %states.1 = (bf16[512,128]{1,0:T(8,128)(2,1)S(1)}, f32[8,128]{1,0:T(8,128)S(1)}) custom-call(s32[1]{0:T(128)} %bitcast.me_ref.refs_0_, bf16[320,1024]{1,0:T(8,128)(2,1)} %bitcast.9, bf16[320,1024]{1,0:T(8,128)(2,1)} %bitcast.18, f32[8,128]{1,0:T(8,128)S(1)} %broadcast_in_dim.3.token_ref), custom_call_target="tpu_custom_call" | custom-call | bytes 4096 | tf_op jit(solution)/shard_map/states/pallas_call | solution.py:124
  2.6 3.2 %collective-permute-start = (bf16[512,128]{1,0:T(8,128)(2,1)S(1)}, bf16[512,128]{1,0:T(8,128)(2,1)S(1)}, u32[]{:S(2)}, u32[]{:S(2)}) collective-permute-start(bf16[512,128]{1,0:T(8,128)(2,1)S(1)} %get-tuple-element.71), channel_id=1, source_target_pairs={{0,4},{1,5},{2,6},{3,7},{16,20},{17,21},{18,22},{19,23}} | collective-permute-start | bytes 393224 | tf_op jit(solution)/shard_map/ppermute | solution.py:365
  5.9 0.3 near_states.3
  6.2 0.7 %collective-permute-start.1 = (bf16[512,128]{1,0:T(8,128)(2,1)S(1)}, bf16[512,128]{1,0:T(8,128)(2,1)S(1)}, u32[]{:S(2)}, u32[]{:S(2)}) collective-permute-start(bf16[512,128]{1,0:T(8,128)(2,1)S(1)} %get-tuple-element.66.refs_0_), channel_id=1, source_target_pairs={{4,8},{5,9},{6,10},{7,11},{20,24},{21,25},{22,26},{23,27}} | collective-permute-start | bytes 393224 | tf_op jit(solution)/shard_map/ppermute | solution.py:365
  6.9 2.7 %collective-permute-start.2 = (bf16[512,128]{1,0:T(8,128)(2,1)S(1)}, bf16[512,128]{1,0:T(8,128)(2,1)S(1)}, u32[]{:S(2)}, u32[]{:S(2)}) collective-permute-start(bf16[512,128]{1,0:T(8,128)(2,1)S(1)} %get-tuple-element.72.refs_1_), channel_id=1, source_target_pairs={{0,8},{8,12},{1,9},{9,13},{2,10},{10,14},{3,11},{11,15},{16,24},{2... | collective-permute-start | bytes 393224 | tf_op jit(solution)/shard_map/ppermute | solution.py:365
  9.7 1.2 %intra.1 = (f32[320,1024]{1,0:T(8,128)S(1)}, bf16[1024,320]{1,0:T(8,128)(2,1)S(1)}, f32[8,128]{1,0:T(8,128)S(1)}) custom-call(bf16[320,1024]{1,0:T(8,128)(2,1)S(1)} %bitcast.27, bf16[320,1024]{1,0:T(8,128)(2,1)S(1)} %bitcast.12, bf16[320,1024]{1,0:T(8,128)(2,1)S(1)} %bitcast.21, f32[8,128]{1,0:T(8,128)S(1)} %get-tuple-element.67.token_ref), custom_call_target="tpu_custom_call" | custom-call | bytes 4096 | tf_op jit(solution)/shard_map/intra/pallas_call | solution.py:154
  10.9 0.8 %collective-permute-start.3 = (bf16[512,128]{1,0:T(8,128)(2,1)S(1)}, bf16[512,128]{1,0:T(8,128)(2,1)S(1)}, u32[]{:S(2)}, u32[]{:S(2)}) collective-permute-start(bf16[512,128]{1,0:T(8,128)(2,1)S(1)} %get-tuple-element.74.refs_0_), channel_id=1, source_target_pairs={{4,12},{5,13},{6,14},{7,15},{20,28},{21,29},{22,30},{23,31}} | collective-permute-start | bytes 393224 | tf_op jit(solution)/shard_map/ppermute | solution.py:365
  11.8 3.2 %collective-permute-start.4 = (bf16[512,128]{1,0:T(8,128)(2,1)S(1)}, bf16[512,128]{1,0:T(8,128)(2,1)S(1)}, u32[]{:S(2)}, u32[]{:S(2)}) collective-permute-start(bf16[512,128]{1,0:T(8,128)(2,1)S(1)} %get-tuple-element.83), channel_id=1, source_target_pairs={{0,4},{4,8},{1,5},{5,9},{2,6},{6,10},{3,7},{7,11},{16,20},{20,24},... | collective-permute-start | bytes 393224 | tf_op jit(solution)/shard_map/ppermute | solution.py:365
  15.1 0.7 %collective-permute-start.5 = (bf16[512,128]{1,0:T(8,128)(2,1)S(1)}, bf16[512,128]{1,0:T(8,128)(2,1)S(1)}, u32[]{:S(2)}, u32[]{:S(2)}) collective-permute-start(bf16[512,128]{1,0:T(8,128)(2,1)S(1)} %get-tuple-element.86), channel_id=1, source_target_pairs={{8,12},{9,13},{10,14},{11,15},{24,28},{25,29},{26,30},{27,31}} | collective-permute-start | bytes 393224 | tf_op jit(solution)/shard_map/ppermute | solution.py:365
  15.7 0.8 %mid.4 = (bf16[320,512]{1,0:T(8,128)(2,1)S(1)}, bf16[320,512]{1,0:T(8,128)(2,1)S(1)}, bf16[512,128]{1,0:T(8,128)(2,1)S(1)}, f32[8,128]{1,0:T(8,128)S(1)}, bf16[512,128]{1,0:T(8,128)(2,1)S(1)}) custom-call(s32[1]{0:T(128)} %bitcast.me_ref.refs_0_, bf16[320,1024]{1,0:T(8,128)(2,1)S(1)} %bitcast.28, bf16[1024,320]{1,0:T(8,128)(2,1)S(1)} %get-tuple-element.68.qt_ref, ...), custom_call_target="tpu_custom_call" | custom-call | bytes 4096 | tf_op jit(solution)/shard_map/mid/pallas_call | solution.py:247
  16.6 0.7 %collective-permute-start.6 = (bf16[512,128]{1,0:T(8,128)(2,1)S(1)}, bf16[512,128]{1,0:T(8,128)(2,1)S(1)}, u32[]{:S(2)}, u32[]{:S(2)}) collective-permute-start(bf16[512,128]{1,0:T(8,128)(2,1)S(1)} %get-tuple-element.95), channel_id=1, source_target_pairs={{12,8},{8,4},{13,9},{9,5},{14,10},{10,6},{15,11},{11,7},{28,24},{2... | collective-permute-start | bytes 393224 | tf_op jit(solution)/shard_map/ppermute | solution.py:365
  17.3 0.2 collective-permute-done.4.refs_0_
  17.4 0.8 %mid.6 = (bf16[320,512]{1,0:T(8,128)(2,1)S(1)}, bf16[320,512]{1,0:T(8,128)(2,1)S(1)}, bf16[512,128]{1,0:T(8,128)(2,1)S(1)}, f32[8,128]{1,0:T(8,128)S(1)}, bf16[512,128]{1,0:T(8,128)(2,1)S(1)}) custom-call(s32[1]{0:T(128)} %bitcast.me_ref.refs_0_, bf16[320,1024]{1,0:T(8,128)(2,1)S(1)} %bitcast.30, bf16[1024,320]{1,0:T(8,128)(2,1)S(1)} %get-tuple-element.68.qt_ref, ...), custom_call_target="tpu_custom_call" | custom-call | bytes 4096 | tf_op jit(solution)/shard_map/mid/pallas_call | solution.py:247
  18.3 1.3 %collective-permute-start.7 = (bf16[512,128]{1,0:T(8,128)(2,1)S(1)}, bf16[512,128]{1,0:T(8,128)(2,1)S(1)}, u32[]{:S(2)}, u32[]{:S(2)}) collective-permute-start(bf16[512,128]{1,0:T(8,128)(2,1)S(1)} %get-tuple-element.98), channel_id=1, source_target_pairs={{12,4},{4,0},{13,5},{5,1},{14,6},{6,2},{15,7},{7,3},{28,20},{20,16... | collective-permute-start | bytes 393224 | tf_op jit(solution)/shard_map/ppermute | solution.py:365
  19.6 2.6 %back.2 = (bf16[320,1024]{1,0:T(8,128)(2,1)}, bf16[320,1024]{1,0:T(8,128)(2,1)}, f32[320,512]{1,0:T(8,128)S(1)}, f32[320,512]{1,0:T(8,128)S(1)}, f32[8,128]{1,0:T(8,128)S(1)}) custom-call(s32[1]{0:T(128)} %bitcast.me_ref.refs_0_, bf16[320,1024]{1,0:T(8,128)(2,1)S(1)} %bitcast.32, bf16[320,1024]{1,0:T(8,128)(2,1)S(1)} %bitcast.14, ...), custom_call_target="tpu_custom_call" | custom-call | bytes 4096 | tf_op jit(solution)/shard_map/back/pallas_call | solution.py:298
  22.3 1.3 %collective-permute-start.8 = (bf16[512,128]{1,0:T(8,128)(2,1)S(1)}, bf16[512,128]{1,0:T(8,128)(2,1)S(1)}, u32[]{:S(2)}, u32[]{:S(2)}) collective-permute-start(bf16[512,128]{1,0:T(8,128)(2,1)S(1)} %get-tuple-element.115), channel_id=1, source_target_pairs={{8,0},{9,1},{10,2},{11,3},{24,16},{25,17},{26,18},{27,19}} | collective-permute-start | bytes 393224 | tf_op jit(solution)/shard_map/ppermute | solution.py:365
  23.6 0.7 %collective-permute-start.9 = (bf16[512,128]{1,0:T(8,128)(2,1)S(1)}, bf16[512,128]{1,0:T(8,128)(2,1)S(1)}, u32[]{:S(2)}, u32[]{:S(2)}) collective-permute-start(bf16[512,128]{1,0:T(8,128)(2,1)S(1)} %get-tuple-element.115), channel_id=1, source_target_pairs={{12,8},{8,4},{13,9},{9,5},{14,10},{10,6},{15,11},{11,7},{28,24},{2... | collective-permute-start | bytes 393224 | tf_op jit(solution)/shard_map/ppermute | solution.py:365
  24.2 1.9 %collective-permute-done.7.refs_1_.refs_7_ = bf16[512,128]{1,0:T(8,128)(2,1)S(1)} collective-permute-done((bf16[512,128]{1,0:T(8,128)(2,1)S(1)}, bf16[512,128]{1,0:T(8,128)(2,1)S(1)}, u32[]{:S(2)}, u32[]{:S(2)}) %collective-permute-start.7) | collective-permute-done | bytes 131104 | tf_op jit(solution)/shard_map/ppermute | solution.py:365
  26.2 1.3 %collective-permute-start.10 = (bf16[512,128]{1,0:T(8,128)(2,1)S(1)}, bf16[512,128]{1,0:T(8,128)(2,1)S(1)}, u32[]{:S(2)}, u32[]{:S(2)}) collective-permute-start(bf16[512,128]{1,0:T(8,128)(2,1)S(1)} %get-tuple-element.119), channel_id=1, source_target_pairs={{4,0},{5,1},{6,2},{7,3},{20,16},{21,17},{22,18},{23,19}} | collective-permute-start | bytes 393224 | tf_op jit(solution)/shard_map/ppermute | solution.py:365
  27.5 2.6 %back.3 = (bf16[320,1024]{1,0:T(8,128)(2,1)}, bf16[320,1024]{1,0:T(8,128)(2,1)}, f32[320,512]{1,0:T(8,128)S(1)}, f32[320,512]{1,0:T(8,128)S(1)}, f32[8,128]{1,0:T(8,128)S(1)}) custom-call(s32[1]{0:T(128)} %bitcast.me_ref.refs_0_, bf16[320,1024]{1,0:T(8,128)(2,1)S(1)} %bitcast.33, ...), custom_call_target="tpu_custom_call", output_to_operand_aliasing={{0}: (11, {}), {1}: (12, {})} | custom-call | bytes 4096 | tf_op jit(solution)/shard_map/back/pallas_call | solution.py:298
  30.1 1.5 %collective-permute-done.8.refs_8_ = bf16[512,128]{1,0:T(8,128)(2,1)S(1)} collective-permute-done((bf16[512,128]{1,0:T(8,128)(2,1)S(1)}, bf16[512,128]{1,0:T(8,128)(2,1)S(1)}, u32[]{:S(2)}, u32[]{:S(2)}) %collective-permute-start.8) | collective-permute-done | bytes 131104 | tf_op jit(solution)/shard_map/ppermute | solution.py:365
  31.7 1.1 %post.2 = (bf16[320,1024]{1,0:T(8,128)(2,1)}, bf16[320,1024]{1,0:T(8,128)(2,1)}, f32[8,128]{1,0:T(8,128)S(1)}) custom-call(s32[1]{0:T(128)} %bitcast.me_ref.refs_0_, bf16[320,1024]{1,0:T(8,128)(2,1)S(1)} %bitcast.16, bf16[320,1024]{1,0:T(8,128)(2,1)S(1)} %bitcast.25, f32[320,512]{1,0:T(8,128)S(1)} %get-tuple-element.112.refs_3_, ...), custom_call_target="tpu_custom_call" | custom-call | bytes 4096 | tf_op jit(solution)/shard_map/post/pallas_call | solution.py:336
  32.8 1.0 %collective-permute-done.10.refs_1_ = bf16[512,128]{1,0:T(8,128)(2,1)S(1)} collective-permute-done((bf16[512,128]{1,0:T(8,128)(2,1)S(1)}, bf16[512,128]{1,0:T(8,128)(2,1)S(1)}, u32[]{:S(2)}, u32[]{:S(2)}) %collective-permute-start.10) | collective-permute-done | bytes 131104 | tf_op jit(solution)/shard_map/ppermute | solution.py:365
  33.9 1.1 %post.3 = (bf16[320,1024]{1,0:T(8,128)(2,1)}, bf16[320,1024]{1,0:T(8,128)(2,1)}) custom-call(s32[1]{0:T(128)} %bitcast.me_ref.refs_0_, bf16[320,1024]{1,0:T(8,128)(2,1)S(1)} %bitcast.17, bf16[320,1024]{1,0:T(8,128)(2,1)S(1)} %bitcast.26, f32[320,512]{1,0:T(8,128)S(1)} %get-tuple-element.110.gk_in_ref, ...), custom_call_target="tpu_custom_call", output_to_operand_aliasing={{0}: (8, {}), {1}: (9, {})} | custom-call | bytes 4096 | tf_op jit(solution)/shard_map/post/pallas_call | solution.py:336
  (26 shorter events, 0.4 us)
Async XLA Ops:
  0.6 5.2 %copy-start.1 = (bf16[1,320,1024]{2,1,0:T(8,128)(2,1)S(1)}, bf16[1,320,1024]{2,1,0:T(8,128)(2,1)}, u32[]{:S(2)}) copy-start(bf16[1,320,1024]{2,1,0:T(8,128)(2,1)} %param.6) | copy-start | bytes 1966084
  0.6 5.2 %copy-start = (bf16[1,320,1024]{2,1,0:T(8,128)(2,1)S(1)}, bf16[1,320,1024]{2,1,0:T(8,128)(2,1)}, u32[]{:S(2)}) copy-start(bf16[1,320,1024]{2,1,0:T(8,128)(2,1)} %param.5) | copy-start | bytes 1966084
  2.6 8.3 %collective-permute-start = (bf16[512,128]{1,0:T(8,128)(2,1)S(1)}, bf16[512,128]{1,0:T(8,128)(2,1)S(1)}, u32[]{:S(2)}, u32[]{:S(2)}) collective-permute-start(bf16[512,128]{1,0:T(8,128)(2,1)S(1)} %get-tuple-element.71), channel_id=1, source_target_pairs={{0,4},{1,5},{2,6},{3,7},{16,20},{17,21},{18,22},{19,23}} | collective-permute-start | bytes 393224 | tf_op jit(solution)/shard_map/ppermute | solution.py:365
  5.9 3.8 %copy-start.2 = (bf16[1,320,1024]{2,1,0:T(8,128)(2,1)S(1)}, bf16[1,320,1024]{2,1,0:T(8,128)(2,1)}, u32[]{:S(2)}) copy-start(bf16[1,320,1024]{2,1,0:T(8,128)(2,1)} %param.4) | copy-start | bytes 1966084
  6.2 8.7 %collective-permute-start.1 = (bf16[512,128]{1,0:T(8,128)(2,1)S(1)}, bf16[512,128]{1,0:T(8,128)(2,1)S(1)}, u32[]{:S(2)}, u32[]{:S(2)}) collective-permute-start(bf16[512,128]{1,0:T(8,128)(2,1)S(1)} %get-tuple-element.66.refs_0_), channel_id=1, source_target_pairs={{4,8},{5,9},{6,10},{7,11},{20,24},{21,25},{22,26},{23,27}} | collective-permute-start | bytes 393224 | tf_op jit(solution)/shard_map/ppermute | solution.py:365
  6.9 8.1 %collective-permute-start.2 = (bf16[512,128]{1,0:T(8,128)(2,1)S(1)}, bf16[512,128]{1,0:T(8,128)(2,1)S(1)}, u32[]{:S(2)}, u32[]{:S(2)}) collective-permute-start(bf16[512,128]{1,0:T(8,128)(2,1)S(1)} %get-tuple-element.72.refs_1_), channel_id=1, source_target_pairs={{0,8},{8,12},{1,9},{9,13},{2,10},{10,14},{3,11},{11,15},{16,24},{2... | collective-permute-start | bytes 393224 | tf_op jit(solution)/shard_map/ppermute | solution.py:365
  10.9 4.9 %copy-start.3 = (bf16[1,320,1024]{2,1,0:T(8,128)(2,1)S(1)}, bf16[1,320,1024]{2,1,0:T(8,128)(2,1)}, u32[]{:S(2)}) copy-start(bf16[1,320,1024]{2,1,0:T(8,128)(2,1)} %param.7) | copy-start | bytes 1966084
  10.9 5.6 %collective-permute-start.3 = (bf16[512,128]{1,0:T(8,128)(2,1)S(1)}, bf16[512,128]{1,0:T(8,128)(2,1)S(1)}, u32[]{:S(2)}, u32[]{:S(2)}) collective-permute-start(bf16[512,128]{1,0:T(8,128)(2,1)S(1)} %get-tuple-element.74.refs_0_), channel_id=1, source_target_pairs={{4,12},{5,13},{6,14},{7,15},{20,28},{21,29},{22,30},{23,31}} | collective-permute-start | bytes 393224 | tf_op jit(solution)/shard_map/ppermute | solution.py:365
  11.8 5.7 %collective-permute-start.4 = (bf16[512,128]{1,0:T(8,128)(2,1)S(1)}, bf16[512,128]{1,0:T(8,128)(2,1)S(1)}, u32[]{:S(2)}, u32[]{:S(2)}) collective-permute-start(bf16[512,128]{1,0:T(8,128)(2,1)S(1)} %get-tuple-element.83), channel_id=1, source_target_pairs={{0,4},{4,8},{1,5},{5,9},{2,6},{6,10},{3,7},{7,11},{16,20},{20,24},... | collective-permute-start | bytes 393224 | tf_op jit(solution)/shard_map/ppermute | solution.py:365
  15.1 3.2 %collective-permute-start.5 = (bf16[512,128]{1,0:T(8,128)(2,1)S(1)}, bf16[512,128]{1,0:T(8,128)(2,1)S(1)}, u32[]{:S(2)}, u32[]{:S(2)}) collective-permute-start(bf16[512,128]{1,0:T(8,128)(2,1)S(1)} %get-tuple-element.86), channel_id=1, source_target_pairs={{8,12},{9,13},{10,14},{11,15},{24,28},{25,29},{26,30},{27,31}} | collective-permute-start | bytes 393224 | tf_op jit(solution)/shard_map/ppermute | solution.py:365
  16.6 5.6 %collective-permute-start.6 = (bf16[512,128]{1,0:T(8,128)(2,1)S(1)}, bf16[512,128]{1,0:T(8,128)(2,1)S(1)}, u32[]{:S(2)}, u32[]{:S(2)}) collective-permute-start(bf16[512,128]{1,0:T(8,128)(2,1)S(1)} %get-tuple-element.95), channel_id=1, source_target_pairs={{12,8},{8,4},{13,9},{9,5},{14,10},{10,6},{15,11},{11,7},{28,24},{2... | collective-permute-start | bytes 393224 | tf_op jit(solution)/shard_map/ppermute | solution.py:365
  18.3 7.9 %collective-permute-start.7 = (bf16[512,128]{1,0:T(8,128)(2,1)S(1)}, bf16[512,128]{1,0:T(8,128)(2,1)S(1)}, u32[]{:S(2)}, u32[]{:S(2)}) collective-permute-start(bf16[512,128]{1,0:T(8,128)(2,1)S(1)} %get-tuple-element.98), channel_id=1, source_target_pairs={{12,4},{4,0},{13,5},{5,1},{14,6},{6,2},{15,7},{7,3},{28,20},{20,16... | collective-permute-start | bytes 393224 | tf_op jit(solution)/shard_map/ppermute | solution.py:365
  22.3 9.4 %collective-permute-start.8 = (bf16[512,128]{1,0:T(8,128)(2,1)S(1)}, bf16[512,128]{1,0:T(8,128)(2,1)S(1)}, u32[]{:S(2)}, u32[]{:S(2)}) collective-permute-start(bf16[512,128]{1,0:T(8,128)(2,1)S(1)} %get-tuple-element.115), channel_id=1, source_target_pairs={{8,0},{9,1},{10,2},{11,3},{24,16},{25,17},{26,18},{27,19}} | collective-permute-start | bytes 393224 | tf_op jit(solution)/shard_map/ppermute | solution.py:365
  23.6 9.2 %collective-permute-start.9 = (bf16[512,128]{1,0:T(8,128)(2,1)S(1)}, bf16[512,128]{1,0:T(8,128)(2,1)S(1)}, u32[]{:S(2)}, u32[]{:S(2)}) collective-permute-start(bf16[512,128]{1,0:T(8,128)(2,1)S(1)} %get-tuple-element.115), channel_id=1, source_target_pairs={{12,8},{8,4},{13,9},{9,5},{14,10},{10,6},{15,11},{11,7},{28,24},{2... | collective-permute-start | bytes 393224 | tf_op jit(solution)/shard_map/ppermute | solution.py:365
  26.2 7.7 %collective-permute-start.10 = (bf16[512,128]{1,0:T(8,128)(2,1)S(1)}, bf16[512,128]{1,0:T(8,128)(2,1)S(1)}, u32[]{:S(2)}, u32[]{:S(2)}) collective-permute-start(bf16[512,128]{1,0:T(8,128)(2,1)S(1)} %get-tuple-element.119), channel_id=1, source_target_pairs={{4,0},{5,1},{6,2},{7,3},{20,16},{21,17},{22,18},{23,19}} | collective-permute-start | bytes 393224 | tf_op jit(solution)/shard_map/ppermute | solution.py:365

commit v6 on v5

--- a/solution.py
+++ b/solution.py
@@ -90,43 +90,35 @@
     )(me, k, v, token, *spare, *passed)
 
 
-def state_kernel(plan, me_ref, k_ref, v_ref, token_ref, *refs):
-    outs, (done_ref, k_buf, v_buf, k_sem, v_sem) = refs[:-5], refs[-5:]
-    heads = outs[0].shape[0] // DH
+def state_kernel(half, roles, me_ref, k_ref, v_ref, token_ref, out_ref, done_ref, k_buf, v_buf, k_sem, v_sem):
+    width = k_buf.shape[1]
+    heads = width // DH
     done_ref[...] = token_ref[...]
-    for roles, pieces in plan:
-
-        @on(me_ref[0], roles)
-        def _():
-            copies = []
-            for half, out in pieces:
-                for h in range(heads):
-                    cols, slot = head(half * heads + h), len(copies)
-                    pair = (
-                        pltpu.make_async_copy(k_ref.at[:, cols], k_buf.at[slot], k_sem.at[slot]),
-                        pltpu.make_async_copy(v_ref.at[:, cols], v_buf.at[slot], v_sem.at[slot]),
-                    )
-                    for copy in pair:
-                        copy.start()
-                    copies.append((outs[out], head(h), pair))
-            for slot, (out_ref, rows, pair) in enumerate(copies):
-                for copy in pair:
-                    copy.wait()
-                out_ref[rows, :] = dot_tn(k_buf[slot], v_buf[slot]).astype(BF16)
-
-
-def states(plan, me, k, v, token):
+
+    @on(me_ref[0], roles)
+    def _():
+        cols = slice(half * width, (half + 1) * width)
+        copies = (
+            pltpu.make_async_copy(k_ref.at[:, cols], k_buf, k_sem),
+            pltpu.make_async_copy(v_ref.at[:, cols], v_buf, v_sem),
+        )
+        for copy in copies:
+            copy.start()
+        for copy in copies:
+            copy.wait()
+        for h in range(heads):
+            out_ref[head(h), :] = dot_tn(k_buf[:, head(h)], v_buf[:, head(h)]).astype(BF16)
+
+
+def states(half, roles, me, k, v, token):
     length, width = k.shape
-    count = 1 + max(out for _, pieces in plan for _, out in pieces)
-    slots = max(len(pieces) for _, pieces in plan) * width // (2 * DH)
     k, v = (pltpu.with_memory_space_constraint(x, pltpu.HBM) for x in (k, v))
-    shape = jax.ShapeDtypeStruct((width // 2, DH), BF16)
-    return pl.pallas_call(
-        functools.partial(state_kernel, plan),
+    return pl.pallas_call(
+        functools.partial(state_kernel, half, roles),
         in_specs=[SMEM_SPEC, HBM_SPEC, HBM_SPEC, VMEM_SPEC],
-        out_specs=(VMEM_SPEC,) * (count + 1),
-        scratch_shapes=[pltpu.VMEM((slots, length, DH), BF16)] * 2 + [pltpu.SemaphoreType.DMA((slots,))] * 2,
-        **params("states", (shape,) * count + (TOKEN,)),
+        out_specs=(VMEM_SPEC,) * 2,
+        scratch_shapes=[pltpu.VMEM((length, width // 2), BF16)] * 2 + [pltpu.SemaphoreType.DMA] * 2,
+        **params("states", (jax.ShapeDtypeStruct((width // 2, DH), BF16), TOKEN)),
     )(me, k, v, token)
 
 
@@ -364,9 +356,9 @@
     def send(x, pairs):
         return lax.ppermute(x, "ctx", pairs)
 
-    s_a, token = states((((0,), ((0, 0),)),), me, k, v, token)
+    s_a, token = states(0, (0,), me, k, v, token)
     r_a = send(s_a, [(0, 1)])
-    s_b, token = near_states(1, (0, 1), me, k, v, token)
+    s_b, token = states(1, (0, 1), me, k, v, token)
     r_b = send(s_b, [(1, 2)])
     s_c, token = near_states(0, (1, 2), me, k, v, token, (0,), (s_b,))
     r_c = send(s_c, [(0, 2), (2, 3)])
@@ -424,7 +416,8 @@
     q, k, v, g = (rows_of(x) for x in (queries, key_vectors, value_vectors, grad_output))
     me = lax.axis_index("ctx").astype(jnp.int32).reshape(1)
     token = jnp.zeros(TOKEN.shape, TOKEN.dtype)
-    s1, s2, token = states((((), ((0, 0), (1, 1))),), me, k, v, token)
+    s1, token = near_states(0, (), me, k, v, token)
+    s2, token = near_states(1, (), me, k, v, token)
     e1, e2 = scan_states(s1, s2, count, False)
     intra_out, qt, token = intra(q, k, v, token)
     shared = (q, qt, g, intra_out)

time: 35.3 us -> 35 us (level)
  starting transfers between devices: 16.5 us -> 15.4 us
  Pallas kernels: 12.9 us -> 13.5 us
    ppermute x11, starting transfers between devices: 16.5 us -> 15.4 us  [send(): return lax.ppermute(x, 'ctx', pairs)]
    pallas_call x1 -> x2, Pallas kernels: 1.95 us -> 2.95 us  [states(): pl.pallas_call(functools.partial(state_kernel, half, roles), in_specs=[SM...]
  transfers between devices with their start and end apart: 11 -> 11, of which waited for: 4 -> 4; matrix products, arithmetic and copies ran while one was open for 0% -> 0% of each run, Pallas kernels for 28% -> 32%
where the time goes in v6:
time: 35 us; the launch traced here: 34.7 us
  starting transfers between devices  15.4 us (44%)
  Pallas kernels  13.5 us (39%)
  waiting for transfers between devices  4.67 us (13%)
  between operations  0.98 us (3%)
    ppermute x11, starting transfers between devices, send(): return lax.ppermute(x, 'ctx', pairs)  15.4 us
    pallas_call x2, Pallas kernels, back(): pl.pallas_call(functools.partial(back_kernel, half_of, roles, len(sets)),...  5.24 us
    ppermute x11, waiting for transfers between devices, send(): return lax.ppermute(x, 'ctx', pairs)  4.67 us
    pallas_call x2, Pallas kernels, states(): pl.pallas_call(functools.partial(state_kernel, half, roles), in_specs=[SM...  2.95 us
    pallas_call x2, Pallas kernels, post(): pl.pallas_call(functools.partial(post_kernel if filled else post_first_ke...  2.25 us
    pallas_call x4, Pallas kernels, mid(): pl.pallas_call(functools.partial(mid_kernel, half_of, roles, keep, merge)...  1.63 us
    pallas_call x1, Pallas kernels, intra(): pl.pallas_call(intra_kernel, in_specs=[VMEM_SPEC] * 4, out_specs=(VMEM_SP...  1.2 us
  transfers between devices with their start and end apart: 11, of which 4 were waited for; matrix products, arithmetic and copies ran while one was open for 0% of the time, Pallas kernels for 32%

profile of v6, /device:TPU:0, one launch (start us, length us, event | category | flops | bytes accessed | tf_op | source)
XLA Modules:
  0.0 34.7 jit_solution(6319361989388437395)
XLA Ops:
  0.7 1.5 %states.2 = (bf16[512,128]{1,0:T(8,128)(2,1)S(1)}, f32[8,128]{1,0:T(8,128)S(1)}) custom-call(s32[1]{0:T(128)} %bitcast.me_ref.refs_0_, bf16[320,1024]{1,0:T(8,128)(2,1)} %bitcast.9, bf16[320,1024]{1,0:T(8,128)(2,1)} %bitcast.18, f32[8,128]{1,0:T(8,128)S(1)} %broadcast_in_dim.3.token_ref), custom_call_target="tpu_custom_call" | custom-call | bytes 4096 | tf_op jit(solution)/shard_map/states/pallas_call | solution.py:116
  2.2 3.6 %collective-permute-start = (bf16[512,128]{1,0:T(8,128)(2,1)S(1)}, bf16[512,128]{1,0:T(8,128)(2,1)S(1)}, u32[]{:S(2)}, u32[]{:S(2)}) collective-permute-start(bf16[512,128]{1,0:T(8,128)(2,1)S(1)} %get-tuple-element.71), channel_id=1, source_target_pairs={{0,4},{1,5},{2,6},{3,7},{16,20},{17,21},{18,22},{19,23}} | collective-permute-start | bytes 393224 | tf_op jit(solution)/shard_map/ppermute | solution.py:357
  5.8 1.5 %states.3 = (bf16[512,128]{1,0:T(8,128)(2,1)S(1)}, f32[8,128]{1,0:T(8,128)S(1)}) custom-call(s32[1]{0:T(128)} %bitcast.me_ref.refs_0_, bf16[320,1024]{1,0:T(8,128)(2,1)} %bitcast.10, bf16[320,1024]{1,0:T(8,128)(2,1)} %bitcast.19, f32[8,128]{1,0:T(8,128)S(1)} %get-tuple-element.64.token_ref), custom_call_target="tpu_custom_call" | custom-call | bytes 4096 | tf_op jit(solution)/shard_map/states/pallas_call | solution.py:116
  7.3 0.7 %collective-permute-start.1 = (bf16[512,128]{1,0:T(8,128)(2,1)S(1)}, bf16[512,128]{1,0:T(8,128)(2,1)S(1)}, u32[]{:S(2)}, u32[]{:S(2)}) collective-permute-start(bf16[512,128]{1,0:T(8,128)(2,1)S(1)} %get-tuple-element.66.refs_0_), channel_id=1, source_target_pairs={{4,8},{5,9},{6,10},{7,11},{20,24},{21,25},{22,26},{23,27}} | collective-permute-start | bytes 393224 | tf_op jit(solution)/shard_map/ppermute | solution.py:357
  8.0 1.3 %collective-permute-start.2 = (bf16[512,128]{1,0:T(8,128)(2,1)S(1)}, bf16[512,128]{1,0:T(8,128)(2,1)S(1)}, u32[]{:S(2)}, u32[]{:S(2)}) collective-permute-start(bf16[512,128]{1,0:T(8,128)(2,1)S(1)} %get-tuple-element.72.refs_1_), channel_id=1, source_target_pairs={{0,8},{8,12},{1,9},{9,13},{2,10},{10,14},{3,11},{11,15},{16,24},{2... | collective-permute-start | bytes 393224 | tf_op jit(solution)/shard_map/ppermute | solution.py:357
  9.3 1.2 %intra.1 = (f32[320,1024]{1,0:T(8,128)S(1)}, bf16[1024,320]{1,0:T(8,128)(2,1)S(1)}, f32[8,128]{1,0:T(8,128)S(1)}) custom-call(bf16[320,1024]{1,0:T(8,128)(2,1)S(1)} %bitcast.27, bf16[320,1024]{1,0:T(8,128)(2,1)S(1)} %bitcast.12, bf16[320,1024]{1,0:T(8,128)(2,1)S(1)} %bitcast.21, f32[8,128]{1,0:T(8,128)S(1)} %get-tuple-element.67.token_ref), custom_call_target="tpu_custom_call" | custom-call | bytes 4096 | tf_op jit(solution)/shard_map/intra/pallas_call | solution.py:146
  10.6 0.8 %collective-permute-start.3 = (bf16[512,128]{1,0:T(8,128)(2,1)S(1)}, bf16[512,128]{1,0:T(8,128)(2,1)S(1)}, u32[]{:S(2)}, u32[]{:S(2)}) collective-permute-start(bf16[512,128]{1,0:T(8,128)(2,1)S(1)} %get-tuple-element.74.refs_0_), channel_id=1, source_target_pairs={{4,12},{5,13},{6,14},{7,15},{20,28},{21,29},{22,30},{23,31}} | collective-permute-start | bytes 393224 | tf_op jit(solution)/shard_map/ppermute | solution.py:357
  11.4 3.2 %collective-permute-start.4 = (bf16[512,128]{1,0:T(8,128)(2,1)S(1)}, bf16[512,128]{1,0:T(8,128)(2,1)S(1)}, u32[]{:S(2)}, u32[]{:S(2)}) collective-permute-start(bf16[512,128]{1,0:T(8,128)(2,1)S(1)} %get-tuple-element.83), channel_id=1, source_target_pairs={{0,4},{4,8},{1,5},{5,9},{2,6},{6,10},{3,7},{7,11},{16,20},{20,24},... | collective-permute-start | bytes 393224 | tf_op jit(solution)/shard_map/ppermute | solution.py:357
  14.7 0.7 %collective-permute-start.5 = (bf16[512,128]{1,0:T(8,128)(2,1)S(1)}, bf16[512,128]{1,0:T(8,128)(2,1)S(1)}, u32[]{:S(2)}, u32[]{:S(2)}) collective-permute-start(bf16[512,128]{1,0:T(8,128)(2,1)S(1)} %get-tuple-element.86), channel_id=1, source_target_pairs={{8,12},{9,13},{10,14},{11,15},{24,28},{25,29},{26,30},{27,31}} | collective-permute-start | bytes 393224 | tf_op jit(solution)/shard_map/ppermute | solution.py:357
  15.4 0.8 %mid.4 = (bf16[320,512]{1,0:T(8,128)(2,1)S(1)}, bf16[320,512]{1,0:T(8,128)(2,1)S(1)}, bf16[512,128]{1,0:T(8,128)(2,1)S(1)}, f32[8,128]{1,0:T(8,128)S(1)}, bf16[512,128]{1,0:T(8,128)(2,1)S(1)}) custom-call(s32[1]{0:T(128)} %bitcast.me_ref.refs_0_, bf16[320,1024]{1,0:T(8,128)(2,1)S(1)} %bitcast.28, bf16[1024,320]{1,0:T(8,128)(2,1)S(1)} %get-tuple-element.68.qt_ref, ...), custom_call_target="tpu_custom_call" | custom-call | bytes 4096 | tf_op jit(solution)/shard_map/mid/pallas_call | solution.py:239
  16.3 0.7 %collective-permute-start.6 = (bf16[512,128]{1,0:T(8,128)(2,1)S(1)}, bf16[512,128]{1,0:T(8,128)(2,1)S(1)}, u32[]{:S(2)}, u32[]{:S(2)}) collective-permute-start(bf16[512,128]{1,0:T(8,128)(2,1)S(1)} %get-tuple-element.95), channel_id=1, source_target_pairs={{12,8},{8,4},{13,9},{9,5},{14,10},{10,6},{15,11},{11,7},{28,24},{2... | collective-permute-start | bytes 393224 | tf_op jit(solution)/shard_map/ppermute | solution.py:357
  16.9 0.2 collective-permute-done.4.refs_0_
  17.1 0.8 %mid.6 = (bf16[320,512]{1,0:T(8,128)(2,1)S(1)}, bf16[320,512]{1,0:T(8,128)(2,1)S(1)}, bf16[512,128]{1,0:T(8,128)(2,1)S(1)}, f32[8,128]{1,0:T(8,128)S(1)}, bf16[512,128]{1,0:T(8,128)(2,1)S(1)}) custom-call(s32[1]{0:T(128)} %bitcast.me_ref.refs_0_, bf16[320,1024]{1,0:T(8,128)(2,1)S(1)} %bitcast.30, bf16[1024,320]{1,0:T(8,128)(2,1)S(1)} %get-tuple-element.68.qt_ref, ...), custom_call_target="tpu_custom_call" | custom-call | bytes 4096 | tf_op jit(solution)/shard_map/mid/pallas_call | solution.py:239
  17.9 1.3 %collective-permute-start.7 = (bf16[512,128]{1,0:T(8,128)(2,1)S(1)}, bf16[512,128]{1,0:T(8,128)(2,1)S(1)}, u32[]{:S(2)}, u32[]{:S(2)}) collective-permute-start(bf16[512,128]{1,0:T(8,128)(2,1)S(1)} %get-tuple-element.98), channel_id=1, source_target_pairs={{12,4},{4,0},{13,5},{5,1},{14,6},{6,2},{15,7},{7,3},{28,20},{20,16... | collective-permute-start | bytes 393224 | tf_op jit(solution)/shard_map/ppermute | solution.py:357
  19.2 2.6 %back.2 = (bf16[320,1024]{1,0:T(8,128)(2,1)}, bf16[320,1024]{1,0:T(8,128)(2,1)}, f32[320,512]{1,0:T(8,128)S(1)}, f32[320,512]{1,0:T(8,128)S(1)}, f32[8,128]{1,0:T(8,128)S(1)}) custom-call(s32[1]{0:T(128)} %bitcast.me_ref.refs_0_, bf16[320,1024]{1,0:T(8,128)(2,1)S(1)} %bitcast.32, bf16[320,1024]{1,0:T(8,128)(2,1)S(1)} %bitcast.14, ...), custom_call_target="tpu_custom_call" | custom-call | bytes 4096 | tf_op jit(solution)/shard_map/back/pallas_call | solution.py:290
  21.9 1.3 %collective-permute-start.8 = (bf16[512,128]{1,0:T(8,128)(2,1)S(1)}, bf16[512,128]{1,0:T(8,128)(2,1)S(1)}, u32[]{:S(2)}, u32[]{:S(2)}) collective-permute-start(bf16[512,128]{1,0:T(8,128)(2,1)S(1)} %get-tuple-element.115), channel_id=1, source_target_pairs={{8,0},{9,1},{10,2},{11,3},{24,16},{25,17},{26,18},{27,19}} | collective-permute-start | bytes 393224 | tf_op jit(solution)/shard_map/ppermute | solution.py:357
  23.2 0.7 %collective-permute-start.9 = (bf16[512,128]{1,0:T(8,128)(2,1)S(1)}, bf16[512,128]{1,0:T(8,128)(2,1)S(1)}, u32[]{:S(2)}, u32[]{:S(2)}) collective-permute-start(bf16[512,128]{1,0:T(8,128)(2,1)S(1)} %get-tuple-element.115), channel_id=1, source_target_pairs={{12,8},{8,4},{13,9},{9,5},{14,10},{10,6},{15,11},{11,7},{28,24},{2... | collective-permute-start | bytes 393224 | tf_op jit(solution)/shard_map/ppermute | solution.py:357
  23.9 1.9 %collective-permute-done.7.refs_1_.refs_7_ = bf16[512,128]{1,0:T(8,128)(2,1)S(1)} collective-permute-done((bf16[512,128]{1,0:T(8,128)(2,1)S(1)}, bf16[512,128]{1,0:T(8,128)(2,1)S(1)}, u32[]{:S(2)}, u32[]{:S(2)}) %collective-permute-start.7) | collective-permute-done | bytes 131104 | tf_op jit(solution)/shard_map/ppermute | solution.py:357
  25.9 1.3 %collective-permute-start.10 = (bf16[512,128]{1,0:T(8,128)(2,1)S(1)}, bf16[512,128]{1,0:T(8,128)(2,1)S(1)}, u32[]{:S(2)}, u32[]{:S(2)}) collective-permute-start(bf16[512,128]{1,0:T(8,128)(2,1)S(1)} %get-tuple-element.119), channel_id=1, source_target_pairs={{4,0},{5,1},{6,2},{7,3},{20,16},{21,17},{22,18},{23,19}} | collective-permute-start | bytes 393224 | tf_op jit(solution)/shard_map/ppermute | solution.py:357
  27.2 2.6 %back.3 = (bf16[320,1024]{1,0:T(8,128)(2,1)}, bf16[320,1024]{1,0:T(8,128)(2,1)}, f32[320,512]{1,0:T(8,128)S(1)}, f32[320,512]{1,0:T(8,128)S(1)}, f32[8,128]{1,0:T(8,128)S(1)}) custom-call(s32[1]{0:T(128)} %bitcast.me_ref.refs_0_, bf16[320,1024]{1,0:T(8,128)(2,1)S(1)} %bitcast.33, ...), custom_call_target="tpu_custom_call", output_to_operand_aliasing={{0}: (11, {}), {1}: (12, {})} | custom-call | bytes 4096 | tf_op jit(solution)/shard_map/back/pallas_call | solution.py:290
  29.8 1.5 %collective-permute-done.8.refs_8_ = bf16[512,128]{1,0:T(8,128)(2,1)S(1)} collective-permute-done((bf16[512,128]{1,0:T(8,128)(2,1)S(1)}, bf16[512,128]{1,0:T(8,128)(2,1)S(1)}, u32[]{:S(2)}, u32[]{:S(2)}) %collective-permute-start.8) | collective-permute-done | bytes 131104 | tf_op jit(solution)/shard_map/ppermute | solution.py:357
  31.3 1.1 %post.2 = (bf16[320,1024]{1,0:T(8,128)(2,1)}, bf16[320,1024]{1,0:T(8,128)(2,1)}, f32[8,128]{1,0:T(8,128)S(1)}) custom-call(s32[1]{0:T(128)} %bitcast.me_ref.refs_0_, bf16[320,1024]{1,0:T(8,128)(2,1)S(1)} %bitcast.16, bf16[320,1024]{1,0:T(8,128)(2,1)S(1)} %bitcast.25, f32[320,512]{1,0:T(8,128)S(1)} %get-tuple-element.112.refs_3_, ...), custom_call_target="tpu_custom_call" | custom-call | bytes 4096 | tf_op jit(solution)/shard_map/post/pallas_call | solution.py:328
  32.5 1.0 %collective-permute-done.10.refs_1_ = bf16[512,128]{1,0:T(8,128)(2,1)S(1)} collective-permute-done((bf16[512,128]{1,0:T(8,128)(2,1)S(1)}, bf16[512,128]{1,0:T(8,128)(2,1)S(1)}, u32[]{:S(2)}, u32[]{:S(2)}) %collective-permute-start.10) | collective-permute-done | bytes 131104 | tf_op jit(solution)/shard_map/ppermute | solution.py:357
  33.6 1.1 %post.3 = (bf16[320,1024]{1,0:T(8,128)(2,1)}, bf16[320,1024]{1,0:T(8,128)(2,1)}) custom-call(s32[1]{0:T(128)} %bitcast.me_ref.refs_0_, bf16[320,1024]{1,0:T(8,128)(2,1)S(1)} %bitcast.17, bf16[320,1024]{1,0:T(8,128)(2,1)S(1)} %bitcast.26, f32[320,512]{1,0:T(8,128)S(1)} %get-tuple-element.110.gk_in_ref, ...), custom_call_target="tpu_custom_call", output_to_operand_aliasing={{0}: (8, {}), {1}: (9, {})} | custom-call | bytes 4096 | tf_op jit(solution)/shard_map/post/pallas_call | solution.py:328
  (26 shorter events, 0.4 us)
Async XLA Ops:
  0.6 7.3 %copy-start = (bf16[1,320,1024]{2,1,0:T(8,128)(2,1)S(1)}, bf16[1,320,1024]{2,1,0:T(8,128)(2,1)}, u32[]{:S(2)}) copy-start(bf16[1,320,1024]{2,1,0:T(8,128)(2,1)} %param.5) | copy-start | bytes 1966084
  0.7 7.3 %copy-start.1 = (bf16[1,320,1024]{2,1,0:T(8,128)(2,1)S(1)}, bf16[1,320,1024]{2,1,0:T(8,128)(2,1)}, u32[]{:S(2)}) copy-start(bf16[1,320,1024]{2,1,0:T(8,128)(2,1)} %param.6) | copy-start | bytes 1966084
  2.2 8.4 %collective-permute-start = (bf16[512,128]{1,0:T(8,128)(2,1)S(1)}, bf16[512,128]{1,0:T(8,128)(2,1)S(1)}, u32[]{:S(2)}, u32[]{:S(2)}) collective-permute-start(bf16[512,128]{1,0:T(8,128)(2,1)S(1)} %get-tuple-element.71), channel_id=1, source_target_pairs={{0,4},{1,5},{2,6},{3,7},{16,20},{17,21},{18,22},{19,23}} | collective-permute-start | bytes 393224 | tf_op jit(solution)/shard_map/ppermute | solution.py:357
  5.8 3.5 %copy-start.2 = (bf16[1,320,1024]{2,1,0:T(8,128)(2,1)S(1)}, bf16[1,320,1024]{2,1,0:T(8,128)(2,1)}, u32[]{:S(2)}) copy-start(bf16[1,320,1024]{2,1,0:T(8,128)(2,1)} %param.4) | copy-start | bytes 1966084
  7.3 7.4 %collective-permute-start.1 = (bf16[512,128]{1,0:T(8,128)(2,1)S(1)}, bf16[512,128]{1,0:T(8,128)(2,1)S(1)}, u32[]{:S(2)}, u32[]{:S(2)}) collective-permute-start(bf16[512,128]{1,0:T(8,128)(2,1)S(1)} %get-tuple-element.66.refs_0_), channel_id=1, source_target_pairs={{4,8},{5,9},{6,10},{7,11},{20,24},{21,25},{22,26},{23,27}} | collective-permute-start | bytes 393224 | tf_op jit(solution)/shard_map/ppermute | solution.py:357
  8.0 6.7 %collective-permute-start.2 = (bf16[512,128]{1,0:T(8,128)(2,1)S(1)}, bf16[512,128]{1,0:T(8,128)(2,1)S(1)}, u32[]{:S(2)}, u32[]{:S(2)}) collective-permute-start(bf16[512,128]{1,0:T(8,128)(2,1)S(1)} %get-tuple-element.72.refs_1_), channel_id=1, source_target_pairs={{0,8},{8,12},{1,9},{9,13},{2,10},{10,14},{3,11},{11,15},{16,24},{2... | collective-permute-start | bytes 393224 | tf_op jit(solution)/shard_map/ppermute | solution.py:357
  10.5 4.9 %copy-start.3 = (bf16[1,320,1024]{2,1,0:T(8,128)(2,1)S(1)}, bf16[1,320,1024]{2,1,0:T(8,128)(2,1)}, u32[]{:S(2)}) copy-start(bf16[1,320,1024]{2,1,0:T(8,128)(2,1)} %param.7) | copy-start | bytes 1966084
  10.6 5.6 %collective-permute-start.3 = (bf16[512,128]{1,0:T(8,128)(2,1)S(1)}, bf16[512,128]{1,0:T(8,128)(2,1)S(1)}, u32[]{:S(2)}, u32[]{:S(2)}) collective-permute-start(bf16[512,128]{1,0:T(8,128)(2,1)S(1)} %get-tuple-element.74.refs_0_), channel_id=1, source_target_pairs={{4,12},{5,13},{6,14},{7,15},{20,28},{21,29},{22,30},{23,31}} | collective-permute-start | bytes 393224 | tf_op jit(solution)/shard_map/ppermute | solution.py:357
  11.4 5.7 %collective-permute-start.4 = (bf16[512,128]{1,0:T(8,128)(2,1)S(1)}, bf16[512,128]{1,0:T(8,128)(2,1)S(1)}, u32[]{:S(2)}, u32[]{:S(2)}) collective-permute-start(bf16[512,128]{1,0:T(8,128)(2,1)S(1)} %get-tuple-element.83), channel_id=1, source_target_pairs={{0,4},{4,8},{1,5},{5,9},{2,6},{6,10},{3,7},{7,11},{16,20},{20,24},... | collective-permute-start | bytes 393224 | tf_op jit(solution)/shard_map/ppermute | solution.py:357
  14.7 3.2 %collective-permute-start.5 = (bf16[512,128]{1,0:T(8,128)(2,1)S(1)}, bf16[512,128]{1,0:T(8,128)(2,1)S(1)}, u32[]{:S(2)}, u32[]{:S(2)}) collective-permute-start(bf16[512,128]{1,0:T(8,128)(2,1)S(1)} %get-tuple-element.86), channel_id=1, source_target_pairs={{8,12},{9,13},{10,14},{11,15},{24,28},{25,29},{26,30},{27,31}} | collective-permute-start | bytes 393224 | tf_op jit(solution)/shard_map/ppermute | solution.py:357
  16.3 5.6 %collective-permute-start.6 = (bf16[512,128]{1,0:T(8,128)(2,1)S(1)}, bf16[512,128]{1,0:T(8,128)(2,1)S(1)}, u32[]{:S(2)}, u32[]{:S(2)}) collective-permute-start(bf16[512,128]{1,0:T(8,128)(2,1)S(1)} %get-tuple-element.95), channel_id=1, source_target_pairs={{12,8},{8,4},{13,9},{9,5},{14,10},{10,6},{15,11},{11,7},{28,24},{2... | collective-permute-start | bytes 393224 | tf_op jit(solution)/shard_map/ppermute | solution.py:357
  17.9 7.9 %collective-permute-start.7 = (bf16[512,128]{1,0:T(8,128)(2,1)S(1)}, bf16[512,128]{1,0:T(8,128)(2,1)S(1)}, u32[]{:S(2)}, u32[]{:S(2)}) collective-permute-start(bf16[512,128]{1,0:T(8,128)(2,1)S(1)} %get-tuple-element.98), channel_id=1, source_target_pairs={{12,4},{4,0},{13,5},{5,1},{14,6},{6,2},{15,7},{7,3},{28,20},{20,16... | collective-permute-start | bytes 393224 | tf_op jit(solution)/shard_map/ppermute | solution.py:357
  21.9 9.4 %collective-permute-start.8 = (bf16[512,128]{1,0:T(8,128)(2,1)S(1)}, bf16[512,128]{1,0:T(8,128)(2,1)S(1)}, u32[]{:S(2)}, u32[]{:S(2)}) collective-permute-start(bf16[512,128]{1,0:T(8,128)(2,1)S(1)} %get-tuple-element.115), channel_id=1, source_target_pairs={{8,0},{9,1},{10,2},{11,3},{24,16},{25,17},{26,18},{27,19}} | collective-permute-start | bytes 393224 | tf_op jit(solution)/shard_map/ppermute | solution.py:357
  23.2 9.3 %collective-permute-start.9 = (bf16[512,128]{1,0:T(8,128)(2,1)S(1)}, bf16[512,128]{1,0:T(8,128)(2,1)S(1)}, u32[]{:S(2)}, u32[]{:S(2)}) collective-permute-start(bf16[512,128]{1,0:T(8,128)(2,1)S(1)} %get-tuple-element.115), channel_id=1, source_target_pairs={{12,8},{8,4},{13,9},{9,5},{14,10},{10,6},{15,11},{11,7},{28,24},{2... | collective-permute-start | bytes 393224 | tf_op jit(solution)/shard_map/ppermute | solution.py:357
  25.9 7.7 %collective-permute-start.10 = (bf16[512,128]{1,0:T(8,128)(2,1)S(1)}, bf16[512,128]{1,0:T(8,128)(2,1)S(1)}, u32[]{:S(2)}, u32[]{:S(2)}) collective-permute-start(bf16[512,128]{1,0:T(8,128)(2,1)S(1)} %get-tuple-element.119), channel_id=1, source_target_pairs={{4,0},{5,1},{6,2},{7,3},{20,16},{21,17},{22,18},{23,19}} | collective-permute-start | bytes 393224 | tf_op jit(solution)/shard_map/ppermute | solution.py:357

commit v7 on v6

--- a/solution.py
+++ b/solution.py
@@ -90,36 +90,46 @@
     )(me, k, v, token, *spare, *passed)
 
 
-def state_kernel(half, roles, me_ref, k_ref, v_ref, token_ref, out_ref, done_ref, k_buf, v_buf, k_sem, v_sem):
-    width = k_buf.shape[1]
+def state_kernel(halves, roles, keep, me_ref, k_ref, v_ref, token_ref, *refs):
+    done_ref, k_buf, v_buf, k_sem, v_sem = refs[-5:]
+    outs = refs[len(keep) : -5]
+    width = k_buf.shape[2]
     heads = width // DH
     done_ref[...] = token_ref[...]
+    if keep:
+
+        @on(me_ref[0], keep)
+        def _():
+            outs[0][...] = refs[0][...]
 
     @on(me_ref[0], roles)
     def _():
-        cols = slice(half * width, (half + 1) * width)
-        copies = (
-            pltpu.make_async_copy(k_ref.at[:, cols], k_buf, k_sem),
-            pltpu.make_async_copy(v_ref.at[:, cols], v_buf, v_sem),
-        )
+        copies = []
+        for slot, half in enumerate(halves):
+            cols = slice(half * width, (half + 1) * width)
+            copies.append(pltpu.make_async_copy(k_ref.at[:, cols], k_buf.at[slot], k_sem.at[slot]))
+            copies.append(pltpu.make_async_copy(v_ref.at[:, cols], v_buf.at[slot], v_sem.at[slot]))
         for copy in copies:
             copy.start()
         for copy in copies:
             copy.wait()
-        for h in range(heads):
-            out_ref[head(h), :] = dot_tn(k_buf[:, head(h)], v_buf[:, head(h)]).astype(BF16)
-
-
-def states(half, roles, me, k, v, token):
+        for slot, out_ref in enumerate(outs):
+            for h in range(heads):
+                out_ref[head(h), :] = dot_tn(k_buf[slot, :, head(h)], v_buf[slot, :, head(h)]).astype(BF16)
+
+
+def states(halves, roles, me, k, v, token, keep=(), spare=()):
     length, width = k.shape
+    count = len(halves)
     k, v = (pltpu.with_memory_space_constraint(x, pltpu.HBM) for x in (k, v))
-    return pl.pallas_call(
-        functools.partial(state_kernel, half, roles),
-        in_specs=[SMEM_SPEC, HBM_SPEC, HBM_SPEC, VMEM_SPEC],
-        out_specs=(VMEM_SPEC,) * 2,
-        scratch_shapes=[pltpu.VMEM((length, width // 2), BF16)] * 2 + [pltpu.SemaphoreType.DMA] * 2,
-        **params("states", (jax.ShapeDtypeStruct((width // 2, DH), BF16), TOKEN)),
-    )(me, k, v, token)
+    shape = jax.ShapeDtypeStruct((width // 2, DH), BF16)
+    return pl.pallas_call(
+        functools.partial(state_kernel, halves, roles, keep),
+        in_specs=[SMEM_SPEC, HBM_SPEC, HBM_SPEC] + [VMEM_SPEC] * (1 + len(spare)),
+        out_specs=(VMEM_SPEC,) * (count + 1),
+        scratch_shapes=[pltpu.VMEM((count, length, width // 2), BF16)] * 2 + [pltpu.SemaphoreType.DMA((count,))] * 2,
+        **params("states", (shape,) * count + (TOKEN,)),
+    )(me, k, v, token, *spare)
 
 
 TOKEN = jax.ShapeDtypeStruct((8, DH), F32)
@@ -356,9 +366,9 @@
     def send(x, pairs):
         return lax.ppermute(x, "ctx", pairs)
 
-    s_a, token = states(0, (0,), me, k, v, token)
+    s_a, s_kept, token = states((0, 1), (0,), me, k, v, token)
     r_a = send(s_a, [(0, 1)])
-    s_b, token = states(1, (0, 1), me, k, v, token)
+    s_b, token = states((1,), (1,), me, k, v, token, (0,), (s_kept,))
     r_b = send(s_b, [(1, 2)])
     s_c, token = near_states(0, (1, 2), me, k, v, token, (0,), (s_b,))
     r_c = send(s_c, [(0, 2), (2, 3)])

time: 35 us -> 35 us (level)
  starting transfers between devices: 15.4 us -> 16.6 us
  Pallas kernels: 13.5 us -> 12.4 us
    ppermute x11, starting transfers between devices: 15.4 us -> 16.6 us  [send(): return lax.ppermute(x, 'ctx', pairs)]
    pallas_call x2, Pallas kernels: 2.95 us -> 1.85 us  [states(): pl.pallas_call(functools.partial(state_kernel, halves, roles, keep), in_s...]
  transfers between devices with their start and end apart: 11 -> 11, of which waited for: 4 -> 4; matrix products, arithmetic and copies ran while one was open for 0% -> 0% of each run, Pallas kernels for 32% -> 27%
where the time goes in v7:
time: 35 us; the launch traced here: 34.7 us
  starting transfers between devices  16.6 us (47%)
  Pallas kernels  12.4 us (35%)
  waiting for transfers between devices  4.67 us (13%)
  between operations  0.98 us (3%)
    ppermute x11, starting transfers between devices, send(): return lax.ppermute(x, 'ctx', pairs)  16.6 us
    pallas_call x2, Pallas kernels, back(): pl.pallas_call(functools.partial(back_kernel, half_of, roles, len(sets)),...  5.24 us
    ppermute x11, waiting for transfers between devices, send(): return lax.ppermute(x, 'ctx', pairs)  4.67 us
    pallas_call x2, Pallas kernels, post(): pl.pallas_call(functools.partial(post_kernel if filled else post_first_ke...  2.24 us
    pallas_call x2, Pallas kernels, states(): pl.pallas_call(functools.partial(state_kernel, halves, roles, keep), in_s...  1.85 us
    pallas_call x4, Pallas kernels, mid(): pl.pallas_call(functools.partial(mid_kernel, half_of, roles, keep, merge)...  1.63 us
    pallas_call x1, Pallas kernels, intra(): pl.pallas_call(intra_kernel, in_specs=[VMEM_SPEC] * 4, out_specs=(VMEM_SP...  1.2 us
  transfers between devices with their start and end apart: 11, of which 4 were waited for; matrix products, arithmetic and copies ran while one was open for 0% of the time, Pallas kernels for 27%

profile of v7, /device:TPU:0, one launch (start us, length us, event | category | flops | bytes accessed | tf_op | source)
XLA Modules:
  0.0 34.7 jit_solution(9621891144684536259)
XLA Ops:
  0.7 1.8 %states.2 = (bf16[512,128]{1,0:T(8,128)(2,1)S(1)}, bf16[512,128]{1,0:T(8,128)(2,1)S(1)}, f32[8,128]{1,0:T(8,128)S(1)}) custom-call(s32[1]{0:T(128)} %bitcast.me_ref.refs_0_, bf16[320,1024]{1,0:T(8,128)(2,1)} %bitcast.9, bf16[320,1024]{1,0:T(8,128)(2,1)} %bitcast.18, f32[8,128]{1,0:T(8,128)S(1)} %broadcast_in_dim.3.token_ref), custom_call_target="tpu_custom_call" | custom-call | bytes 4096 | tf_op jit(solution)/shard_map/states/pallas_call | solution.py:126
  2.5 3.3 %collective-permute-start = (bf16[512,128]{1,0:T(8,128)(2,1)S(1)}, bf16[512,128]{1,0:T(8,128)(2,1)S(1)}, u32[]{:S(2)}, u32[]{:S(2)}) collective-permute-start(bf16[512,128]{1,0:T(8,128)(2,1)S(1)} %get-tuple-element.73), channel_id=1, source_target_pairs={{0,4},{1,5},{2,6},{3,7},{16,20},{17,21},{18,22},{19,23}} | collective-permute-start | bytes 393224 | tf_op jit(solution)/shard_map/ppermute | solution.py:367
  5.9 0.8 %collective-permute-start.1 = (bf16[512,128]{1,0:T(8,128)(2,1)S(1)}, bf16[512,128]{1,0:T(8,128)(2,1)S(1)}, u32[]{:S(2)}, u32[]{:S(2)}) collective-permute-start(bf16[512,128]{1,0:T(8,128)(2,1)S(1)} %get-tuple-element.68.refs_0_), channel_id=1, source_target_pairs={{4,8},{5,9},{6,10},{7,11},{20,24},{21,25},{22,26},{23,27}} | collective-permute-start | bytes 393224 | tf_op jit(solution)/shard_map/ppermute | solution.py:367
  6.7 2.6 %collective-permute-start.2 = (bf16[512,128]{1,0:T(8,128)(2,1)S(1)}, bf16[512,128]{1,0:T(8,128)(2,1)S(1)}, u32[]{:S(2)}, u32[]{:S(2)}) collective-permute-start(bf16[512,128]{1,0:T(8,128)(2,1)S(1)} %get-tuple-element.74.refs_1_), channel_id=1, source_target_pairs={{0,8},{8,12},{1,9},{9,13},{2,10},{10,14},{3,11},{11,15},{16,24},{2... | collective-permute-start | bytes 393224 | tf_op jit(solution)/shard_map/ppermute | solution.py:367
  9.3 1.2 %intra.1 = (f32[320,1024]{1,0:T(8,128)S(1)}, bf16[1024,320]{1,0:T(8,128)(2,1)S(1)}, f32[8,128]{1,0:T(8,128)S(1)}) custom-call(bf16[320,1024]{1,0:T(8,128)(2,1)S(1)} %bitcast.27, bf16[320,1024]{1,0:T(8,128)(2,1)S(1)} %bitcast.12, bf16[320,1024]{1,0:T(8,128)(2,1)S(1)} %bitcast.21, f32[8,128]{1,0:T(8,128)S(1)} %get-tuple-element.69.token_ref), custom_call_target="tpu_custom_call" | custom-call | bytes 4096 | tf_op jit(solution)/shard_map/intra/pallas_call | solution.py:156
  10.6 0.8 %collective-permute-start.3 = (bf16[512,128]{1,0:T(8,128)(2,1)S(1)}, bf16[512,128]{1,0:T(8,128)(2,1)S(1)}, u32[]{:S(2)}, u32[]{:S(2)}) collective-permute-start(bf16[512,128]{1,0:T(8,128)(2,1)S(1)} %get-tuple-element.76.refs_0_), channel_id=1, source_target_pairs={{4,12},{5,13},{6,14},{7,15},{20,28},{21,29},{22,30},{23,31}} | collective-permute-start | bytes 393224 | tf_op jit(solution)/shard_map/ppermute | solution.py:367
  11.5 3.2 %collective-permute-start.4 = (bf16[512,128]{1,0:T(8,128)(2,1)S(1)}, bf16[512,128]{1,0:T(8,128)(2,1)S(1)}, u32[]{:S(2)}, u32[]{:S(2)}) collective-permute-start(bf16[512,128]{1,0:T(8,128)(2,1)S(1)} %get-tuple-element.85), channel_id=1, source_target_pairs={{0,4},{4,8},{1,5},{5,9},{2,6},{6,10},{3,7},{7,11},{16,20},{20,24},... | collective-permute-start | bytes 393224 | tf_op jit(solution)/shard_map/ppermute | solution.py:367
  14.7 0.1 add.8
  14.7 0.7 %collective-permute-start.5 = (bf16[512,128]{1,0:T(8,128)(2,1)S(1)}, bf16[512,128]{1,0:T(8,128)(2,1)S(1)}, u32[]{:S(2)}, u32[]{:S(2)}) collective-permute-start(bf16[512,128]{1,0:T(8,128)(2,1)S(1)} %get-tuple-element.88), channel_id=1, source_target_pairs={{8,12},{9,13},{10,14},{11,15},{24,28},{25,29},{26,30},{27,31}} | collective-permute-start | bytes 393224 | tf_op jit(solution)/shard_map/ppermute | solution.py:367
  15.4 0.8 %mid.4 = (bf16[320,512]{1,0:T(8,128)(2,1)S(1)}, bf16[320,512]{1,0:T(8,128)(2,1)S(1)}, bf16[512,128]{1,0:T(8,128)(2,1)S(1)}, f32[8,128]{1,0:T(8,128)S(1)}, bf16[512,128]{1,0:T(8,128)(2,1)S(1)}) custom-call(s32[1]{0:T(128)} %bitcast.me_ref.refs_0_, bf16[320,1024]{1,0:T(8,128)(2,1)S(1)} %bitcast.28, bf16[1024,320]{1,0:T(8,128)(2,1)S(1)} %get-tuple-element.70.qt_ref, ...), custom_call_target="tpu_custom_call" | custom-call | bytes 4096 | tf_op jit(solution)/shard_map/mid/pallas_call | solution.py:249
  16.3 0.7 %collective-permute-start.6 = (bf16[512,128]{1,0:T(8,128)(2,1)S(1)}, bf16[512,128]{1,0:T(8,128)(2,1)S(1)}, u32[]{:S(2)}, u32[]{:S(2)}) collective-permute-start(bf16[512,128]{1,0:T(8,128)(2,1)S(1)} %get-tuple-element.97), channel_id=1, source_target_pairs={{12,8},{8,4},{13,9},{9,5},{14,10},{10,6},{15,11},{11,7},{28,24},{2... | collective-permute-start | bytes 393224 | tf_op jit(solution)/shard_map/ppermute | solution.py:367
  17.0 0.2 collective-permute-done.4.refs_0_
  17.1 0.8 %mid.6 = (bf16[320,512]{1,0:T(8,128)(2,1)S(1)}, bf16[320,512]{1,0:T(8,128)(2,1)S(1)}, bf16[512,128]{1,0:T(8,128)(2,1)S(1)}, f32[8,128]{1,0:T(8,128)S(1)}, bf16[512,128]{1,0:T(8,128)(2,1)S(1)}) custom-call(s32[1]{0:T(128)} %bitcast.me_ref.refs_0_, bf16[320,1024]{1,0:T(8,128)(2,1)S(1)} %bitcast.30, bf16[1024,320]{1,0:T(8,128)(2,1)S(1)} %get-tuple-element.70.qt_ref, ...), custom_call_target="tpu_custom_call" | custom-call | bytes 4096 | tf_op jit(solution)/shard_map/mid/pallas_call | solution.py:249
  18.0 1.3 %collective-permute-start.7 = (bf16[512,128]{1,0:T(8,128)(2,1)S(1)}, bf16[512,128]{1,0:T(8,128)(2,1)S(1)}, u32[]{:S(2)}, u32[]{:S(2)}) collective-permute-start(bf16[512,128]{1,0:T(8,128)(2,1)S(1)} %get-tuple-element.100), channel_id=1, source_target_pairs={{12,4},{4,0},{13,5},{5,1},{14,6},{6,2},{15,7},{7,3},{28,20},{20,16... | collective-permute-start | bytes 393224 | tf_op jit(solution)/shard_map/ppermute | solution.py:367
  19.3 2.6 %back.2 = (bf16[320,1024]{1,0:T(8,128)(2,1)}, bf16[320,1024]{1,0:T(8,128)(2,1)}, f32[320,512]{1,0:T(8,128)S(1)}, f32[320,512]{1,0:T(8,128)S(1)}, f32[8,128]{1,0:T(8,128)S(1)}) custom-call(s32[1]{0:T(128)} %bitcast.me_ref.refs_0_, bf16[320,1024]{1,0:T(8,128)(2,1)S(1)} %bitcast.32, bf16[320,1024]{1,0:T(8,128)(2,1)S(1)} %bitcast.14, ...), custom_call_target="tpu_custom_call" | custom-call | bytes 4096 | tf_op jit(solution)/shard_map/back/pallas_call | solution.py:300
  21.9 1.3 %collective-permute-start.8 = (bf16[512,128]{1,0:T(8,128)(2,1)S(1)}, bf16[512,128]{1,0:T(8,128)(2,1)S(1)}, u32[]{:S(2)}, u32[]{:S(2)}) collective-permute-start(bf16[512,128]{1,0:T(8,128)(2,1)S(1)} %get-tuple-element.117), channel_id=1, source_target_pairs={{8,0},{9,1},{10,2},{11,3},{24,16},{25,17},{26,18},{27,19}} | collective-permute-start | bytes 393224 | tf_op jit(solution)/shard_map/ppermute | solution.py:367
  23.2 0.7 %collective-permute-start.9 = (bf16[512,128]{1,0:T(8,128)(2,1)S(1)}, bf16[512,128]{1,0:T(8,128)(2,1)S(1)}, u32[]{:S(2)}, u32[]{:S(2)}) collective-permute-start(bf16[512,128]{1,0:T(8,128)(2,1)S(1)} %get-tuple-element.117), channel_id=1, source_target_pairs={{12,8},{8,4},{13,9},{9,5},{14,10},{10,6},{15,11},{11,7},{28,24},{2... | collective-permute-start | bytes 393224 | tf_op jit(solution)/shard_map/ppermute | solution.py:367
  23.9 1.9 %collective-permute-done.7.refs_1_.refs_7_ = bf16[512,128]{1,0:T(8,128)(2,1)S(1)} collective-permute-done((bf16[512,128]{1,0:T(8,128)(2,1)S(1)}, bf16[512,128]{1,0:T(8,128)(2,1)S(1)}, u32[]{:S(2)}, u32[]{:S(2)}) %collective-permute-start.7) | collective-permute-done | bytes 131104 | tf_op jit(solution)/shard_map/ppermute | solution.py:367
  25.9 1.3 %collective-permute-start.10 = (bf16[512,128]{1,0:T(8,128)(2,1)S(1)}, bf16[512,128]{1,0:T(8,128)(2,1)S(1)}, u32[]{:S(2)}, u32[]{:S(2)}) collective-permute-start(bf16[512,128]{1,0:T(8,128)(2,1)S(1)} %get-tuple-element.121), channel_id=1, source_target_pairs={{4,0},{5,1},{6,2},{7,3},{20,16},{21,17},{22,18},{23,19}} | collective-permute-start | bytes 393224 | tf_op jit(solution)/shard_map/ppermute | solution.py:367
  27.2 2.6 %back.3 = (bf16[320,1024]{1,0:T(8,128)(2,1)}, bf16[320,1024]{1,0:T(8,128)(2,1)}, f32[320,512]{1,0:T(8,128)S(1)}, f32[320,512]{1,0:T(8,128)S(1)}, f32[8,128]{1,0:T(8,128)S(1)}) custom-call(s32[1]{0:T(128)} %bitcast.me_ref.refs_0_, bf16[320,1024]{1,0:T(8,128)(2,1)S(1)} %bitcast.33, ...), custom_call_target="tpu_custom_call", output_to_operand_aliasing={{0}: (11, {}), {1}: (12, {})} | custom-call | bytes 4096 | tf_op jit(solution)/shard_map/back/pallas_call | solution.py:300
  29.8 1.5 %collective-permute-done.8.refs_8_ = bf16[512,128]{1,0:T(8,128)(2,1)S(1)} collective-permute-done((bf16[512,128]{1,0:T(8,128)(2,1)S(1)}, bf16[512,128]{1,0:T(8,128)(2,1)S(1)}, u32[]{:S(2)}, u32[]{:S(2)}) %collective-permute-start.8) | collective-permute-done | bytes 131104 | tf_op jit(solution)/shard_map/ppermute | solution.py:367
  31.4 1.1 %post.2 = (bf16[320,1024]{1,0:T(8,128)(2,1)}, bf16[320,1024]{1,0:T(8,128)(2,1)}, f32[8,128]{1,0:T(8,128)S(1)}) custom-call(s32[1]{0:T(128)} %bitcast.me_ref.refs_0_, bf16[320,1024]{1,0:T(8,128)(2,1)S(1)} %bitcast.16, bf16[320,1024]{1,0:T(8,128)(2,1)S(1)} %bitcast.25, f32[320,512]{1,0:T(8,128)S(1)} %get-tuple-element.114.refs_3_, ...), custom_call_target="tpu_custom_call" | custom-call | bytes 4096 | tf_op jit(solution)/shard_map/post/pallas_call | solution.py:338
  32.5 1.0 %collective-permute-done.10.refs_1_ = bf16[512,128]{1,0:T(8,128)(2,1)S(1)} collective-permute-done((bf16[512,128]{1,0:T(8,128)(2,1)S(1)}, bf16[512,128]{1,0:T(8,128)(2,1)S(1)}, u32[]{:S(2)}, u32[]{:S(2)}) %collective-permute-start.10) | collective-permute-done | bytes 131104 | tf_op jit(solution)/shard_map/ppermute | solution.py:367
  33.6 1.1 %post.3 = (bf16[320,1024]{1,0:T(8,128)(2,1)}, bf16[320,1024]{1,0:T(8,128)(2,1)}) custom-call(s32[1]{0:T(128)} %bitcast.me_ref.refs_0_, bf16[320,1024]{1,0:T(8,128)(2,1)S(1)} %bitcast.17, bf16[320,1024]{1,0:T(8,128)(2,1)S(1)} %bitcast.26, f32[320,512]{1,0:T(8,128)S(1)} %get-tuple-element.112.gk_in_ref, ...), custom_call_target="tpu_custom_call", output_to_operand_aliasing={{0}: (8, {}), {1}: (9, {})} | custom-call | bytes 4096 | tf_op jit(solution)/shard_map/post/pallas_call | solution.py:338
  (26 shorter events, 0.4 us)
Async XLA Ops:
  0.6 6.0 %copy-start = (bf16[1,320,1024]{2,1,0:T(8,128)(2,1)S(1)}, bf16[1,320,1024]{2,1,0:T(8,128)(2,1)}, u32[]{:S(2)}) copy-start(bf16[1,320,1024]{2,1,0:T(8,128)(2,1)} %param.5) | copy-start | bytes 1966084
  0.7 6.0 %copy-start.1 = (bf16[1,320,1024]{2,1,0:T(8,128)(2,1)S(1)}, bf16[1,320,1024]{2,1,0:T(8,128)(2,1)}, u32[]{:S(2)}) copy-start(bf16[1,320,1024]{2,1,0:T(8,128)(2,1)} %param.6) | copy-start | bytes 1966084
  2.5 8.1 %collective-permute-start = (bf16[512,128]{1,0:T(8,128)(2,1)S(1)}, bf16[512,128]{1,0:T(8,128)(2,1)S(1)}, u32[]{:S(2)}, u32[]{:S(2)}) collective-permute-start(bf16[512,128]{1,0:T(8,128)(2,1)S(1)} %get-tuple-element.73), channel_id=1, source_target_pairs={{0,4},{1,5},{2,6},{3,7},{16,20},{17,21},{18,22},{19,23}} | collective-permute-start | bytes 393224 | tf_op jit(solution)/shard_map/ppermute | solution.py:367
  5.8 3.5 %copy-start.2 = (bf16[1,320,1024]{2,1,0:T(8,128)(2,1)S(1)}, bf16[1,320,1024]{2,1,0:T(8,128)(2,1)}, u32[]{:S(2)}) copy-start(bf16[1,320,1024]{2,1,0:T(8,128)(2,1)} %param.4) | copy-start | bytes 1966084
  5.9 8.8 %collective-permute-start.1 = (bf16[512,128]{1,0:T(8,128)(2,1)S(1)}, bf16[512,128]{1,0:T(8,128)(2,1)S(1)}, u32[]{:S(2)}, u32[]{:S(2)}) collective-permute-start(bf16[512,128]{1,0:T(8,128)(2,1)S(1)} %get-tuple-element.68.refs_0_), channel_id=1, source_target_pairs={{4,8},{5,9},{6,10},{7,11},{20,24},{21,25},{22,26},{23,27}} | collective-permute-start | bytes 393224 | tf_op jit(solution)/shard_map/ppermute | solution.py:367
  6.7 8.0 %collective-permute-start.2 = (bf16[512,128]{1,0:T(8,128)(2,1)S(1)}, bf16[512,128]{1,0:T(8,128)(2,1)S(1)}, u32[]{:S(2)}, u32[]{:S(2)}) collective-permute-start(bf16[512,128]{1,0:T(8,128)(2,1)S(1)} %get-tuple-element.74.refs_1_), channel_id=1, source_target_pairs={{0,8},{8,12},{1,9},{9,13},{2,10},{10,14},{3,11},{11,15},{16,24},{2... | collective-permute-start | bytes 393224 | tf_op jit(solution)/shard_map/ppermute | solution.py:367
  10.6 4.9 %copy-start.3 = (bf16[1,320,1024]{2,1,0:T(8,128)(2,1)S(1)}, bf16[1,320,1024]{2,1,0:T(8,128)(2,1)}, u32[]{:S(2)}) copy-start(bf16[1,320,1024]{2,1,0:T(8,128)(2,1)} %param.7) | copy-start | bytes 1966084
  10.6 5.6 %collective-permute-start.3 = (bf16[512,128]{1,0:T(8,128)(2,1)S(1)}, bf16[512,128]{1,0:T(8,128)(2,1)S(1)}, u32[]{:S(2)}, u32[]{:S(2)}) collective-permute-start(bf16[512,128]{1,0:T(8,128)(2,1)S(1)} %get-tuple-element.76.refs_0_), channel_id=1, source_target_pairs={{4,12},{5,13},{6,14},{7,15},{20,28},{21,29},{22,30},{23,31}} | collective-permute-start | bytes 393224 | tf_op jit(solution)/shard_map/ppermute | solution.py:367
  11.5 5.7 %collective-permute-start.4 = (bf16[512,128]{1,0:T(8,128)(2,1)S(1)}, bf16[512,128]{1,0:T(8,128)(2,1)S(1)}, u32[]{:S(2)}, u32[]{:S(2)}) collective-permute-start(bf16[512,128]{1,0:T(8,128)(2,1)S(1)} %get-tuple-element.85), channel_id=1, source_target_pairs={{0,4},{4,8},{1,5},{5,9},{2,6},{6,10},{3,7},{7,11},{16,20},{20,24},... | collective-permute-start | bytes 393224 | tf_op jit(solution)/shard_map/ppermute | solution.py:367
  14.7 3.2 %collective-permute-start.5 = (bf16[512,128]{1,0:T(8,128)(2,1)S(1)}, bf16[512,128]{1,0:T(8,128)(2,1)S(1)}, u32[]{:S(2)}, u32[]{:S(2)}) collective-permute-start(bf16[512,128]{1,0:T(8,128)(2,1)S(1)} %get-tuple-element.88), channel_id=1, source_target_pairs={{8,12},{9,13},{10,14},{11,15},{24,28},{25,29},{26,30},{27,31}} | collective-permute-start | bytes 393224 | tf_op jit(solution)/shard_map/ppermute | solution.py:367
  16.3 5.6 %collective-permute-start.6 = (bf16[512,128]{1,0:T(8,128)(2,1)S(1)}, bf16[512,128]{1,0:T(8,128)(2,1)S(1)}, u32[]{:S(2)}, u32[]{:S(2)}) collective-permute-start(bf16[512,128]{1,0:T(8,128)(2,1)S(1)} %get-tuple-element.97), channel_id=1, source_target_pairs={{12,8},{8,4},{13,9},{9,5},{14,10},{10,6},{15,11},{11,7},{28,24},{2... | collective-permute-start | bytes 393224 | tf_op jit(solution)/shard_map/ppermute | solution.py:367
  18.0 7.9 %collective-permute-start.7 = (bf16[512,128]{1,0:T(8,128)(2,1)S(1)}, bf16[512,128]{1,0:T(8,128)(2,1)S(1)}, u32[]{:S(2)}, u32[]{:S(2)}) collective-permute-start(bf16[512,128]{1,0:T(8,128)(2,1)S(1)} %get-tuple-element.100), channel_id=1, source_target_pairs={{12,4},{4,0},{13,5},{5,1},{14,6},{6,2},{15,7},{7,3},{28,20},{20,16... | collective-permute-start | bytes 393224 | tf_op jit(solution)/shard_map/ppermute | solution.py:367
  21.9 9.4 %collective-permute-start.8 = (bf16[512,128]{1,0:T(8,128)(2,1)S(1)}, bf16[512,128]{1,0:T(8,128)(2,1)S(1)}, u32[]{:S(2)}, u32[]{:S(2)}) collective-permute-start(bf16[512,128]{1,0:T(8,128)(2,1)S(1)} %get-tuple-element.117), channel_id=1, source_target_pairs={{8,0},{9,1},{10,2},{11,3},{24,16},{25,17},{26,18},{27,19}} | collective-permute-start | bytes 393224 | tf_op jit(solution)/shard_map/ppermute | solution.py:367
  23.2 9.2 %collective-permute-start.9 = (bf16[512,128]{1,0:T(8,128)(2,1)S(1)}, bf16[512,128]{1,0:T(8,128)(2,1)S(1)}, u32[]{:S(2)}, u32[]{:S(2)}) collective-permute-start(bf16[512,128]{1,0:T(8,128)(2,1)S(1)} %get-tuple-element.117), channel_id=1, source_target_pairs={{12,8},{8,4},{13,9},{9,5},{14,10},{10,6},{15,11},{11,7},{28,24},{2... | collective-permute-start | bytes 393224 | tf_op jit(solution)/shard_map/ppermute | solution.py:367
  25.9 7.7 %collective-permute-start.10 = (bf16[512,128]{1,0:T(8,128)(2,1)S(1)}, bf16[512,128]{1,0:T(8,128)(2,1)S(1)}, u32[]{:S(2)}, u32[]{:S(2)}) collective-permute-start(bf16[512,128]{1,0:T(8,128)(2,1)S(1)} %get-tuple-element.121), channel_id=1, source_target_pairs={{4,0},{5,1},{6,2},{7,3},{20,16},{21,17},{22,18},{23,19}} | collective-permute-start | bytes 393224 | tf_op jit(solution)/shard_map/ppermute | solution.py:367

commit v8 on v7

--- a/solution.py
+++ b/solution.py
@@ -380,10 +380,11 @@
     r_near = send(s12, [(0, 1), (1, 2)])
     r_b, token = add(token, r_b)
     s123, token = add(token, r_b, r_c, s_y)
+    r_last = send(s123, [(2, 3)])
+    first_end, g_one, token = mid(even_half, (3,), me, shared, token, (r_c, r_far))
+    u_one = send(g_one, [(3, 2)])
     first, g_first, token = mid(even_half, (0, 1, 2), me, shared, token, (r_a, r_b, r_c))
-    r_last = send(s123, [(2, 3)])
-    first_end, g_one, token = mid(even_half, (3,), me, shared, token, (r_c, r_far), (2,), (g_first,))
-    u_one = send(g_one, [(3, 2), (2, 1)])
+    u_side = send(g_first, [(2, 1)])
     second, g_rest, token = mid(odd_half, (0, 1, 2), me, shared, token, (r_near,))
     second_end, g_two, g_second, token = mid(odd_half, (3,), me, shared, token, (r_last,), (1,), (g_first, g_rest))
     u_two = send(g_two, [(3, 1), (1, 0)])
@@ -391,12 +392,12 @@
     g12, token = add(token, u_one, g_second)
     w_far = send(g12, [(2, 0)])
     w_near = send(g12, [(3, 2), (2, 1)])
-    g123, token = add(token, u_one, u_two, g_second)
+    g123, token = add(token, u_side, u_two, g_second)
     w_last = send(g123, [(1, 0)])
     normed, grad_q, gk_first, gv_first, token = back(
         even_half, (3,), me, q, k, v, token, (first, first_end), (normed, grad_q)
     )
-    *filled, token = post(odd_half, me, k, v, gk_second, gv_second, token, (u_one, u_two, w_far))
+    *filled, token = post(odd_half, me, k, v, gk_second, gv_second, token, (u_one, u_side, u_two, w_far))
     l_near, token = add(token, w_near)
     grad_k, grad_v = post(even_half, me, k, v, gk_first, gv_first, token, (l_near, w_last), filled)
     return tuple(x.reshape(out_shape) for x in (normed, grad_q, grad_k, grad_v))

time: 35 us -> 35.1 us (level)
  waiting for transfers between devices: 4.67 us -> 4 us
  starting transfers between devices: 16.6 us -> 17.2 us
    ppermute x11 -> x12, waiting for transfers between devices: 4.67 us -> 4 us  [send(): return lax.ppermute(x, 'ctx', pairs)]
    ppermute x11 -> x12, starting transfers between devices: 16.6 us -> 17.2 us  [send(): return lax.ppermute(x, 'ctx', pairs)]
  transfers between devices with their start and end apart: 11 -> 12, of which waited for: 4 -> 3; matrix products, arithmetic and copies ran while one was open for 0% -> 0% of each run, Pallas kernels for 27% -> 28%
where the time goes in v8:
time: 35.1 us; the launch traced here: 34.7 us
  starting transfers between devices  17.2 us (49%)
  Pallas kernels  12.5 us (36%)
  waiting for transfers between devices  4 us (11%)
  between operations  1 us (3%)
    ppermute x12, starting transfers between devices, send(): return lax.ppermute(x, 'ctx', pairs)  17.2 us
    pallas_call x2, Pallas kernels, back(): pl.pallas_call(functools.partial(back_kernel, half_of, roles, len(sets)),...  5.25 us
    ppermute x12, waiting for transfers between devices, send(): return lax.ppermute(x, 'ctx', pairs)  4 us
    pallas_call x2, Pallas kernels, post(): pl.pallas_call(functools.partial(post_kernel if filled else post_first_ke...  2.26 us
    pallas_call x2, Pallas kernels, states(): pl.pallas_call(functools.partial(state_kernel, halves, roles, keep), in_s...  1.85 us
    pallas_call x4, Pallas kernels, mid(): pl.pallas_call(functools.partial(mid_kernel, half_of, roles, keep, merge)...  1.63 us
    pallas_call x1, Pallas kernels, intra(): pl.pallas_call(intra_kernel, in_specs=[VMEM_SPEC] * 4, out_specs=(VMEM_SP...  1.2 us
  transfers between devices with their start and end apart: 12, of which 3 were waited for; matrix products, arithmetic and copies ran while one was open for 0% of the time, Pallas kernels for 28%

profile of v8, /device:TPU:0, one launch (start us, length us, event | category | flops | bytes accessed | tf_op | source)
XLA Modules:
  0.0 34.7 jit_solution(7372077124515334858)
XLA Ops:
  0.7 1.8 %states.2 = (bf16[512,128]{1,0:T(8,128)(2,1)S(1)}, bf16[512,128]{1,0:T(8,128)(2,1)S(1)}, f32[8,128]{1,0:T(8,128)S(1)}) custom-call(s32[1]{0:T(128)} %bitcast.me_ref.refs_0_, bf16[320,1024]{1,0:T(8,128)(2,1)} %bitcast.9, bf16[320,1024]{1,0:T(8,128)(2,1)} %bitcast.18, f32[8,128]{1,0:T(8,128)S(1)} %broadcast_in_dim.3.token_ref), custom_call_target="tpu_custom_call" | custom-call | bytes 4096 | tf_op jit(solution)/shard_map/states/pallas_call | solution.py:126
  2.5 3.3 %collective-permute-start = (bf16[512,128]{1,0:T(8,128)(2,1)S(1)}, bf16[512,128]{1,0:T(8,128)(2,1)S(1)}, u32[]{:S(2)}, u32[]{:S(2)}) collective-permute-start(bf16[512,128]{1,0:T(8,128)(2,1)S(1)} %get-tuple-element.73), channel_id=1, source_target_pairs={{0,4},{1,5},{2,6},{3,7},{16,20},{17,21},{18,22},{19,23}} | collective-permute-start | bytes 393224 | tf_op jit(solution)/shard_map/ppermute | solution.py:367
  5.9 0.8 %collective-permute-start.1 = (bf16[512,128]{1,0:T(8,128)(2,1)S(1)}, bf16[512,128]{1,0:T(8,128)(2,1)S(1)}, u32[]{:S(2)}, u32[]{:S(2)}) collective-permute-start(bf16[512,128]{1,0:T(8,128)(2,1)S(1)} %get-tuple-element.68.refs_0_), channel_id=1, source_target_pairs={{4,8},{5,9},{6,10},{7,11},{20,24},{21,25},{22,26},{23,27}} | collective-permute-start | bytes 393224 | tf_op jit(solution)/shard_map/ppermute | solution.py:367
  6.7 2.6 %collective-permute-start.2 = (bf16[512,128]{1,0:T(8,128)(2,1)S(1)}, bf16[512,128]{1,0:T(8,128)(2,1)S(1)}, u32[]{:S(2)}, u32[]{:S(2)}) collective-permute-start(bf16[512,128]{1,0:T(8,128)(2,1)S(1)} %get-tuple-element.74.refs_1_), channel_id=1, source_target_pairs={{0,8},{8,12},{1,9},{9,13},{2,10},{10,14},{3,11},{11,15},{16,24},{2... | collective-permute-start | bytes 393224 | tf_op jit(solution)/shard_map/ppermute | solution.py:367
  9.3 1.2 %intra.1 = (f32[320,1024]{1,0:T(8,128)S(1)}, bf16[1024,320]{1,0:T(8,128)(2,1)S(1)}, f32[8,128]{1,0:T(8,128)S(1)}) custom-call(bf16[320,1024]{1,0:T(8,128)(2,1)S(1)} %bitcast.27, bf16[320,1024]{1,0:T(8,128)(2,1)S(1)} %bitcast.12, bf16[320,1024]{1,0:T(8,128)(2,1)S(1)} %bitcast.21, f32[8,128]{1,0:T(8,128)S(1)} %get-tuple-element.69.token_ref), custom_call_target="tpu_custom_call" | custom-call | bytes 4096 | tf_op jit(solution)/shard_map/intra/pallas_call | solution.py:156
  10.6 0.8 %collective-permute-start.3 = (bf16[512,128]{1,0:T(8,128)(2,1)S(1)}, bf16[512,128]{1,0:T(8,128)(2,1)S(1)}, u32[]{:S(2)}, u32[]{:S(2)}) collective-permute-start(bf16[512,128]{1,0:T(8,128)(2,1)S(1)} %get-tuple-element.76.refs_0_), channel_id=1, source_target_pairs={{4,12},{5,13},{6,14},{7,15},{20,28},{21,29},{22,30},{23,31}} | collective-permute-start | bytes 393224 | tf_op jit(solution)/shard_map/ppermute | solution.py:367
  11.5 3.2 %collective-permute-start.4 = (bf16[512,128]{1,0:T(8,128)(2,1)S(1)}, bf16[512,128]{1,0:T(8,128)(2,1)S(1)}, u32[]{:S(2)}, u32[]{:S(2)}) collective-permute-start(bf16[512,128]{1,0:T(8,128)(2,1)S(1)} %get-tuple-element.84), channel_id=1, source_target_pairs={{0,4},{4,8},{1,5},{5,9},{2,6},{6,10},{3,7},{7,11},{16,20},{20,24},... | collective-permute-start | bytes 393224 | tf_op jit(solution)/shard_map/ppermute | solution.py:367
  14.7 0.1 add.8
  14.7 0.7 %collective-permute-start.5 = (bf16[512,128]{1,0:T(8,128)(2,1)S(1)}, bf16[512,128]{1,0:T(8,128)(2,1)S(1)}, u32[]{:S(2)}, u32[]{:S(2)}) collective-permute-start(bf16[512,128]{1,0:T(8,128)(2,1)S(1)} %get-tuple-element.88), channel_id=1, source_target_pairs={{8,12},{9,13},{10,14},{11,15},{24,28},{25,29},{26,30},{27,31}} | collective-permute-start | bytes 393224 | tf_op jit(solution)/shard_map/ppermute | solution.py:367
  15.5 0.7 %collective-permute-start.6 = (bf16[512,128]{1,0:T(8,128)(2,1)S(1)}, bf16[512,128]{1,0:T(8,128)(2,1)S(1)}, u32[]{:S(2)}, u32[]{:S(2)}) collective-permute-start(bf16[512,128]{1,0:T(8,128)(2,1)S(1)} %get-tuple-element.97), channel_id=1, source_target_pairs={{12,8},{13,9},{14,10},{15,11},{28,24},{29,25},{30,26},{31,27}} | collective-permute-start | bytes 393224 | tf_op jit(solution)/shard_map/ppermute | solution.py:367
  16.1 0.8 %mid.5 = (bf16[320,512]{1,0:T(8,128)(2,1)S(1)}, bf16[320,512]{1,0:T(8,128)(2,1)S(1)}, bf16[512,128]{1,0:T(8,128)(2,1)S(1)}, f32[8,128]{1,0:T(8,128)S(1)}, bf16[512,128]{1,0:T(8,128)(2,1)S(1)}) custom-call(s32[1]{0:T(128)} %bitcast.me_ref.refs_0_, bf16[320,1024]{1,0:T(8,128)(2,1)S(1)} %bitcast.29, bf16[1024,320]{1,0:T(8,128)(2,1)S(1)} %get-tuple-element.70.qt_ref, ...), custom_call_target="tpu_custom_call" | custom-call | bytes 4096 | tf_op jit(solution)/shard_map/mid/pallas_call | solution.py:249
  16.9 0.7 %collective-permute-start.7 = (bf16[512,128]{1,0:T(8,128)(2,1)S(1)}, bf16[512,128]{1,0:T(8,128)(2,1)S(1)}, u32[]{:S(2)}, u32[]{:S(2)}) collective-permute-start(bf16[512,128]{1,0:T(8,128)(2,1)S(1)} %get-tuple-element.86.refs_0_), channel_id=1, source_target_pairs={{8,4},{9,5},{10,6},{11,7},{24,20},{25,21},{26,22},{27,23}} | collective-permute-start | bytes 393224 | tf_op jit(solution)/shard_map/ppermute | solution.py:367
  17.6 0.8 %mid.6 = (bf16[320,512]{1,0:T(8,128)(2,1)S(1)}, bf16[320,512]{1,0:T(8,128)(2,1)S(1)}, bf16[512,128]{1,0:T(8,128)(2,1)S(1)}, f32[8,128]{1,0:T(8,128)S(1)}, bf16[512,128]{1,0:T(8,128)(2,1)S(1)}) custom-call(s32[1]{0:T(128)} %bitcast.me_ref.refs_0_, bf16[320,1024]{1,0:T(8,128)(2,1)S(1)} %bitcast.30, bf16[1024,320]{1,0:T(8,128)(2,1)S(1)} %get-tuple-element.70.qt_ref, ...), custom_call_target="tpu_custom_call" | custom-call | bytes 4096 | tf_op jit(solution)/shard_map/mid/pallas_call | solution.py:249
  18.5 1.3 %collective-permute-start.8 = (bf16[512,128]{1,0:T(8,128)(2,1)S(1)}, bf16[512,128]{1,0:T(8,128)(2,1)S(1)}, u32[]{:S(2)}, u32[]{:S(2)}) collective-permute-start(bf16[512,128]{1,0:T(8,128)(2,1)S(1)} %get-tuple-element.100), channel_id=1, source_target_pairs={{12,4},{4,0},{13,5},{5,1},{14,6},{6,2},{15,7},{7,3},{28,20},{20,16... | collective-permute-start | bytes 393224 | tf_op jit(solution)/shard_map/ppermute | solution.py:367
  19.8 2.6 %back.2 = (bf16[320,1024]{1,0:T(8,128)(2,1)}, bf16[320,1024]{1,0:T(8,128)(2,1)}, f32[320,512]{1,0:T(8,128)S(1)}, f32[320,512]{1,0:T(8,128)S(1)}, f32[8,128]{1,0:T(8,128)S(1)}) custom-call(s32[1]{0:T(128)} %bitcast.me_ref.refs_0_, bf16[320,1024]{1,0:T(8,128)(2,1)S(1)} %bitcast.32, bf16[320,1024]{1,0:T(8,128)(2,1)S(1)} %bitcast.14, ...), custom_call_target="tpu_custom_call" | custom-call | bytes 4096 | tf_op jit(solution)/shard_map/back/pallas_call | solution.py:300
  22.5 1.3 %collective-permute-start.9 = (bf16[512,128]{1,0:T(8,128)(2,1)S(1)}, bf16[512,128]{1,0:T(8,128)(2,1)S(1)}, u32[]{:S(2)}, u32[]{:S(2)}) collective-permute-start(bf16[512,128]{1,0:T(8,128)(2,1)S(1)} %get-tuple-element.117), channel_id=1, source_target_pairs={{8,0},{9,1},{10,2},{11,3},{24,16},{25,17},{26,18},{27,19}} | collective-permute-start | bytes 393224 | tf_op jit(solution)/shard_map/ppermute | solution.py:367
  23.8 0.7 %collective-permute-start.10 = (bf16[512,128]{1,0:T(8,128)(2,1)S(1)}, bf16[512,128]{1,0:T(8,128)(2,1)S(1)}, u32[]{:S(2)}, u32[]{:S(2)}) collective-permute-start(bf16[512,128]{1,0:T(8,128)(2,1)S(1)} %get-tuple-element.117), channel_id=1, source_target_pairs={{12,8},{8,4},{13,9},{9,5},{14,10},{10,6},{15,11},{11,7},{28,24},{2... | collective-permute-start | bytes 393224 | tf_op jit(solution)/shard_map/ppermute | solution.py:367
  24.5 1.4 %collective-permute-done.8.refs_1_.refs_8_ = bf16[512,128]{1,0:T(8,128)(2,1)S(1)} collective-permute-done((bf16[512,128]{1,0:T(8,128)(2,1)S(1)}, bf16[512,128]{1,0:T(8,128)(2,1)S(1)}, u32[]{:S(2)}, u32[]{:S(2)}) %collective-permute-start.8) | collective-permute-done | bytes 131104 | tf_op jit(solution)/shard_map/ppermute | solution.py:367
  25.9 1.3 %collective-permute-start.11 = (bf16[512,128]{1,0:T(8,128)(2,1)S(1)}, bf16[512,128]{1,0:T(8,128)(2,1)S(1)}, u32[]{:S(2)}, u32[]{:S(2)}) collective-permute-start(bf16[512,128]{1,0:T(8,128)(2,1)S(1)} %get-tuple-element.121), channel_id=1, source_target_pairs={{4,0},{5,1},{6,2},{7,3},{20,16},{21,17},{22,18},{23,19}} | collective-permute-start | bytes 393224 | tf_op jit(solution)/shard_map/ppermute | solution.py:367
  27.2 2.6 %back.3 = (bf16[320,1024]{1,0:T(8,128)(2,1)}, bf16[320,1024]{1,0:T(8,128)(2,1)}, f32[320,512]{1,0:T(8,128)S(1)}, f32[320,512]{1,0:T(8,128)S(1)}, f32[8,128]{1,0:T(8,128)S(1)}) custom-call(s32[1]{0:T(128)} %bitcast.me_ref.refs_0_, bf16[320,1024]{1,0:T(8,128)(2,1)S(1)} %bitcast.33, ...), custom_call_target="tpu_custom_call", output_to_operand_aliasing={{0}: (11, {}), {1}: (12, {})} | custom-call | bytes 4096 | tf_op jit(solution)/shard_map/back/pallas_call | solution.py:300
  29.8 1.8 %collective-permute-done.9.refs_9_ = bf16[512,128]{1,0:T(8,128)(2,1)S(1)} collective-permute-done((bf16[512,128]{1,0:T(8,128)(2,1)S(1)}, bf16[512,128]{1,0:T(8,128)(2,1)S(1)}, u32[]{:S(2)}, u32[]{:S(2)}) %collective-permute-start.9) | collective-permute-done | bytes 131104 | tf_op jit(solution)/shard_map/ppermute | solution.py:367
  31.7 1.1 %post.2 = (bf16[320,1024]{1,0:T(8,128)(2,1)}, bf16[320,1024]{1,0:T(8,128)(2,1)}, f32[8,128]{1,0:T(8,128)S(1)}) custom-call(s32[1]{0:T(128)} %bitcast.me_ref.refs_0_, bf16[320,1024]{1,0:T(8,128)(2,1)S(1)} %bitcast.16, bf16[320,1024]{1,0:T(8,128)(2,1)S(1)} %bitcast.25, f32[320,512]{1,0:T(8,128)S(1)} %get-tuple-element.114.refs_3_, ...), custom_call_target="tpu_custom_call" | custom-call | bytes 4096 | tf_op jit(solution)/shard_map/post/pallas_call | solution.py:338
  32.8 0.8 %collective-permute-done.11.refs_1_ = bf16[512,128]{1,0:T(8,128)(2,1)S(1)} collective-permute-done((bf16[512,128]{1,0:T(8,128)(2,1)S(1)}, bf16[512,128]{1,0:T(8,128)(2,1)S(1)}, u32[]{:S(2)}, u32[]{:S(2)}) %collective-permute-start.11) | collective-permute-done | bytes 131104 | tf_op jit(solution)/shard_map/ppermute | solution.py:367
  33.6 1.1 %post.3 = (bf16[320,1024]{1,0:T(8,128)(2,1)}, bf16[320,1024]{1,0:T(8,128)(2,1)}) custom-call(s32[1]{0:T(128)} %bitcast.me_ref.refs_0_, bf16[320,1024]{1,0:T(8,128)(2,1)S(1)} %bitcast.17, bf16[320,1024]{1,0:T(8,128)(2,1)S(1)} %bitcast.26, f32[320,512]{1,0:T(8,128)S(1)} %get-tuple-element.112.gk_in_ref, ...), custom_call_target="tpu_custom_call", output_to_operand_aliasing={{0}: (8, {}), {1}: (9, {})} | custom-call | bytes 4096 | tf_op jit(solution)/shard_map/post/pallas_call | solution.py:338
  (28 shorter events, 0.4 us)
Async XLA Ops:
  0.6 6.0 %copy-start = (bf16[1,320,1024]{2,1,0:T(8,128)(2,1)S(1)}, bf16[1,320,1024]{2,1,0:T(8,128)(2,1)}, u32[]{:S(2)}) copy-start(bf16[1,320,1024]{2,1,0:T(8,128)(2,1)} %param.5) | copy-start | bytes 1966084
  0.7 6.0 %copy-start.1 = (bf16[1,320,1024]{2,1,0:T(8,128)(2,1)S(1)}, bf16[1,320,1024]{2,1,0:T(8,128)(2,1)}, u32[]{:S(2)}) copy-start(bf16[1,320,1024]{2,1,0:T(8,128)(2,1)} %param.6) | copy-start | bytes 1966084
  2.5 8.1 %collective-permute-start = (bf16[512,128]{1,0:T(8,128)(2,1)S(1)}, bf16[512,128]{1,0:T(8,128)(2,1)S(1)}, u32[]{:S(2)}, u32[]{:S(2)}) collective-permute-start(bf16[512,128]{1,0:T(8,128)(2,1)S(1)} %get-tuple-element.73), channel_id=1, source_target_pairs={{0,4},{1,5},{2,6},{3,7},{16,20},{17,21},{18,22},{19,23}} | collective-permute-start | bytes 393224 | tf_op jit(solution)/shard_map/ppermute | solution.py:367
  5.8 3.5 %copy-start.2 = (bf16[1,320,1024]{2,1,0:T(8,128)(2,1)S(1)}, bf16[1,320,1024]{2,1,0:T(8,128)(2,1)}, u32[]{:S(2)}) copy-start(bf16[1,320,1024]{2,1,0:T(8,128)(2,1)} %param.4) | copy-start | bytes 1966084
  5.9 8.8 %collective-permute-start.1 = (bf16[512,128]{1,0:T(8,128)(2,1)S(1)}, bf16[512,128]{1,0:T(8,128)(2,1)S(1)}, u32[]{:S(2)}, u32[]{:S(2)}) collective-permute-start(bf16[512,128]{1,0:T(8,128)(2,1)S(1)} %get-tuple-element.68.refs_0_), channel_id=1, source_target_pairs={{4,8},{5,9},{6,10},{7,11},{20,24},{21,25},{22,26},{23,27}} | collective-permute-start | bytes 393224 | tf_op jit(solution)/shard_map/ppermute | solution.py:367
  6.7 8.0 %collective-permute-start.2 = (bf16[512,128]{1,0:T(8,128)(2,1)S(1)}, bf16[512,128]{1,0:T(8,128)(2,1)S(1)}, u32[]{:S(2)}, u32[]{:S(2)}) collective-permute-start(bf16[512,128]{1,0:T(8,128)(2,1)S(1)} %get-tuple-element.74.refs_1_), channel_id=1, source_target_pairs={{0,8},{8,12},{1,9},{9,13},{2,10},{10,14},{3,11},{11,15},{16,24},{2... | collective-permute-start | bytes 393224 | tf_op jit(solution)/shard_map/ppermute | solution.py:367
  10.6 4.9 %copy-start.3 = (bf16[1,320,1024]{2,1,0:T(8,128)(2,1)S(1)}, bf16[1,320,1024]{2,1,0:T(8,128)(2,1)}, u32[]{:S(2)}) copy-start(bf16[1,320,1024]{2,1,0:T(8,128)(2,1)} %param.7) | copy-start | bytes 1966084
  10.6 4.8 %collective-permute-start.3 = (bf16[512,128]{1,0:T(8,128)(2,1)S(1)}, bf16[512,128]{1,0:T(8,128)(2,1)S(1)}, u32[]{:S(2)}, u32[]{:S(2)}) collective-permute-start(bf16[512,128]{1,0:T(8,128)(2,1)S(1)} %get-tuple-element.76.refs_0_), channel_id=1, source_target_pairs={{4,12},{5,13},{6,14},{7,15},{20,28},{21,29},{22,30},{23,31}} | collective-permute-start | bytes 393224 | tf_op jit(solution)/shard_map/ppermute | solution.py:367
  11.5 6.2 %collective-permute-start.4 = (bf16[512,128]{1,0:T(8,128)(2,1)S(1)}, bf16[512,128]{1,0:T(8,128)(2,1)S(1)}, u32[]{:S(2)}, u32[]{:S(2)}) collective-permute-start(bf16[512,128]{1,0:T(8,128)(2,1)S(1)} %get-tuple-element.84), channel_id=1, source_target_pairs={{0,4},{4,8},{1,5},{5,9},{2,6},{6,10},{3,7},{7,11},{16,20},{20,24},... | collective-permute-start | bytes 393224 | tf_op jit(solution)/shard_map/ppermute | solution.py:367
  14.7 3.7 %collective-permute-start.5 = (bf16[512,128]{1,0:T(8,128)(2,1)S(1)}, bf16[512,128]{1,0:T(8,128)(2,1)S(1)}, u32[]{:S(2)}, u32[]{:S(2)}) collective-permute-start(bf16[512,128]{1,0:T(8,128)(2,1)S(1)} %get-tuple-element.88), channel_id=1, source_target_pairs={{8,12},{9,13},{10,14},{11,15},{24,28},{25,29},{26,30},{27,31}} | collective-permute-start | bytes 393224 | tf_op jit(solution)/shard_map/ppermute | solution.py:367
  15.5 7.0 %collective-permute-start.6 = (bf16[512,128]{1,0:T(8,128)(2,1)S(1)}, bf16[512,128]{1,0:T(8,128)(2,1)S(1)}, u32[]{:S(2)}, u32[]{:S(2)}) collective-permute-start(bf16[512,128]{1,0:T(8,128)(2,1)S(1)} %get-tuple-element.97), channel_id=1, source_target_pairs={{12,8},{13,9},{14,10},{15,11},{28,24},{29,25},{30,26},{31,27}} | collective-permute-start | bytes 393224 | tf_op jit(solution)/shard_map/ppermute | solution.py:367
  16.9 7.5 %collective-permute-start.7 = (bf16[512,128]{1,0:T(8,128)(2,1)S(1)}, bf16[512,128]{1,0:T(8,128)(2,1)S(1)}, u32[]{:S(2)}, u32[]{:S(2)}) collective-permute-start(bf16[512,128]{1,0:T(8,128)(2,1)S(1)} %get-tuple-element.86.refs_0_), channel_id=1, source_target_pairs={{8,4},{9,5},{10,6},{11,7},{24,20},{25,21},{26,22},{27,23}} | collective-permute-start | bytes 393224 | tf_op jit(solution)/shard_map/ppermute | solution.py:367
  18.5 7.3 %collective-permute-start.8 = (bf16[512,128]{1,0:T(8,128)(2,1)S(1)}, bf16[512,128]{1,0:T(8,128)(2,1)S(1)}, u32[]{:S(2)}, u32[]{:S(2)}) collective-permute-start(bf16[512,128]{1,0:T(8,128)(2,1)S(1)} %get-tuple-element.100), channel_id=1, source_target_pairs={{12,4},{4,0},{13,5},{5,1},{14,6},{6,2},{15,7},{7,3},{28,20},{20,16... | collective-permute-start | bytes 393224 | tf_op jit(solution)/shard_map/ppermute | solution.py:367
  22.5 9.2 %collective-permute-start.9 = (bf16[512,128]{1,0:T(8,128)(2,1)S(1)}, bf16[512,128]{1,0:T(8,128)(2,1)S(1)}, u32[]{:S(2)}, u32[]{:S(2)}) collective-permute-start(bf16[512,128]{1,0:T(8,128)(2,1)S(1)} %get-tuple-element.117), channel_id=1, source_target_pairs={{8,0},{9,1},{10,2},{11,3},{24,16},{25,17},{26,18},{27,19}} | collective-permute-start | bytes 393224 | tf_op jit(solution)/shard_map/ppermute | solution.py:367
  23.8 9.0 %collective-permute-start.10 = (bf16[512,128]{1,0:T(8,128)(2,1)S(1)}, bf16[512,128]{1,0:T(8,128)(2,1)S(1)}, u32[]{:S(2)}, u32[]{:S(2)}) collective-permute-start(bf16[512,128]{1,0:T(8,128)(2,1)S(1)} %get-tuple-element.117), channel_id=1, source_target_pairs={{12,8},{8,4},{13,9},{9,5},{14,10},{10,6},{15,11},{11,7},{28,24},{2... | collective-permute-start | bytes 393224 | tf_op jit(solution)/shard_map/ppermute | solution.py:367
  25.9 7.7 %collective-permute-start.11 = (bf16[512,128]{1,0:T(8,128)(2,1)S(1)}, bf16[512,128]{1,0:T(8,128)(2,1)S(1)}, u32[]{:S(2)}, u32[]{:S(2)}) collective-permute-start(bf16[512,128]{1,0:T(8,128)(2,1)S(1)} %get-tuple-element.121), channel_id=1, source_target_pairs={{4,0},{5,1},{6,2},{7,3},{20,16},{21,17},{22,18},{23,19}} | collective-permute-start | bytes 393224 | tf_op jit(solution)/shard_map/ppermute | solution.py:367

commit v9 on v7

--- a/solution.py
+++ b/solution.py
@@ -318,15 +318,15 @@
     half = half_of(me_ref[0])
     laters = [total(l_refs, head(h)) for h in range(heads)]
     for h in range(heads):
+        k = k_ref[:, half_columns(half, h, heads)]
+        gv_buf[:, head(h)] = (gv_in_ref[:, head(h)] + dot_nn(k, laters[h])).astype(BF16)
+    gv_copy = half_copy(half, gv_buf, gv_ref, gv_sem)
+    gv_copy.start()
+    for h in range(heads):
         v = v_ref[:, half_columns(half, h, heads)]
         gk_buf[:, head(h)] = (gk_in_ref[:, head(h)] + dot_nt(v, laters[h])).astype(BF16)
     gk_copy = half_copy(half, gk_buf, gk_ref, gk_sem)
     gk_copy.start()
-    for h in range(heads):
-        k = k_ref[:, half_columns(half, h, heads)]
-        gv_buf[:, head(h)] = (gv_in_ref[:, head(h)] + dot_nn(k, laters[h])).astype(BF16)
-    gv_copy = half_copy(half, gv_buf, gv_ref, gv_sem)
-    gv_copy.start()
     gk_copy.wait()
     gv_copy.wait()
 

time: 35 us -> 35 us (level)
  no operation moved by 1% of the time
where the time goes in v9:
time: 35 us; the launch traced here: 34.7 us
  starting transfers between devices  16.6 us (47%)
  Pallas kernels  12.4 us (35%)
  waiting for transfers between devices  4.67 us (13%)
  between operations  0.98 us (3%)
    ppermute x11, starting transfers between devices, send(): return lax.ppermute(x, 'ctx', pairs)  16.6 us
    pallas_call x2, Pallas kernels, back(): pl.pallas_call(functools.partial(back_kernel, half_of, roles, len(sets)),...  5.24 us
    ppermute x11, waiting for transfers between devices, send(): return lax.ppermute(x, 'ctx', pairs)  4.67 us
    pallas_call x2, Pallas kernels, post(): pl.pallas_call(functools.partial(post_kernel if filled else post_first_ke...  2.24 us
    pallas_call x2, Pallas kernels, states(): pl.pallas_call(functools.partial(state_kernel, halves, roles, keep), in_s...  1.85 us
    pallas_call x4, Pallas kernels, mid(): pl.pallas_call(functools.partial(mid_kernel, half_of, roles, keep, merge)...  1.63 us
    pallas_call x1, Pallas kernels, intra(): pl.pallas_call(intra_kernel, in_specs=[VMEM_SPEC] * 4, out_specs=(VMEM_SP...  1.2 us
  transfers between devices with their start and end apart: 11, of which 4 were waited for; matrix products, arithmetic and copies ran while one was open for 0% of the time, Pallas kernels for 27%

profile of v9, /device:TPU:0, one launch (start us, length us, event | category | flops | bytes accessed | tf_op | source)
XLA Modules:
  0.0 34.7 jit_solution(2604474960402505782)
XLA Ops:
  0.7 1.8 %states.2 = (bf16[512,128]{1,0:T(8,128)(2,1)S(1)}, bf16[512,128]{1,0:T(8,128)(2,1)S(1)}, f32[8,128]{1,0:T(8,128)S(1)}) custom-call(s32[1]{0:T(128)} %bitcast.me_ref.refs_0_, bf16[320,1024]{1,0:T(8,128)(2,1)} %bitcast.9, bf16[320,1024]{1,0:T(8,128)(2,1)} %bitcast.18, f32[8,128]{1,0:T(8,128)S(1)} %broadcast_in_dim.3.token_ref), custom_call_target="tpu_custom_call" | custom-call | bytes 4096 | tf_op jit(solution)/shard_map/states/pallas_call | solution.py:126
  2.5 3.3 %collective-permute-start = (bf16[512,128]{1,0:T(8,128)(2,1)S(1)}, bf16[512,128]{1,0:T(8,128)(2,1)S(1)}, u32[]{:S(2)}, u32[]{:S(2)}) collective-permute-start(bf16[512,128]{1,0:T(8,128)(2,1)S(1)} %get-tuple-element.73), channel_id=1, source_target_pairs={{0,4},{1,5},{2,6},{3,7},{16,20},{17,21},{18,22},{19,23}} | collective-permute-start | bytes 393224 | tf_op jit(solution)/shard_map/ppermute | solution.py:367
  5.9 0.8 %collective-permute-start.1 = (bf16[512,128]{1,0:T(8,128)(2,1)S(1)}, bf16[512,128]{1,0:T(8,128)(2,1)S(1)}, u32[]{:S(2)}, u32[]{:S(2)}) collective-permute-start(bf16[512,128]{1,0:T(8,128)(2,1)S(1)} %get-tuple-element.68.refs_0_), channel_id=1, source_target_pairs={{4,8},{5,9},{6,10},{7,11},{20,24},{21,25},{22,26},{23,27}} | collective-permute-start | bytes 393224 | tf_op jit(solution)/shard_map/ppermute | solution.py:367
  6.7 2.6 %collective-permute-start.2 = (bf16[512,128]{1,0:T(8,128)(2,1)S(1)}, bf16[512,128]{1,0:T(8,128)(2,1)S(1)}, u32[]{:S(2)}, u32[]{:S(2)}) collective-permute-start(bf16[512,128]{1,0:T(8,128)(2,1)S(1)} %get-tuple-element.74.refs_1_), channel_id=1, source_target_pairs={{0,8},{8,12},{1,9},{9,13},{2,10},{10,14},{3,11},{11,15},{16,24},{2... | collective-permute-start | bytes 393224 | tf_op jit(solution)/shard_map/ppermute | solution.py:367
  9.3 1.2 %intra.1 = (f32[320,1024]{1,0:T(8,128)S(1)}, bf16[1024,320]{1,0:T(8,128)(2,1)S(1)}, f32[8,128]{1,0:T(8,128)S(1)}) custom-call(bf16[320,1024]{1,0:T(8,128)(2,1)S(1)} %bitcast.27, bf16[320,1024]{1,0:T(8,128)(2,1)S(1)} %bitcast.12, bf16[320,1024]{1,0:T(8,128)(2,1)S(1)} %bitcast.21, f32[8,128]{1,0:T(8,128)S(1)} %get-tuple-element.69.token_ref), custom_call_target="tpu_custom_call" | custom-call | bytes 4096 | tf_op jit(solution)/shard_map/intra/pallas_call | solution.py:156
  10.6 0.8 %collective-permute-start.3 = (bf16[512,128]{1,0:T(8,128)(2,1)S(1)}, bf16[512,128]{1,0:T(8,128)(2,1)S(1)}, u32[]{:S(2)}, u32[]{:S(2)}) collective-permute-start(bf16[512,128]{1,0:T(8,128)(2,1)S(1)} %get-tuple-element.76.refs_0_), channel_id=1, source_target_pairs={{4,12},{5,13},{6,14},{7,15},{20,28},{21,29},{22,30},{23,31}} | collective-permute-start | bytes 393224 | tf_op jit(solution)/shard_map/ppermute | solution.py:367
  11.5 3.2 %collective-permute-start.4 = (bf16[512,128]{1,0:T(8,128)(2,1)S(1)}, bf16[512,128]{1,0:T(8,128)(2,1)S(1)}, u32[]{:S(2)}, u32[]{:S(2)}) collective-permute-start(bf16[512,128]{1,0:T(8,128)(2,1)S(1)} %get-tuple-element.85), channel_id=1, source_target_pairs={{0,4},{4,8},{1,5},{5,9},{2,6},{6,10},{3,7},{7,11},{16,20},{20,24},... | collective-permute-start | bytes 393224 | tf_op jit(solution)/shard_map/ppermute | solution.py:367
  14.7 0.1 add.8
  14.7 0.7 %collective-permute-start.5 = (bf16[512,128]{1,0:T(8,128)(2,1)S(1)}, bf16[512,128]{1,0:T(8,128)(2,1)S(1)}, u32[]{:S(2)}, u32[]{:S(2)}) collective-permute-start(bf16[512,128]{1,0:T(8,128)(2,1)S(1)} %get-tuple-element.88), channel_id=1, source_target_pairs={{8,12},{9,13},{10,14},{11,15},{24,28},{25,29},{26,30},{27,31}} | collective-permute-start | bytes 393224 | tf_op jit(solution)/shard_map/ppermute | solution.py:367
  15.4 0.8 %mid.4 = (bf16[320,512]{1,0:T(8,128)(2,1)S(1)}, bf16[320,512]{1,0:T(8,128)(2,1)S(1)}, bf16[512,128]{1,0:T(8,128)(2,1)S(1)}, f32[8,128]{1,0:T(8,128)S(1)}, bf16[512,128]{1,0:T(8,128)(2,1)S(1)}) custom-call(s32[1]{0:T(128)} %bitcast.me_ref.refs_0_, bf16[320,1024]{1,0:T(8,128)(2,1)S(1)} %bitcast.28, bf16[1024,320]{1,0:T(8,128)(2,1)S(1)} %get-tuple-element.70.qt_ref, ...), custom_call_target="tpu_custom_call" | custom-call | bytes 4096 | tf_op jit(solution)/shard_map/mid/pallas_call | solution.py:249
  16.3 0.7 %collective-permute-start.6 = (bf16[512,128]{1,0:T(8,128)(2,1)S(1)}, bf16[512,128]{1,0:T(8,128)(2,1)S(1)}, u32[]{:S(2)}, u32[]{:S(2)}) collective-permute-start(bf16[512,128]{1,0:T(8,128)(2,1)S(1)} %get-tuple-element.97), channel_id=1, source_target_pairs={{12,8},{8,4},{13,9},{9,5},{14,10},{10,6},{15,11},{11,7},{28,24},{2... | collective-permute-start | bytes 393224 | tf_op jit(solution)/shard_map/ppermute | solution.py:367
  17.0 0.2 collective-permute-done.4.refs_0_
  17.1 0.8 %mid.6 = (bf16[320,512]{1,0:T(8,128)(2,1)S(1)}, bf16[320,512]{1,0:T(8,128)(2,1)S(1)}, bf16[512,128]{1,0:T(8,128)(2,1)S(1)}, f32[8,128]{1,0:T(8,128)S(1)}, bf16[512,128]{1,0:T(8,128)(2,1)S(1)}) custom-call(s32[1]{0:T(128)} %bitcast.me_ref.refs_0_, bf16[320,1024]{1,0:T(8,128)(2,1)S(1)} %bitcast.30, bf16[1024,320]{1,0:T(8,128)(2,1)S(1)} %get-tuple-element.70.qt_ref, ...), custom_call_target="tpu_custom_call" | custom-call | bytes 4096 | tf_op jit(solution)/shard_map/mid/pallas_call | solution.py:249
  18.0 1.3 %collective-permute-start.7 = (bf16[512,128]{1,0:T(8,128)(2,1)S(1)}, bf16[512,128]{1,0:T(8,128)(2,1)S(1)}, u32[]{:S(2)}, u32[]{:S(2)}) collective-permute-start(bf16[512,128]{1,0:T(8,128)(2,1)S(1)} %get-tuple-element.100), channel_id=1, source_target_pairs={{12,4},{4,0},{13,5},{5,1},{14,6},{6,2},{15,7},{7,3},{28,20},{20,16... | collective-permute-start | bytes 393224 | tf_op jit(solution)/shard_map/ppermute | solution.py:367
  19.3 2.6 %back.2 = (bf16[320,1024]{1,0:T(8,128)(2,1)}, bf16[320,1024]{1,0:T(8,128)(2,1)}, f32[320,512]{1,0:T(8,128)S(1)}, f32[320,512]{1,0:T(8,128)S(1)}, f32[8,128]{1,0:T(8,128)S(1)}) custom-call(s32[1]{0:T(128)} %bitcast.me_ref.refs_0_, bf16[320,1024]{1,0:T(8,128)(2,1)S(1)} %bitcast.32, bf16[320,1024]{1,0:T(8,128)(2,1)S(1)} %bitcast.14, ...), custom_call_target="tpu_custom_call" | custom-call | bytes 4096 | tf_op jit(solution)/shard_map/back/pallas_call | solution.py:300
  21.9 1.3 %collective-permute-start.8 = (bf16[512,128]{1,0:T(8,128)(2,1)S(1)}, bf16[512,128]{1,0:T(8,128)(2,1)S(1)}, u32[]{:S(2)}, u32[]{:S(2)}) collective-permute-start(bf16[512,128]{1,0:T(8,128)(2,1)S(1)} %get-tuple-element.117), channel_id=1, source_target_pairs={{8,0},{9,1},{10,2},{11,3},{24,16},{25,17},{26,18},{27,19}} | collective-permute-start | bytes 393224 | tf_op jit(solution)/shard_map/ppermute | solution.py:367
  23.2 0.7 %collective-permute-start.9 = (bf16[512,128]{1,0:T(8,128)(2,1)S(1)}, bf16[512,128]{1,0:T(8,128)(2,1)S(1)}, u32[]{:S(2)}, u32[]{:S(2)}) collective-permute-start(bf16[512,128]{1,0:T(8,128)(2,1)S(1)} %get-tuple-element.117), channel_id=1, source_target_pairs={{12,8},{8,4},{13,9},{9,5},{14,10},{10,6},{15,11},{11,7},{28,24},{2... | collective-permute-start | bytes 393224 | tf_op jit(solution)/shard_map/ppermute | solution.py:367
  23.9 1.9 %collective-permute-done.7.refs_1_.refs_7_ = bf16[512,128]{1,0:T(8,128)(2,1)S(1)} collective-permute-done((bf16[512,128]{1,0:T(8,128)(2,1)S(1)}, bf16[512,128]{1,0:T(8,128)(2,1)S(1)}, u32[]{:S(2)}, u32[]{:S(2)}) %collective-permute-start.7) | collective-permute-done | bytes 131104 | tf_op jit(solution)/shard_map/ppermute | solution.py:367
  25.9 1.3 %collective-permute-start.10 = (bf16[512,128]{1,0:T(8,128)(2,1)S(1)}, bf16[512,128]{1,0:T(8,128)(2,1)S(1)}, u32[]{:S(2)}, u32[]{:S(2)}) collective-permute-start(bf16[512,128]{1,0:T(8,128)(2,1)S(1)} %get-tuple-element.121), channel_id=1, source_target_pairs={{4,0},{5,1},{6,2},{7,3},{20,16},{21,17},{22,18},{23,19}} | collective-permute-start | bytes 393224 | tf_op jit(solution)/shard_map/ppermute | solution.py:367
  27.2 2.6 %back.3 = (bf16[320,1024]{1,0:T(8,128)(2,1)}, bf16[320,1024]{1,0:T(8,128)(2,1)}, f32[320,512]{1,0:T(8,128)S(1)}, f32[320,512]{1,0:T(8,128)S(1)}, f32[8,128]{1,0:T(8,128)S(1)}) custom-call(s32[1]{0:T(128)} %bitcast.me_ref.refs_0_, bf16[320,1024]{1,0:T(8,128)(2,1)S(1)} %bitcast.33, ...), custom_call_target="tpu_custom_call", output_to_operand_aliasing={{0}: (11, {}), {1}: (12, {})} | custom-call | bytes 4096 | tf_op jit(solution)/shard_map/back/pallas_call | solution.py:300
  29.8 1.5 %collective-permute-done.8.refs_8_ = bf16[512,128]{1,0:T(8,128)(2,1)S(1)} collective-permute-done((bf16[512,128]{1,0:T(8,128)(2,1)S(1)}, bf16[512,128]{1,0:T(8,128)(2,1)S(1)}, u32[]{:S(2)}, u32[]{:S(2)}) %collective-permute-start.8) | collective-permute-done | bytes 131104 | tf_op jit(solution)/shard_map/ppermute | solution.py:367
  31.4 1.1 %post.2 = (bf16[320,1024]{1,0:T(8,128)(2,1)}, bf16[320,1024]{1,0:T(8,128)(2,1)}, f32[8,128]{1,0:T(8,128)S(1)}) custom-call(s32[1]{0:T(128)} %bitcast.me_ref.refs_0_, bf16[320,1024]{1,0:T(8,128)(2,1)S(1)} %bitcast.16, bf16[320,1024]{1,0:T(8,128)(2,1)S(1)} %bitcast.25, f32[320,512]{1,0:T(8,128)S(1)} %get-tuple-element.114.refs_3_, ...), custom_call_target="tpu_custom_call" | custom-call | bytes 4096 | tf_op jit(solution)/shard_map/post/pallas_call | solution.py:338
  32.5 1.0 %collective-permute-done.10.refs_1_ = bf16[512,128]{1,0:T(8,128)(2,1)S(1)} collective-permute-done((bf16[512,128]{1,0:T(8,128)(2,1)S(1)}, bf16[512,128]{1,0:T(8,128)(2,1)S(1)}, u32[]{:S(2)}, u32[]{:S(2)}) %collective-permute-start.10) | collective-permute-done | bytes 131104 | tf_op jit(solution)/shard_map/ppermute | solution.py:367
  33.6 1.1 %post.3 = (bf16[320,1024]{1,0:T(8,128)(2,1)}, bf16[320,1024]{1,0:T(8,128)(2,1)}) custom-call(s32[1]{0:T(128)} %bitcast.me_ref.refs_0_, bf16[320,1024]{1,0:T(8,128)(2,1)S(1)} %bitcast.17, bf16[320,1024]{1,0:T(8,128)(2,1)S(1)} %bitcast.26, f32[320,512]{1,0:T(8,128)S(1)} %get-tuple-element.112.gk_in_ref, ...), custom_call_target="tpu_custom_call", output_to_operand_aliasing={{0}: (8, {}), {1}: (9, {})} | custom-call | bytes 4096 | tf_op jit(solution)/shard_map/post/pallas_call | solution.py:338
  (26 shorter events, 0.4 us)
Async XLA Ops:
  0.6 6.0 %copy-start = (bf16[1,320,1024]{2,1,0:T(8,128)(2,1)S(1)}, bf16[1,320,1024]{2,1,0:T(8,128)(2,1)}, u32[]{:S(2)}) copy-start(bf16[1,320,1024]{2,1,0:T(8,128)(2,1)} %param.5) | copy-start | bytes 1966084
  0.7 6.0 %copy-start.1 = (bf16[1,320,1024]{2,1,0:T(8,128)(2,1)S(1)}, bf16[1,320,1024]{2,1,0:T(8,128)(2,1)}, u32[]{:S(2)}) copy-start(bf16[1,320,1024]{2,1,0:T(8,128)(2,1)} %param.6) | copy-start | bytes 1966084
  2.5 8.1 %collective-permute-start = (bf16[512,128]{1,0:T(8,128)(2,1)S(1)}, bf16[512,128]{1,0:T(8,128)(2,1)S(1)}, u32[]{:S(2)}, u32[]{:S(2)}) collective-permute-start(bf16[512,128]{1,0:T(8,128)(2,1)S(1)} %get-tuple-element.73), channel_id=1, source_target_pairs={{0,4},{1,5},{2,6},{3,7},{16,20},{17,21},{18,22},{19,23}} | collective-permute-start | bytes 393224 | tf_op jit(solution)/shard_map/ppermute | solution.py:367
  5.8 3.5 %copy-start.2 = (bf16[1,320,1024]{2,1,0:T(8,128)(2,1)S(1)}, bf16[1,320,1024]{2,1,0:T(8,128)(2,1)}, u32[]{:S(2)}) copy-start(bf16[1,320,1024]{2,1,0:T(8,128)(2,1)} %param.4) | copy-start | bytes 1966084
  5.9 8.8 %collective-permute-start.1 = (bf16[512,128]{1,0:T(8,128)(2,1)S(1)}, bf16[512,128]{1,0:T(8,128)(2,1)S(1)}, u32[]{:S(2)}, u32[]{:S(2)}) collective-permute-start(bf16[512,128]{1,0:T(8,128)(2,1)S(1)} %get-tuple-element.68.refs_0_), channel_id=1, source_target_pairs={{4,8},{5,9},{6,10},{7,11},{20,24},{21,25},{22,26},{23,27}} | collective-permute-start | bytes 393224 | tf_op jit(solution)/shard_map/ppermute | solution.py:367
  6.7 8.0 %collective-permute-start.2 = (bf16[512,128]{1,0:T(8,128)(2,1)S(1)}, bf16[512,128]{1,0:T(8,128)(2,1)S(1)}, u32[]{:S(2)}, u32[]{:S(2)}) collective-permute-start(bf16[512,128]{1,0:T(8,128)(2,1)S(1)} %get-tuple-element.74.refs_1_), channel_id=1, source_target_pairs={{0,8},{8,12},{1,9},{9,13},{2,10},{10,14},{3,11},{11,15},{16,24},{2... | collective-permute-start | bytes 393224 | tf_op jit(solution)/shard_map/ppermute | solution.py:367
  10.6 4.9 %copy-start.3 = (bf16[1,320,1024]{2,1,0:T(8,128)(2,1)S(1)}, bf16[1,320,1024]{2,1,0:T(8,128)(2,1)}, u32[]{:S(2)}) copy-start(bf16[1,320,1024]{2,1,0:T(8,128)(2,1)} %param.7) | copy-start | bytes 1966084
  10.6 5.6 %collective-permute-start.3 = (bf16[512,128]{1,0:T(8,128)(2,1)S(1)}, bf16[512,128]{1,0:T(8,128)(2,1)S(1)}, u32[]{:S(2)}, u32[]{:S(2)}) collective-permute-start(bf16[512,128]{1,0:T(8,128)(2,1)S(1)} %get-tuple-element.76.refs_0_), channel_id=1, source_target_pairs={{4,12},{5,13},{6,14},{7,15},{20,28},{21,29},{22,30},{23,31}} | collective-permute-start | bytes 393224 | tf_op jit(solution)/shard_map/ppermute | solution.py:367
  11.5 5.7 %collective-permute-start.4 = (bf16[512,128]{1,0:T(8,128)(2,1)S(1)}, bf16[512,128]{1,0:T(8,128)(2,1)S(1)}, u32[]{:S(2)}, u32[]{:S(2)}) collective-permute-start(bf16[512,128]{1,0:T(8,128)(2,1)S(1)} %get-tuple-element.85), channel_id=1, source_target_pairs={{0,4},{4,8},{1,5},{5,9},{2,6},{6,10},{3,7},{7,11},{16,20},{20,24},... | collective-permute-start | bytes 393224 | tf_op jit(solution)/shard_map/ppermute | solution.py:367
  14.7 3.2 %collective-permute-start.5 = (bf16[512,128]{1,0:T(8,128)(2,1)S(1)}, bf16[512,128]{1,0:T(8,128)(2,1)S(1)}, u32[]{:S(2)}, u32[]{:S(2)}) collective-permute-start(bf16[512,128]{1,0:T(8,128)(2,1)S(1)} %get-tuple-element.88), channel_id=1, source_target_pairs={{8,12},{9,13},{10,14},{11,15},{24,28},{25,29},{26,30},{27,31}} | collective-permute-start | bytes 393224 | tf_op jit(solution)/shard_map/ppermute | solution.py:367
  16.3 5.6 %collective-permute-start.6 = (bf16[512,128]{1,0:T(8,128)(2,1)S(1)}, bf16[512,128]{1,0:T(8,128)(2,1)S(1)}, u32[]{:S(2)}, u32[]{:S(2)}) collective-permute-start(bf16[512,128]{1,0:T(8,128)(2,1)S(1)} %get-tuple-element.97), channel_id=1, source_target_pairs={{12,8},{8,4},{13,9},{9,5},{14,10},{10,6},{15,11},{11,7},{28,24},{2... | collective-permute-start | bytes 393224 | tf_op jit(solution)/shard_map/ppermute | solution.py:367
  18.0 7.9 %collective-permute-start.7 = (bf16[512,128]{1,0:T(8,128)(2,1)S(1)}, bf16[512,128]{1,0:T(8,128)(2,1)S(1)}, u32[]{:S(2)}, u32[]{:S(2)}) collective-permute-start(bf16[512,128]{1,0:T(8,128)(2,1)S(1)} %get-tuple-element.100), channel_id=1, source_target_pairs={{12,4},{4,0},{13,5},{5,1},{14,6},{6,2},{15,7},{7,3},{28,20},{20,16... | collective-permute-start | bytes 393224 | tf_op jit(solution)/shard_map/ppermute | solution.py:367
  21.9 9.4 %collective-permute-start.8 = (bf16[512,128]{1,0:T(8,128)(2,1)S(1)}, bf16[512,128]{1,0:T(8,128)(2,1)S(1)}, u32[]{:S(2)}, u32[]{:S(2)}) collective-permute-start(bf16[512,128]{1,0:T(8,128)(2,1)S(1)} %get-tuple-element.117), channel_id=1, source_target_pairs={{8,0},{9,1},{10,2},{11,3},{24,16},{25,17},{26,18},{27,19}} | collective-permute-start | bytes 393224 | tf_op jit(solution)/shard_map/ppermute | solution.py:367
  23.2 9.2 %collective-permute-start.9 = (bf16[512,128]{1,0:T(8,128)(2,1)S(1)}, bf16[512,128]{1,0:T(8,128)(2,1)S(1)}, u32[]{:S(2)}, u32[]{:S(2)}) collective-permute-start(bf16[512,128]{1,0:T(8,128)(2,1)S(1)} %get-tuple-element.117), channel_id=1, source_target_pairs={{12,8},{8,4},{13,9},{9,5},{14,10},{10,6},{15,11},{11,7},{28,24},{2... | collective-permute-start | bytes 393224 | tf_op jit(solution)/shard_map/ppermute | solution.py:367
  25.9 7.7 %collective-permute-start.10 = (bf16[512,128]{1,0:T(8,128)(2,1)S(1)}, bf16[512,128]{1,0:T(8,128)(2,1)S(1)}, u32[]{:S(2)}, u32[]{:S(2)}) collective-permute-start(bf16[512,128]{1,0:T(8,128)(2,1)S(1)} %get-tuple-element.121), channel_id=1, source_target_pairs={{4,0},{5,1},{6,2},{7,3},{20,16},{21,17},{22,18},{23,19}} | collective-permute-start | bytes 393224 | tf_op jit(solution)/shard_map/ppermute | solution.py:367

commit v10 on v8

--- a/solution.py
+++ b/solution.py
@@ -318,15 +318,15 @@
     half = half_of(me_ref[0])
     laters = [total(l_refs, head(h)) for h in range(heads)]
     for h in range(heads):
+        k = k_ref[:, half_columns(half, h, heads)]
+        gv_buf[:, head(h)] = (gv_in_ref[:, head(h)] + dot_nn(k, laters[h])).astype(BF16)
+    gv_copy = half_copy(half, gv_buf, gv_ref, gv_sem)
+    gv_copy.start()
+    for h in range(heads):
         v = v_ref[:, half_columns(half, h, heads)]
         gk_buf[:, head(h)] = (gk_in_ref[:, head(h)] + dot_nt(v, laters[h])).astype(BF16)
     gk_copy = half_copy(half, gk_buf, gk_ref, gk_sem)
     gk_copy.start()
-    for h in range(heads):
-        k = k_ref[:, half_columns(half, h, heads)]
-        gv_buf[:, head(h)] = (gv_in_ref[:, head(h)] + dot_nn(k, laters[h])).astype(BF16)
-    gv_copy = half_copy(half, gv_buf, gv_ref, gv_sem)
-    gv_copy.start()
     gk_copy.wait()
     gv_copy.wait()
 

time: 35.1 us -> 35.1 us (level)
  transfers between devices with their start and end apart: 12 -> 12, of which waited for: 3 -> 3; matrix products, arithmetic and copies ran while one was open for 0% -> 0% of each run, Pallas kernels for 28% -> 27%
where the time goes in v10:
time: 35.1 us; the launch traced here: 34.7 us
  starting transfers between devices  17.2 us (49%)
  Pallas kernels  12.5 us (36%)
  waiting for transfers between devices  4.01 us (11%)
  between operations  1 us (3%)
    ppermute x12, starting transfers between devices, send(): return lax.ppermute(x, 'ctx', pairs)  17.2 us
    pallas_call x2, Pallas kernels, back(): pl.pallas_call(functools.partial(back_kernel, half_of, roles, len(sets)),...  5.25 us
    ppermute x12, waiting for transfers between devices, send(): return lax.ppermute(x, 'ctx', pairs)  4.01 us
    pallas_call x2, Pallas kernels, post(): pl.pallas_call(functools.partial(post_kernel if filled else post_first_ke...  2.26 us
    pallas_call x2, Pallas kernels, states(): pl.pallas_call(functools.partial(state_kernel, halves, roles, keep), in_s...  1.85 us
    pallas_call x4, Pallas kernels, mid(): pl.pallas_call(functools.partial(mid_kernel, half_of, roles, keep, merge)...  1.63 us
    pallas_call x1, Pallas kernels, intra(): pl.pallas_call(intra_kernel, in_specs=[VMEM_SPEC] * 4, out_specs=(VMEM_SP...  1.2 us
  transfers between devices with their start and end apart: 12, of which 3 were waited for; matrix products, arithmetic and copies ran while one was open for 0% of the time, Pallas kernels for 27%

profile of v10, /device:TPU:0, one launch (start us, length us, event | category | flops | bytes accessed | tf_op | source)
XLA Modules:
  0.0 34.7 jit_solution(12496739470021901331)
XLA Ops:
  0.7 1.8 %states.2 = (bf16[512,128]{1,0:T(8,128)(2,1)S(1)}, bf16[512,128]{1,0:T(8,128)(2,1)S(1)}, f32[8,128]{1,0:T(8,128)S(1)}) custom-call(s32[1]{0:T(128)} %bitcast.me_ref.refs_0_, bf16[320,1024]{1,0:T(8,128)(2,1)} %bitcast.9, bf16[320,1024]{1,0:T(8,128)(2,1)} %bitcast.18, f32[8,128]{1,0:T(8,128)S(1)} %broadcast_in_dim.3.token_ref), custom_call_target="tpu_custom_call" | custom-call | bytes 4096 | tf_op jit(solution)/shard_map/states/pallas_call | solution.py:126
  2.5 3.3 %collective-permute-start = (bf16[512,128]{1,0:T(8,128)(2,1)S(1)}, bf16[512,128]{1,0:T(8,128)(2,1)S(1)}, u32[]{:S(2)}, u32[]{:S(2)}) collective-permute-start(bf16[512,128]{1,0:T(8,128)(2,1)S(1)} %get-tuple-element.73), channel_id=1, source_target_pairs={{0,4},{1,5},{2,6},{3,7},{16,20},{17,21},{18,22},{19,23}} | collective-permute-start | bytes 393224 | tf_op jit(solution)/shard_map/ppermute | solution.py:367
  5.9 0.8 %collective-permute-start.1 = (bf16[512,128]{1,0:T(8,128)(2,1)S(1)}, bf16[512,128]{1,0:T(8,128)(2,1)S(1)}, u32[]{:S(2)}, u32[]{:S(2)}) collective-permute-start(bf16[512,128]{1,0:T(8,128)(2,1)S(1)} %get-tuple-element.68.refs_0_), channel_id=1, source_target_pairs={{4,8},{5,9},{6,10},{7,11},{20,24},{21,25},{22,26},{23,27}} | collective-permute-start | bytes 393224 | tf_op jit(solution)/shard_map/ppermute | solution.py:367
  6.7 2.6 %collective-permute-start.2 = (bf16[512,128]{1,0:T(8,128)(2,1)S(1)}, bf16[512,128]{1,0:T(8,128)(2,1)S(1)}, u32[]{:S(2)}, u32[]{:S(2)}) collective-permute-start(bf16[512,128]{1,0:T(8,128)(2,1)S(1)} %get-tuple-element.74.refs_1_), channel_id=1, source_target_pairs={{0,8},{8,12},{1,9},{9,13},{2,10},{10,14},{3,11},{11,15},{16,24},{2... | collective-permute-start | bytes 393224 | tf_op jit(solution)/shard_map/ppermute | solution.py:367
  9.3 1.2 %intra.1 = (f32[320,1024]{1,0:T(8,128)S(1)}, bf16[1024,320]{1,0:T(8,128)(2,1)S(1)}, f32[8,128]{1,0:T(8,128)S(1)}) custom-call(bf16[320,1024]{1,0:T(8,128)(2,1)S(1)} %bitcast.27, bf16[320,1024]{1,0:T(8,128)(2,1)S(1)} %bitcast.12, bf16[320,1024]{1,0:T(8,128)(2,1)S(1)} %bitcast.21, f32[8,128]{1,0:T(8,128)S(1)} %get-tuple-element.69.token_ref), custom_call_target="tpu_custom_call" | custom-call | bytes 4096 | tf_op jit(solution)/shard_map/intra/pallas_call | solution.py:156
  10.6 0.8 %collective-permute-start.3 = (bf16[512,128]{1,0:T(8,128)(2,1)S(1)}, bf16[512,128]{1,0:T(8,128)(2,1)S(1)}, u32[]{:S(2)}, u32[]{:S(2)}) collective-permute-start(bf16[512,128]{1,0:T(8,128)(2,1)S(1)} %get-tuple-element.76.refs_0_), channel_id=1, source_target_pairs={{4,12},{5,13},{6,14},{7,15},{20,28},{21,29},{22,30},{23,31}} | collective-permute-start | bytes 393224 | tf_op jit(solution)/shard_map/ppermute | solution.py:367
  11.5 3.2 %collective-permute-start.4 = (bf16[512,128]{1,0:T(8,128)(2,1)S(1)}, bf16[512,128]{1,0:T(8,128)(2,1)S(1)}, u32[]{:S(2)}, u32[]{:S(2)}) collective-permute-start(bf16[512,128]{1,0:T(8,128)(2,1)S(1)} %get-tuple-element.84), channel_id=1, source_target_pairs={{0,4},{4,8},{1,5},{5,9},{2,6},{6,10},{3,7},{7,11},{16,20},{20,24},... | collective-permute-start | bytes 393224 | tf_op jit(solution)/shard_map/ppermute | solution.py:367
  14.7 0.1 add.8
  14.7 0.7 %collective-permute-start.5 = (bf16[512,128]{1,0:T(8,128)(2,1)S(1)}, bf16[512,128]{1,0:T(8,128)(2,1)S(1)}, u32[]{:S(2)}, u32[]{:S(2)}) collective-permute-start(bf16[512,128]{1,0:T(8,128)(2,1)S(1)} %get-tuple-element.88), channel_id=1, source_target_pairs={{8,12},{9,13},{10,14},{11,15},{24,28},{25,29},{26,30},{27,31}} | collective-permute-start | bytes 393224 | tf_op jit(solution)/shard_map/ppermute | solution.py:367
  15.5 0.7 %collective-permute-start.6 = (bf16[512,128]{1,0:T(8,128)(2,1)S(1)}, bf16[512,128]{1,0:T(8,128)(2,1)S(1)}, u32[]{:S(2)}, u32[]{:S(2)}) collective-permute-start(bf16[512,128]{1,0:T(8,128)(2,1)S(1)} %get-tuple-element.97), channel_id=1, source_target_pairs={{12,8},{13,9},{14,10},{15,11},{28,24},{29,25},{30,26},{31,27}} | collective-permute-start | bytes 393224 | tf_op jit(solution)/shard_map/ppermute | solution.py:367
  16.1 0.8 %mid.5 = (bf16[320,512]{1,0:T(8,128)(2,1)S(1)}, bf16[320,512]{1,0:T(8,128)(2,1)S(1)}, bf16[512,128]{1,0:T(8,128)(2,1)S(1)}, f32[8,128]{1,0:T(8,128)S(1)}, bf16[512,128]{1,0:T(8,128)(2,1)S(1)}) custom-call(s32[1]{0:T(128)} %bitcast.me_ref.refs_0_, bf16[320,1024]{1,0:T(8,128)(2,1)S(1)} %bitcast.29, bf16[1024,320]{1,0:T(8,128)(2,1)S(1)} %get-tuple-element.70.qt_ref, ...), custom_call_target="tpu_custom_call" | custom-call | bytes 4096 | tf_op jit(solution)/shard_map/mid/pallas_call | solution.py:249
  16.9 0.7 %collective-permute-start.7 = (bf16[512,128]{1,0:T(8,128)(2,1)S(1)}, bf16[512,128]{1,0:T(8,128)(2,1)S(1)}, u32[]{:S(2)}, u32[]{:S(2)}) collective-permute-start(bf16[512,128]{1,0:T(8,128)(2,1)S(1)} %get-tuple-element.86.refs_0_), channel_id=1, source_target_pairs={{8,4},{9,5},{10,6},{11,7},{24,20},{25,21},{26,22},{27,23}} | collective-permute-start | bytes 393224 | tf_op jit(solution)/shard_map/ppermute | solution.py:367
  17.6 0.8 %mid.6 = (bf16[320,512]{1,0:T(8,128)(2,1)S(1)}, bf16[320,512]{1,0:T(8,128)(2,1)S(1)}, bf16[512,128]{1,0:T(8,128)(2,1)S(1)}, f32[8,128]{1,0:T(8,128)S(1)}, bf16[512,128]{1,0:T(8,128)(2,1)S(1)}) custom-call(s32[1]{0:T(128)} %bitcast.me_ref.refs_0_, bf16[320,1024]{1,0:T(8,128)(2,1)S(1)} %bitcast.30, bf16[1024,320]{1,0:T(8,128)(2,1)S(1)} %get-tuple-element.70.qt_ref, ...), custom_call_target="tpu_custom_call" | custom-call | bytes 4096 | tf_op jit(solution)/shard_map/mid/pallas_call | solution.py:249
  18.5 1.3 %collective-permute-start.8 = (bf16[512,128]{1,0:T(8,128)(2,1)S(1)}, bf16[512,128]{1,0:T(8,128)(2,1)S(1)}, u32[]{:S(2)}, u32[]{:S(2)}) collective-permute-start(bf16[512,128]{1,0:T(8,128)(2,1)S(1)} %get-tuple-element.100), channel_id=1, source_target_pairs={{12,4},{4,0},{13,5},{5,1},{14,6},{6,2},{15,7},{7,3},{28,20},{20,16... | collective-permute-start | bytes 393224 | tf_op jit(solution)/shard_map/ppermute | solution.py:367
  19.8 2.6 %back.2 = (bf16[320,1024]{1,0:T(8,128)(2,1)}, bf16[320,1024]{1,0:T(8,128)(2,1)}, f32[320,512]{1,0:T(8,128)S(1)}, f32[320,512]{1,0:T(8,128)S(1)}, f32[8,128]{1,0:T(8,128)S(1)}) custom-call(s32[1]{0:T(128)} %bitcast.me_ref.refs_0_, bf16[320,1024]{1,0:T(8,128)(2,1)S(1)} %bitcast.32, bf16[320,1024]{1,0:T(8,128)(2,1)S(1)} %bitcast.14, ...), custom_call_target="tpu_custom_call" | custom-call | bytes 4096 | tf_op jit(solution)/shard_map/back/pallas_call | solution.py:300
  22.5 1.3 %collective-permute-start.9 = (bf16[512,128]{1,0:T(8,128)(2,1)S(1)}, bf16[512,128]{1,0:T(8,128)(2,1)S(1)}, u32[]{:S(2)}, u32[]{:S(2)}) collective-permute-start(bf16[512,128]{1,0:T(8,128)(2,1)S(1)} %get-tuple-element.117), channel_id=1, source_target_pairs={{8,0},{9,1},{10,2},{11,3},{24,16},{25,17},{26,18},{27,19}} | collective-permute-start | bytes 393224 | tf_op jit(solution)/shard_map/ppermute | solution.py:367
  23.8 0.7 %collective-permute-start.10 = (bf16[512,128]{1,0:T(8,128)(2,1)S(1)}, bf16[512,128]{1,0:T(8,128)(2,1)S(1)}, u32[]{:S(2)}, u32[]{:S(2)}) collective-permute-start(bf16[512,128]{1,0:T(8,128)(2,1)S(1)} %get-tuple-element.117), channel_id=1, source_target_pairs={{12,8},{8,4},{13,9},{9,5},{14,10},{10,6},{15,11},{11,7},{28,24},{2... | collective-permute-start | bytes 393224 | tf_op jit(solution)/shard_map/ppermute | solution.py:367
  24.5 1.4 %collective-permute-done.8.refs_1_.refs_8_ = bf16[512,128]{1,0:T(8,128)(2,1)S(1)} collective-permute-done((bf16[512,128]{1,0:T(8,128)(2,1)S(1)}, bf16[512,128]{1,0:T(8,128)(2,1)S(1)}, u32[]{:S(2)}, u32[]{:S(2)}) %collective-permute-start.8) | collective-permute-done | bytes 131104 | tf_op jit(solution)/shard_map/ppermute | solution.py:367
  25.9 1.3 %collective-permute-start.11 = (bf16[512,128]{1,0:T(8,128)(2,1)S(1)}, bf16[512,128]{1,0:T(8,128)(2,1)S(1)}, u32[]{:S(2)}, u32[]{:S(2)}) collective-permute-start(bf16[512,128]{1,0:T(8,128)(2,1)S(1)} %get-tuple-element.121), channel_id=1, source_target_pairs={{4,0},{5,1},{6,2},{7,3},{20,16},{21,17},{22,18},{23,19}} | collective-permute-start | bytes 393224 | tf_op jit(solution)/shard_map/ppermute | solution.py:367
  27.2 2.6 %back.3 = (bf16[320,1024]{1,0:T(8,128)(2,1)}, bf16[320,1024]{1,0:T(8,128)(2,1)}, f32[320,512]{1,0:T(8,128)S(1)}, f32[320,512]{1,0:T(8,128)S(1)}, f32[8,128]{1,0:T(8,128)S(1)}) custom-call(s32[1]{0:T(128)} %bitcast.me_ref.refs_0_, bf16[320,1024]{1,0:T(8,128)(2,1)S(1)} %bitcast.33, ...), custom_call_target="tpu_custom_call", output_to_operand_aliasing={{0}: (11, {}), {1}: (12, {})} | custom-call | bytes 4096 | tf_op jit(solution)/shard_map/back/pallas_call | solution.py:300
  29.8 1.8 %collective-permute-done.9.refs_9_ = bf16[512,128]{1,0:T(8,128)(2,1)S(1)} collective-permute-done((bf16[512,128]{1,0:T(8,128)(2,1)S(1)}, bf16[512,128]{1,0:T(8,128)(2,1)S(1)}, u32[]{:S(2)}, u32[]{:S(2)}) %collective-permute-start.9) | collective-permute-done | bytes 131104 | tf_op jit(solution)/shard_map/ppermute | solution.py:367
  31.7 1.1 %post.2 = (bf16[320,1024]{1,0:T(8,128)(2,1)}, bf16[320,1024]{1,0:T(8,128)(2,1)}, f32[8,128]{1,0:T(8,128)S(1)}) custom-call(s32[1]{0:T(128)} %bitcast.me_ref.refs_0_, bf16[320,1024]{1,0:T(8,128)(2,1)S(1)} %bitcast.16, bf16[320,1024]{1,0:T(8,128)(2,1)S(1)} %bitcast.25, f32[320,512]{1,0:T(8,128)S(1)} %get-tuple-element.114.refs_3_, ...), custom_call_target="tpu_custom_call" | custom-call | bytes 4096 | tf_op jit(solution)/shard_map/post/pallas_call | solution.py:338
  32.8 0.8 %collective-permute-done.11.refs_1_ = bf16[512,128]{1,0:T(8,128)(2,1)S(1)} collective-permute-done((bf16[512,128]{1,0:T(8,128)(2,1)S(1)}, bf16[512,128]{1,0:T(8,128)(2,1)S(1)}, u32[]{:S(2)}, u32[]{:S(2)}) %collective-permute-start.11) | collective-permute-done | bytes 131104 | tf_op jit(solution)/shard_map/ppermute | solution.py:367
  33.6 1.1 %post.3 = (bf16[320,1024]{1,0:T(8,128)(2,1)}, bf16[320,1024]{1,0:T(8,128)(2,1)}) custom-call(s32[1]{0:T(128)} %bitcast.me_ref.refs_0_, bf16[320,1024]{1,0:T(8,128)(2,1)S(1)} %bitcast.17, bf16[320,1024]{1,0:T(8,128)(2,1)S(1)} %bitcast.26, f32[320,512]{1,0:T(8,128)S(1)} %get-tuple-element.112.gk_in_ref, ...), custom_call_target="tpu_custom_call", output_to_operand_aliasing={{0}: (8, {}), {1}: (9, {})} | custom-call | bytes 4096 | tf_op jit(solution)/shard_map/post/pallas_call | solution.py:338
  (28 shorter events, 0.4 us)
Async XLA Ops:
  0.6 6.0 %copy-start = (bf16[1,320,1024]{2,1,0:T(8,128)(2,1)S(1)}, bf16[1,320,1024]{2,1,0:T(8,128)(2,1)}, u32[]{:S(2)}) copy-start(bf16[1,320,1024]{2,1,0:T(8,128)(2,1)} %param.5) | copy-start | bytes 1966084
  0.7 6.0 %copy-start.1 = (bf16[1,320,1024]{2,1,0:T(8,128)(2,1)S(1)}, bf16[1,320,1024]{2,1,0:T(8,128)(2,1)}, u32[]{:S(2)}) copy-start(bf16[1,320,1024]{2,1,0:T(8,128)(2,1)} %param.6) | copy-start | bytes 1966084
  2.5 8.1 %collective-permute-start = (bf16[512,128]{1,0:T(8,128)(2,1)S(1)}, bf16[512,128]{1,0:T(8,128)(2,1)S(1)}, u32[]{:S(2)}, u32[]{:S(2)}) collective-permute-start(bf16[512,128]{1,0:T(8,128)(2,1)S(1)} %get-tuple-element.73), channel_id=1, source_target_pairs={{0,4},{1,5},{2,6},{3,7},{16,20},{17,21},{18,22},{19,23}} | collective-permute-start | bytes 393224 | tf_op jit(solution)/shard_map/ppermute | solution.py:367
  5.8 3.5 %copy-start.2 = (bf16[1,320,1024]{2,1,0:T(8,128)(2,1)S(1)}, bf16[1,320,1024]{2,1,0:T(8,128)(2,1)}, u32[]{:S(2)}) copy-start(bf16[1,320,1024]{2,1,0:T(8,128)(2,1)} %param.4) | copy-start | bytes 1966084
  5.9 8.8 %collective-permute-start.1 = (bf16[512,128]{1,0:T(8,128)(2,1)S(1)}, bf16[512,128]{1,0:T(8,128)(2,1)S(1)}, u32[]{:S(2)}, u32[]{:S(2)}) collective-permute-start(bf16[512,128]{1,0:T(8,128)(2,1)S(1)} %get-tuple-element.68.refs_0_), channel_id=1, source_target_pairs={{4,8},{5,9},{6,10},{7,11},{20,24},{21,25},{22,26},{23,27}} | collective-permute-start | bytes 393224 | tf_op jit(solution)/shard_map/ppermute | solution.py:367
  6.7 8.0 %collective-permute-start.2 = (bf16[512,128]{1,0:T(8,128)(2,1)S(1)}, bf16[512,128]{1,0:T(8,128)(2,1)S(1)}, u32[]{:S(2)}, u32[]{:S(2)}) collective-permute-start(bf16[512,128]{1,0:T(8,128)(2,1)S(1)} %get-tuple-element.74.refs_1_), channel_id=1, source_target_pairs={{0,8},{8,12},{1,9},{9,13},{2,10},{10,14},{3,11},{11,15},{16,24},{2... | collective-permute-start | bytes 393224 | tf_op jit(solution)/shard_map/ppermute | solution.py:367
  10.6 4.9 %copy-start.3 = (bf16[1,320,1024]{2,1,0:T(8,128)(2,1)S(1)}, bf16[1,320,1024]{2,1,0:T(8,128)(2,1)}, u32[]{:S(2)}) copy-start(bf16[1,320,1024]{2,1,0:T(8,128)(2,1)} %param.7) | copy-start | bytes 1966084
  10.6 4.8 %collective-permute-start.3 = (bf16[512,128]{1,0:T(8,128)(2,1)S(1)}, bf16[512,128]{1,0:T(8,128)(2,1)S(1)}, u32[]{:S(2)}, u32[]{:S(2)}) collective-permute-start(bf16[512,128]{1,0:T(8,128)(2,1)S(1)} %get-tuple-element.76.refs_0_), channel_id=1, source_target_pairs={{4,12},{5,13},{6,14},{7,15},{20,28},{21,29},{22,30},{23,31}} | collective-permute-start | bytes 393224 | tf_op jit(solution)/shard_map/ppermute | solution.py:367
  11.5 6.2 %collective-permute-start.4 = (bf16[512,128]{1,0:T(8,128)(2,1)S(1)}, bf16[512,128]{1,0:T(8,128)(2,1)S(1)}, u32[]{:S(2)}, u32[]{:S(2)}) collective-permute-start(bf16[512,128]{1,0:T(8,128)(2,1)S(1)} %get-tuple-element.84), channel_id=1, source_target_pairs={{0,4},{4,8},{1,5},{5,9},{2,6},{6,10},{3,7},{7,11},{16,20},{20,24},... | collective-permute-start | bytes 393224 | tf_op jit(solution)/shard_map/ppermute | solution.py:367
  14.7 3.7 %collective-permute-start.5 = (bf16[512,128]{1,0:T(8,128)(2,1)S(1)}, bf16[512,128]{1,0:T(8,128)(2,1)S(1)}, u32[]{:S(2)}, u32[]{:S(2)}) collective-permute-start(bf16[512,128]{1,0:T(8,128)(2,1)S(1)} %get-tuple-element.88), channel_id=1, source_target_pairs={{8,12},{9,13},{10,14},{11,15},{24,28},{25,29},{26,30},{27,31}} | collective-permute-start | bytes 393224 | tf_op jit(solution)/shard_map/ppermute | solution.py:367
  15.5 7.0 %collective-permute-start.6 = (bf16[512,128]{1,0:T(8,128)(2,1)S(1)}, bf16[512,128]{1,0:T(8,128)(2,1)S(1)}, u32[]{:S(2)}, u32[]{:S(2)}) collective-permute-start(bf16[512,128]{1,0:T(8,128)(2,1)S(1)} %get-tuple-element.97), channel_id=1, source_target_pairs={{12,8},{13,9},{14,10},{15,11},{28,24},{29,25},{30,26},{31,27}} | collective-permute-start | bytes 393224 | tf_op jit(solution)/shard_map/ppermute | solution.py:367
  16.9 7.5 %collective-permute-start.7 = (bf16[512,128]{1,0:T(8,128)(2,1)S(1)}, bf16[512,128]{1,0:T(8,128)(2,1)S(1)}, u32[]{:S(2)}, u32[]{:S(2)}) collective-permute-start(bf16[512,128]{1,0:T(8,128)(2,1)S(1)} %get-tuple-element.86.refs_0_), channel_id=1, source_target_pairs={{8,4},{9,5},{10,6},{11,7},{24,20},{25,21},{26,22},{27,23}} | collective-permute-start | bytes 393224 | tf_op jit(solution)/shard_map/ppermute | solution.py:367
  18.5 7.3 %collective-permute-start.8 = (bf16[512,128]{1,0:T(8,128)(2,1)S(1)}, bf16[512,128]{1,0:T(8,128)(2,1)S(1)}, u32[]{:S(2)}, u32[]{:S(2)}) collective-permute-start(bf16[512,128]{1,0:T(8,128)(2,1)S(1)} %get-tuple-element.100), channel_id=1, source_target_pairs={{12,4},{4,0},{13,5},{5,1},{14,6},{6,2},{15,7},{7,3},{28,20},{20,16... | collective-permute-start | bytes 393224 | tf_op jit(solution)/shard_map/ppermute | solution.py:367
  22.5 9.2 %collective-permute-start.9 = (bf16[512,128]{1,0:T(8,128)(2,1)S(1)}, bf16[512,128]{1,0:T(8,128)(2,1)S(1)}, u32[]{:S(2)}, u32[]{:S(2)}) collective-permute-start(bf16[512,128]{1,0:T(8,128)(2,1)S(1)} %get-tuple-element.117), channel_id=1, source_target_pairs={{8,0},{9,1},{10,2},{11,3},{24,16},{25,17},{26,18},{27,19}} | collective-permute-start | bytes 393224 | tf_op jit(solution)/shard_map/ppermute | solution.py:367
  23.8 9.0 %collective-permute-start.10 = (bf16[512,128]{1,0:T(8,128)(2,1)S(1)}, bf16[512,128]{1,0:T(8,128)(2,1)S(1)}, u32[]{:S(2)}, u32[]{:S(2)}) collective-permute-start(bf16[512,128]{1,0:T(8,128)(2,1)S(1)} %get-tuple-element.117), channel_id=1, source_target_pairs={{12,8},{8,4},{13,9},{9,5},{14,10},{10,6},{15,11},{11,7},{28,24},{2... | collective-permute-start | bytes 393224 | tf_op jit(solution)/shard_map/ppermute | solution.py:367
  25.9 7.7 %collective-permute-start.11 = (bf16[512,128]{1,0:T(8,128)(2,1)S(1)}, bf16[512,128]{1,0:T(8,128)(2,1)S(1)}, u32[]{:S(2)}, u32[]{:S(2)}) collective-permute-start(bf16[512,128]{1,0:T(8,128)(2,1)S(1)} %get-tuple-element.121), channel_id=1, source_target_pairs={{4,0},{5,1},{6,2},{7,3},{20,16},{21,17},{22,18},{23,19}} | collective-permute-start | bytes 393224 | tf_op jit(solution)/shard_map/ppermute | solution.py:367
